TPU v7x, 32 devices: a whole 2x2x4 slice. The times are simulated.
32 devices in a mesh: dp: 4 (over y, x), ctx: 8 (over z, core).
Axes of the slice: x: 2, y: 2, z: 4, core: 2. Of those that a mesh axis runs over, the one named last changes fastest.
Arguments:
- tokens: bfloat16 [8, 2048, 1024], P('dp', 'ctx'), may hold values from -6 to 6
- cotangent: bfloat16 [8, 2048, 1024], P('dp', 'ctx'), may hold values from -6 to 6
- starts: int32 [8, 4], P('dp'), may hold values from 0 to 1792, as said below
- w_query: bfloat16 [1024, 2048], P(('dp', 'ctx')), may hold values from -0.1875 to 0.1875
- key_matrix: bfloat16 [1024, 1024], P(('dp', 'ctx')), may hold values from -0.1875 to 0.1875
- value_matrix: bfloat16 [1024, 1024], P(('dp', 'ctx')), may hold values from -0.1875 to 0.1875
- w_out: bfloat16 [2048, 1024], P(('dp', 'ctx')), may hold values from -3 to 3
- w_gate: bfloat16 [1024, 3072], P(('dp', 'ctx')), may hold values from -0.1875 to 0.1875
- w_up: bfloat16 [1024, 3072], P(('dp', 'ctx')), may hold values from -0.1875 to 0.1875
- w_down: bfloat16 [3072, 1024], P(('dp', 'ctx')), may hold values from -0.109375 to 0.109375
- gains: bfloat16 [2304], P(('dp', 'ctx')), may hold values from 0.5 to 1.5
Outputs:
- output: bfloat16 [8, 2048, 1024], P('dp', 'ctx')
- grad_tokens: float32 [8, 2048, 1024], P('dp', 'ctx')
- grad_query: float32 [1024, 2048], P(('dp', 'ctx'))
- grad_key: float32 [1024, 1024], P(('dp', 'ctx'))
- grad_value: float32 [1024, 1024], P(('dp', 'ctx'))
- grad_out: float32 [2048, 1024], P(('dp', 'ctx'))
- grad_gate: float32 [1024, 3072], P(('dp', 'ctx'))
- grad_up: float32 [1024, 3072], P(('dp', 'ctx'))
- grad_down: float32 [3072, 1024], P(('dp', 'ctx'))
- grad_gains: float32 [2304], P(('dp', 'ctx'))
Inputs may be any that keep to these rules, and one draw needn't show every extreme that they name: `starts`: each row holds 4 distinct multiples of 256 in increasing order, so pieces never intersect.
All inputs are finite; a program needn't handle non-finite values.
Results may differ from a plain program's by a relative error of at most 0.017.
Values may be sent and summed in bfloat16 or wider, within the bound.
A program may use at most 320 MiB of HBM per device.

v0:
```python
import math

import jax
import jax.numpy as jnp
from jax import lax
from jax.sharding import PartitionSpec as P

MODEL_DIM = 1024
QUERY_HEADS = 16
KEY_VALUE_HEADS = 8
HEAD_DIM = 128
SEQUENCE_TOKENS = 2048
PIECE = 256
NPIECE = 4


EPS = 1e-06
THETA = 1000000.0
NEG = -1e30


def rms_norm(incoming_values, gain_vector):
    return (
        incoming_values
        * lax.rsqrt(jnp.mean(incoming_values * incoming_values, axis=-1, keepdims=True) + EPS)
        * gain_vector
    )


def rope_tables(positions):
    half_steps = jnp.arange(HEAD_DIM // 2, dtype=jnp.float32)
    inverse = THETA ** (-2.0 * half_steps / HEAD_DIM)
    angles = positions.astype(jnp.float32)[:, None] * inverse[None, :]
    angles = jnp.concatenate([angles, angles], axis=-1)
    return (jnp.cos(angles), jnp.sin(angles))


def rotate(incoming_values, cosine_table, sine_table):
    half_dim = HEAD_DIM // 2
    turned = jnp.concatenate(
        [-incoming_values[..., half_dim:], incoming_values[..., :half_dim]], axis=-1
    )
    return incoming_values * cosine_table[:, None, :] + turned * sine_table[:, None, :]


def per_head_route(unrotated_projection, gain_vector, cosine_table, sine_table, head_count):
    shaped = unrotated_projection.reshape(unrotated_projection.shape[:-1] + (head_count, HEAD_DIM))
    return rotate(rms_norm(shaped, gain_vector), cosine_table, sine_table).reshape(
        unrotated_projection.shape
    )


def piece_ids(positions, piece_starts):
    inside = (positions[:, None] >= piece_starts[None, :]) & (
        positions[:, None] < piece_starts[None, :] + PIECE
    )
    number = jnp.arange(1, NPIECE + 1, dtype=jnp.int32)
    return jnp.sum(jnp.where(inside, number[None, :], 0), axis=1) - 1


def visible(query_pos, query_id, key_pos, key_id):
    causal = key_pos[None, :] <= query_pos[:, None]
    same_piece = (query_id[:, None] == key_id[None, :]) & (query_id[:, None] >= 0)
    return causal | same_piece


def swiglu(gate_proj, up_proj):
    return jax.nn.silu(gate_proj) * up_proj


def block_extent(kv_count, per_head):
    target = max(1, 512 // per_head)
    chosen = 1
    for candidate in range(1, kv_count + 1):
        if kv_count % candidate == 0 and candidate <= target:
            chosen = candidate
    return chosen


def attend_forward(incoming_query, incoming_keys, incoming_values, allowed, head_group_block):
    sequence_rows = incoming_query.shape[0]
    query_group_factor = QUERY_HEADS // KEY_VALUE_HEADS
    scaling = 1.0 / math.sqrt(HEAD_DIM)
    query_per_head = incoming_query.reshape(
        sequence_rows, KEY_VALUE_HEADS, query_group_factor, HEAD_DIM
    )
    key_per_head = incoming_keys.reshape(incoming_keys.shape[0], KEY_VALUE_HEADS, HEAD_DIM)
    value_per_head = incoming_values.reshape(incoming_values.shape[0], KEY_VALUE_HEADS, HEAD_DIM)
    mixed_parts = []
    total_parts = []
    for head_offset in range(0, KEY_VALUE_HEADS, head_group_block):
        q_part = query_per_head[:, head_offset : head_offset + head_group_block]
        k_part = key_per_head[:, head_offset : head_offset + head_group_block]
        v_part = value_per_head[:, head_offset : head_offset + head_group_block]
        scores = (
            jnp.einsum("tagd,kad->agtk", q_part, k_part, preferred_element_type=jnp.float32)
            * scaling
        )
        scores = jnp.where(allowed[None, None], scores, NEG)
        row_max = jnp.max(scores, axis=-1, keepdims=True)
        exp_scores = jnp.exp(scores - row_max)
        summed = jnp.sum(exp_scores, axis=-1, keepdims=True)
        prob_low = (exp_scores / summed).astype(jnp.bfloat16)
        mixed_parts.append(
            jnp.einsum("agtk,kad->tagd", prob_low, v_part, preferred_element_type=jnp.float32)
        )
        total_parts.append(row_max + jnp.log(summed))
    mixed_out = jnp.concatenate(mixed_parts, axis=1).reshape(sequence_rows, QUERY_HEADS * HEAD_DIM)
    return (mixed_out, jnp.concatenate(total_parts, axis=0))


def attend_backward(
    incoming_query,
    incoming_keys,
    incoming_values,
    allowed,
    log_total,
    mixed_gradient,
    head_group_block,
):
    sequence_rows = incoming_query.shape[0]
    key_row_matrix = incoming_keys.shape[0]
    query_group_factor = QUERY_HEADS // KEY_VALUE_HEADS
    scaling = 1.0 / math.sqrt(HEAD_DIM)
    query_per_head = incoming_query.reshape(
        sequence_rows, KEY_VALUE_HEADS, query_group_factor, HEAD_DIM
    )
    gradient_per_head = mixed_gradient.reshape(
        sequence_rows, KEY_VALUE_HEADS, query_group_factor, HEAD_DIM
    )
    key_per_head = incoming_keys.reshape(key_row_matrix, KEY_VALUE_HEADS, HEAD_DIM)
    value_per_head = incoming_values.reshape(key_row_matrix, KEY_VALUE_HEADS, HEAD_DIM)
    dq_parts = []
    key_gradient_pieces = []
    value_gradient_pieces = []
    for head_offset in range(0, KEY_VALUE_HEADS, head_group_block):
        q_part = query_per_head[:, head_offset : head_offset + head_group_block]
        g_part = gradient_per_head[:, head_offset : head_offset + head_group_block]
        k_part = key_per_head[:, head_offset : head_offset + head_group_block]
        v_part = value_per_head[:, head_offset : head_offset + head_group_block]
        scores = (
            jnp.einsum("tagd,kad->agtk", q_part, k_part, preferred_element_type=jnp.float32)
            * scaling
        )
        scores = jnp.where(allowed[None, None], scores, NEG)
        prob_all = jnp.exp(scores - log_total[head_offset : head_offset + head_group_block])
        prob_low = prob_all.astype(jnp.bfloat16)
        d_probs = jnp.einsum("tagd,kad->agtk", g_part, v_part, preferred_element_type=jnp.float32)
        row_dot = jnp.sum(prob_all * d_probs, axis=-1, keepdims=True)
        d_scores = (prob_all * (d_probs - row_dot)).astype(jnp.bfloat16)
        dq_parts.append(
            jnp.einsum("agtk,kad->tagd", d_scores, k_part, preferred_element_type=jnp.float32)
            * scaling
        )
        key_gradient_pieces.append(
            jnp.einsum("agtk,tagd->kad", d_scores, q_part, preferred_element_type=jnp.float32)
            * scaling
        )
        value_gradient_pieces.append(
            jnp.einsum("agtk,tagd->kad", prob_low, g_part, preferred_element_type=jnp.float32)
        )
    d_query = jnp.concatenate(dq_parts, axis=1).reshape(sequence_rows, QUERY_HEADS * HEAD_DIM)
    key_gradient = jnp.concatenate(key_gradient_pieces, axis=1).reshape(
        key_row_matrix, KEY_VALUE_HEADS * HEAD_DIM
    )
    value_gradient = jnp.concatenate(value_gradient_pieces, axis=1).reshape(
        key_row_matrix, KEY_VALUE_HEADS * HEAD_DIM
    )
    return (d_query, key_gradient, value_gradient)


def per_device(
    tokens, cotangent, starts, w_query, key_matrix, value_matrix, w_out, w_gate, w_up, w_down, gains
):
    sequence_count, sequence_rows, model_width = tokens.shape
    number_of_rows = sequence_count * sequence_rows
    head_group_block = block_extent(KEY_VALUE_HEADS, QUERY_HEADS // KEY_VALUE_HEADS * sequence_rows)
    attn_set = (
        lax.all_gather(w_query, ("dp", "ctx"), axis=0, tiled=True),
        lax.all_gather(key_matrix, ("dp", "ctx"), axis=0, tiled=True),
        lax.all_gather(value_matrix, ("dp", "ctx"), axis=0, tiled=True),
        lax.all_gather(w_out, ("dp", "ctx"), axis=0, tiled=True),
        lax.all_gather(gains, ("dp", "ctx"), axis=0, tiled=True),
    )
    mlp_set = (
        lax.all_gather(w_gate, ("dp", "ctx"), axis=0, tiled=True),
        lax.all_gather(w_up, ("dp", "ctx"), axis=0, tiled=True),
        lax.all_gather(w_down, ("dp", "ctx"), axis=0, tiled=True),
    )
    gain_all = attn_set[4].astype(jnp.float32)
    g_attn = gain_all[:MODEL_DIM]
    g_mlp = gain_all[MODEL_DIM : 2 * MODEL_DIM]
    g_query = gain_all[2 * MODEL_DIM : 2 * MODEL_DIM + HEAD_DIM]
    key_grad_total = gain_all[2 * MODEL_DIM + HEAD_DIM :]
    positions = lax.axis_index("ctx") * sequence_rows + jnp.arange(sequence_rows, dtype=jnp.int32)
    key_places = jnp.arange(SEQUENCE_TOKENS, dtype=jnp.int32)
    cosine_table, sine_table = rope_tables(positions)

    def query_map(unrotated_projection, gain_vector):
        return per_head_route(
            unrotated_projection, gain_vector, cosine_table, sine_table, QUERY_HEADS
        )

    def key_map(unrotated_projection, gain_vector):
        return per_head_route(
            unrotated_projection, gain_vector, cosine_table, sine_table, KEY_VALUE_HEADS
        )

    flat_in = tokens.reshape(number_of_rows, model_width).astype(jnp.float32)
    normed = rms_norm(flat_in, g_attn).astype(jnp.bfloat16)
    query_raw = jnp.dot(normed, attn_set[0], preferred_element_type=jnp.float32).reshape(
        sequence_count, sequence_rows, QUERY_HEADS * HEAD_DIM
    )
    key_unrotated = jnp.dot(normed, attn_set[1], preferred_element_type=jnp.float32).reshape(
        sequence_count, sequence_rows, KEY_VALUE_HEADS * HEAD_DIM
    )
    value_reduced = jnp.dot(normed, attn_set[2], preferred_element_type=jnp.float32).astype(
        jnp.bfloat16
    )
    value_reduced = value_reduced.reshape(sequence_count, sequence_rows, KEY_VALUE_HEADS * HEAD_DIM)
    query_reduced = query_map(query_raw, g_query).astype(jnp.bfloat16)
    key_reduced = key_map(key_unrotated, key_grad_total).astype(jnp.bfloat16)
    mask_list = []
    mixed_list = []
    total_list = []
    for seq_index in range(sequence_count):
        query_ids = piece_ids(positions, starts[seq_index])
        key_ids = piece_ids(key_places, starts[seq_index])
        allowed = visible(positions, query_ids, key_places, key_ids)
        key_full, value_full = (
            lax.all_gather(key_reduced[seq_index], "ctx", axis=0, tiled=True),
            lax.all_gather(value_reduced[seq_index], "ctx", axis=0, tiled=True),
        )
        mixed_out, log_total = attend_forward(
            query_reduced[seq_index], key_full, value_full, allowed, head_group_block
        )
        mask_list.append(allowed)
        mixed_list.append(mixed_out)
        total_list.append(log_total)
    attn_low = (
        jnp.stack(mixed_list).reshape(number_of_rows, QUERY_HEADS * HEAD_DIM).astype(jnp.bfloat16)
    )
    residual = flat_in + jnp.dot(attn_low, attn_set[3], preferred_element_type=jnp.float32)
    mlp_in = rms_norm(residual, g_mlp).astype(jnp.bfloat16)
    gate_proj = jnp.dot(mlp_in, mlp_set[0], preferred_element_type=jnp.float32)
    up_proj = jnp.dot(mlp_in, mlp_set[1], preferred_element_type=jnp.float32)
    hidden = swiglu(gate_proj, up_proj).astype(jnp.bfloat16)
    result = residual + jnp.dot(hidden, mlp_set[2], preferred_element_type=jnp.float32)
    output = result.astype(jnp.bfloat16).reshape(tokens.shape)
    mlp_back = (
        lax.all_gather(w_gate, ("dp", "ctx"), axis=0, tiled=True),
        lax.all_gather(w_up, ("dp", "ctx"), axis=0, tiled=True),
        lax.all_gather(w_down, ("dp", "ctx"), axis=0, tiled=True),
    )
    grad_flat = cotangent.reshape(number_of_rows, model_width)
    grad_down = jnp.dot(hidden.T, grad_flat, preferred_element_type=jnp.float32)
    d_hidden = jnp.dot(grad_flat, mlp_back[2].T, preferred_element_type=jnp.float32)
    swiglu_pull = jax.vjp(swiglu, gate_proj, up_proj)[1]
    d_gate, d_up = swiglu_pull(d_hidden)
    d_gate = d_gate.astype(jnp.bfloat16)
    d_up = d_up.astype(jnp.bfloat16)
    grad_gate = jnp.dot(mlp_in.T, d_gate, preferred_element_type=jnp.float32)
    grad_up = jnp.dot(mlp_in.T, d_up, preferred_element_type=jnp.float32)
    mlp_grads = (
        lax.psum_scatter(grad_gate, ("dp", "ctx"), scatter_dimension=0, tiled=True),
        lax.psum_scatter(grad_up, ("dp", "ctx"), scatter_dimension=0, tiled=True),
        lax.psum_scatter(grad_down, ("dp", "ctx"), scatter_dimension=0, tiled=True),
    )
    d_mlp_in = jnp.dot(d_gate, mlp_back[0].T, preferred_element_type=jnp.float32)
    d_mlp_in = d_mlp_in + jnp.dot(d_up, mlp_back[1].T, preferred_element_type=jnp.float32)
    mlp_norm_pull = jax.vjp(rms_norm, residual, g_mlp)[1]
    d_resid_norm, d_g_mlp = mlp_norm_pull(d_mlp_in)
    d_resid = grad_flat.astype(jnp.float32) + d_resid_norm
    attn_back = (
        lax.all_gather(w_query, ("dp", "ctx"), axis=0, tiled=True),
        lax.all_gather(key_matrix, ("dp", "ctx"), axis=0, tiled=True),
        lax.all_gather(value_matrix, ("dp", "ctx"), axis=0, tiled=True),
        lax.all_gather(w_out, ("dp", "ctx"), axis=0, tiled=True),
        lax.all_gather(gains, ("dp", "ctx"), axis=0, tiled=True),
    )
    d_branch = d_resid.astype(jnp.bfloat16)
    grad_out = jnp.dot(attn_low.T, d_branch, preferred_element_type=jnp.float32)
    d_attn = jnp.dot(d_branch, attn_back[3].T, preferred_element_type=jnp.float32).astype(
        jnp.bfloat16
    )
    d_attn = d_attn.reshape(sequence_count, sequence_rows, QUERY_HEADS * HEAD_DIM)
    dq_list = []
    dk_list = []
    value_gradient_list = []
    for seq_index in range(sequence_count):
        key_full, value_full = (
            lax.all_gather(key_reduced[seq_index], "ctx", axis=0, tiled=True),
            lax.all_gather(value_reduced[seq_index], "ctx", axis=0, tiled=True),
        )
        d_query_seq, d_key_full, d_value_full = attend_backward(
            query_reduced[seq_index],
            key_full,
            value_full,
            mask_list[seq_index],
            total_list[seq_index],
            d_attn[seq_index],
            head_group_block,
        )
        d_key_seq, d_value_seq = (
            lax.psum_scatter(
                d_key_full.astype(jnp.bfloat16), "ctx", scatter_dimension=0, tiled=True
            ).astype(jnp.float32),
            lax.psum_scatter(
                d_value_full.astype(jnp.bfloat16), "ctx", scatter_dimension=0, tiled=True
            ).astype(jnp.float32),
        )
        dq_list.append(d_query_seq)
        dk_list.append(d_key_seq)
        value_gradient_list.append(d_value_seq)
    d_query = jnp.stack(dq_list)
    key_gradient = jnp.stack(dk_list)
    value_gradient_reduced = (
        jnp.stack(value_gradient_list)
        .reshape(number_of_rows, KEY_VALUE_HEADS * HEAD_DIM)
        .astype(jnp.bfloat16)
    )
    query_pull = jax.vjp(query_map, query_raw, g_query)[1]
    d_query_raw, d_g_query = query_pull(d_query)
    key_pull = jax.vjp(key_map, key_unrotated, key_grad_total)[1]
    key_gradient_unrotated, d_g_key = key_pull(key_gradient)
    d_query_low = d_query_raw.reshape(number_of_rows, QUERY_HEADS * HEAD_DIM).astype(jnp.bfloat16)
    key_gradient_reduced = key_gradient_unrotated.reshape(
        number_of_rows, KEY_VALUE_HEADS * HEAD_DIM
    ).astype(jnp.bfloat16)
    grad_query = jnp.dot(normed.T, d_query_low, preferred_element_type=jnp.float32)
    grad_key = jnp.dot(normed.T, key_gradient_reduced, preferred_element_type=jnp.float32)
    grad_value = jnp.dot(normed.T, value_gradient_reduced, preferred_element_type=jnp.float32)
    d_normed = jnp.dot(d_query_low, attn_back[0].T, preferred_element_type=jnp.float32)
    d_normed = d_normed + jnp.dot(
        key_gradient_reduced, attn_back[1].T, preferred_element_type=jnp.float32
    )
    d_normed = d_normed + jnp.dot(
        value_gradient_reduced, attn_back[2].T, preferred_element_type=jnp.float32
    )
    input_pull = jax.vjp(rms_norm, flat_in, g_attn)[1]
    d_input_norm, d_g_attn = input_pull(d_normed)
    grad_tokens = (d_resid + d_input_norm).reshape(tokens.shape)
    grad_gains = jnp.concatenate([d_g_attn, d_g_mlp, d_g_query, d_g_key])
    attn_grads = (
        lax.psum_scatter(grad_query, ("dp", "ctx"), scatter_dimension=0, tiled=True),
        lax.psum_scatter(grad_key, ("dp", "ctx"), scatter_dimension=0, tiled=True),
        lax.psum_scatter(grad_value, ("dp", "ctx"), scatter_dimension=0, tiled=True),
        lax.psum_scatter(grad_out, ("dp", "ctx"), scatter_dimension=0, tiled=True),
        lax.psum_scatter(grad_gains, ("dp", "ctx"), scatter_dimension=0, tiled=True),
    )
    return (
        output,
        grad_tokens,
        attn_grads[0],
        attn_grads[1],
        attn_grads[2],
        attn_grads[3],
        mlp_grads[0],
        mlp_grads[1],
        mlp_grads[2],
        attn_grads[4],
    )


def solution(mesh):
    return jax.shard_map(
        per_device,
        mesh=mesh,
        in_specs=(
            P("dp", "ctx", None),
            P("dp", "ctx", None),
            P("dp", None),
            P(("dp", "ctx"), None),
            P(("dp", "ctx"), None),
            P(("dp", "ctx"), None),
            P(("dp", "ctx"), None),
            P(("dp", "ctx"), None),
            P(("dp", "ctx"), None),
            P(("dp", "ctx"), None),
            P(("dp", "ctx")),
        ),
        out_specs=(
            P("dp", "ctx", None),
            P("dp", "ctx", None),
            P(("dp", "ctx"), None),
            P(("dp", "ctx"), None),
            P(("dp", "ctx"), None),
            P(("dp", "ctx"), None),
            P(("dp", "ctx"), None),
            P(("dp", "ctx"), None),
            P(("dp", "ctx"), None),
            P(("dp", "ctx")),
        ),
        check_vma=False,
    )
```

profile of v0, /device:TPU:0, one launch (start us, length us, event | category | flops | bytes accessed | tf_op | source)
XLA Modules:
  0.0 1993.6 jit_solution(7207629401726574910)
XLA Ops:
  10.3 42.1 %all-reduce.4 = bf16[2304]{0:T(1024)(128)(2,1)S(1)} all-reduce(bf16[2304]{0:T(1024)(128)(2,1)S(1)} %dynamic-update-slice), channel_id=1, replica_groups=mesh['dp'=4,'ctx'=8] {'dp','ctx'}, use_global_device_ids=true, to_apply=%add.4 | all-reduce | flops 2304 | bytes 9216
  56.8 13.4 all-gather.16.cloned.1.call-done
  70.2 3.9 copy.605
  74.1 2.9 multiply_reduce_fusion.8
  82.2 46.3 %all-gather.12.cloned.1.call-done = bf16[1024,1024]{1,0:T(8,128)(2,1)} async-done(((bf16[32,1024]{1,0:T(8,128)(2,1)}), bf16[1024,1024]{1,0:T(8,128)(2,1)}) %all-gather.12.cloned.1.call-update) | async-done | bytes 2097168 | tf_op jit(solution)/shard_map/all_gather | solution.py:181
  128.6 2.8 convolution_convert_fusion.1
  137.8 54.8 %all-gather.20.cloned.1.call-done = bf16[1024,2048]{1,0:T(8,128)(2,1)} async-done(((bf16[32,2048]{1,0:T(8,128)(2,1)}), bf16[1024,2048]{1,0:T(8,128)(2,1)}) %all-gather.20.cloned.1.call-update) | async-done | bytes 4194320 | tf_op jit(solution)/shard_map/all_gather | solution.py:179
  192.6 6.6 copy.607
  199.2 4.9 multiply_reduce_fusion.2
  207.6 33.4 %all-gather.24.cloned.1.call-done = bf16[2048,1024]{0,1:T(8,128)(2,1)} async-done(((bf16[256,1024]{0,1:T(8,128)(2,1)}), bf16[2048,1024]{0,1:T(8,128)(2,1)}) %all-gather.24.cloned.1.call-update) | async-done | bytes 4194320 | tf_op jit(solution)/shard_map/all_gather | solution.py:231
  241.0 3.9 fusion.550
  264.1 25.0 %all-gather.18.cloned.1.call-done = bf16[2048,1024]{0,1:T(8,128)(2,1)} async-done(((bf16[256,1024]{0,1:T(8,128)(2,1)}), bf16[2048,1024]{0,1:T(8,128)(2,1)}) %all-gather.18.cloned.1.call-update) | async-done | bytes 4194320 | tf_op jit(solution)/shard_map/all_gather | solution.py:231
  289.1 3.9 fusion.558
  295.7 3.3 fusion.556
  309.9 2.9 fusion.559
  321.9 14.0 all-gather.22.cloned.1.call-done
  335.9 6.6 copy.968
  342.6 3.8 fusion.444
  374.4 9.0 all-gather.14.cloned.1.call-done
  383.4 6.7 copy.967
  390.1 3.3 fusion.492
  413.2 34.1 %all-gather.26.cloned.1.call-done = bf16[2048,1024]{1,0:T(8,128)(2,1)} async-done(((bf16[64,1024]{1,0:T(8,128)(2,1)}), bf16[2048,1024]{1,0:T(8,128)(2,1)}) %all-gather.26.cloned.1.call-update) | async-done | bytes 4194320 | tf_op jit(solution)/shard_map/all_gather | solution.py:182
  447.3 5.3 multiply_reduce_fusion.7
  455.7 62.6 %all-gather.30.cloned.1.call-done = bf16[1024,3072]{1,0:T(8,128)(2,1)} async-done(((bf16[32,3072]{1,0:T(8,128)(2,1)}), bf16[1024,3072]{1,0:T(8,128)(2,1)}) %all-gather.30.cloned.1.call-update) | async-done | bytes 6291472 | tf_op jit(solution)/shard_map/all_gather | solution.py:187
  518.4 8.1 fusion.561
  526.5 62.7 %all-gather.28.cloned.1.call-done = bf16[1024,3072]{1,0:T(8,128)(2,1)} async-done(((bf16[32,3072]{1,0:T(8,128)(2,1)}), bf16[1024,3072]{1,0:T(8,128)(2,1)}) %all-gather.28.cloned.1.call-update) | async-done | bytes 6291472 | tf_op jit(solution)/shard_map/all_gather | solution.py:186
  589.2 8.0 fusion.560
  597.2 62.9 %all-gather.32.cloned.1.call-done = bf16[3072,1024]{1,0:T(8,128)(2,1)} async-done(((bf16[96,1024]{1,0:T(8,128)(2,1)}), bf16[3072,1024]{1,0:T(8,128)(2,1)}) %all-gather.32.cloned.1.call-update) | async-done | bytes 6291472 | tf_op jit(solution)/shard_map/all_gather | solution.py:188
  660.1 12.5 multiply_convert_fusion
  672.6 3.5 fusion.562
  676.1 6.7 multiply_reduce_fusion.4
  690.1 3.8 fusion.151
  703.9 6.4 copy.803
  711.3 3.6 fusion.167
  725.2 6.6 copy.786
  731.9 3.5 fusion.28
  736.4 3.7 fusion.183
  748.4 3.0 fusion.181
  756.0 3.3 fusion.179
  759.3 3.5 fusion.19
  784.1 4.7 fusion.46
  789.0 4.5 fusion.49
  793.6 4.5 fusion.238
  826.7 8.0 fusion.505
  857.5 3.1 copy.736
  860.5 7.3 fusion.253
  869.0 8.4 fusion.564
  877.5 8.5 fusion.563
  887.2 8.5 fusion.565
  895.9 4.5 convolution_bitcast_fusion.32
  900.5 9.7 reduce-scatter.12.cloned.1.call-done
  916.1 4.6 fusion.495
  922.3 4.7 fusion.255
  927.1 7.4 add_convert_fusion
  936.5 3.1 fusion.294
  939.7 38.6 %all-reduce.5 = f32[2304]{0:T(1024)S(1)} all-reduce(f32[2304]{0:T(1024)S(1)} %pad_maximum_fusion.5), channel_id=13, replica_groups=mesh['dp'=4,'ctx'=8] {'dp','ctx'}, use_global_device_ids=true, to_apply=%region_75.76.clone | all-reduce | flops 2304 | bytes 18432
  978.9 3.5 fusion.204
  982.3 81.2 %reduce-scatter.26.cloned.1.call-done = f32[64,1024]{1,0:T(8,128)} async-done(((f32[2048,1024]{1,0:T(8,128)}), f32[64,1024]{1,0:T(8,128)}) %reduce-scatter.26.cloned.1.call-update) | async-done | bytes 262160 | tf_op jit(solution)/shard_map/reduce_scatter | solution.py:348
  1063.5 152.4 %reduce-scatter.20.cloned.1.call-done = f32[32,2048]{1,0:T(8,128)} async-done(((f32[1024,2048]{1,0:T(8,128)}), f32[32,2048]{1,0:T(8,128)}) %reduce-scatter.20.cloned.1.call-update) | async-done | bytes 262160 | tf_op jit(solution)/shard_map/reduce_scatter | solution.py:345
  1215.9 160.1 %reduce-scatter.30.cloned.1.call-done = f32[32,3072]{1,0:T(8,128)} async-done(((f32[1024,3072]{1,0:T(8,128)}), f32[32,3072]{1,0:T(8,128)}) %reduce-scatter.30.cloned.1.call-update) | async-done | bytes 393232 | tf_op jit(solution)/shard_map/reduce_scatter | solution.py:266
  1376.0 162.1 %reduce-scatter.28.cloned.1.call-done = f32[32,3072]{1,0:T(8,128)} async-done(((f32[1024,3072]{1,0:T(8,128)}), f32[32,3072]{1,0:T(8,128)}) %reduce-scatter.28.cloned.1.call-update) | async-done | bytes 393232 | tf_op jit(solution)/shard_map/reduce_scatter | solution.py:265
  1538.1 161.0 %reduce-scatter.32.cloned.1.call-done = f32[96,1024]{1,0:T(8,128)} async-done(((f32[3072,1024]{1,0:T(8,128)}), f32[96,1024]{1,0:T(8,128)}) %reduce-scatter.32.cloned.1.call-update) | async-done | bytes 393232 | tf_op jit(solution)/shard_map/reduce_scatter | solution.py:267
  1699.0 144.8 %reduce-scatter.24.cloned.1.call-done = f32[32,1024]{1,0:T(8,128)} async-done(((f32[1024,1024]{1,0:T(8,128)}), f32[32,1024]{1,0:T(8,128)}) %reduce-scatter.24.cloned.1.call-update) | async-done | bytes 131088 | tf_op jit(solution)/shard_map/reduce_scatter | solution.py:347
  1843.8 142.7 %reduce-scatter.22.cloned.1.call-done = f32[32,1024]{1,0:T(8,128)} async-done(((f32[1024,1024]{1,0:T(8,128)}), f32[32,1024]{1,0:T(8,128)}) %reduce-scatter.22.cloned.1.call-update) | async-done | bytes 131088 | tf_op jit(solution)/shard_map/reduce_scatter | solution.py:346
  (645 shorter events, 241.1 us)
Async XLA Ops:
  7.2 63.0 %all-gather.16.cloned.1.call-start = ((), (), s32[]{:S(2)}) async-start(), calls=%async_computation.13 | async-start | bytes 2162688 | tf_op jit(solution)/shard_map/all_gather | solution.py:180
  7.9 120.7 %all-gather.12.cloned.1.call-start = ((), (), s32[]{:S(2)}) async-start(), calls=%async_computation.11 | async-start | bytes 2162688 | tf_op jit(solution)/shard_map/all_gather | solution.py:181
  8.7 183.9 %all-gather.20.cloned.1.call-start = ((), (), s32[]{:S(2)}) async-start(), calls=%async_computation.15 | async-start | bytes 4325376 | tf_op jit(solution)/shard_map/all_gather | solution.py:179
  9.4 231.6 %all-gather.24.cloned.1.call-start = ((), (), s32[]{:S(2)}) async-start(), calls=%async_computation.17 | async-start | bytes 4718592 | tf_op jit(solution)/shard_map/all_gather | solution.py:231
  53.0 153.0 %copy-start.105 = (f32[256,128]{0,1:T(8,128)}, f32[256,128]{0,1:T(8,128)S(1)}, u32[]{:S(2)}) copy-start(f32[256,128]{0,1:T(8,128)S(1)} %get-tuple-element.58) | copy-start | bytes 393220
  53.0 153.0 %copy-start.119 = (f32[256,128]{0,1:T(8,128)}, f32[256,128]{0,1:T(8,128)S(1)}, u32[]{:S(2)}) copy-start(f32[256,128]{0,1:T(8,128)S(1)} %get-tuple-element.59) | copy-start | bytes 393220
  54.6 23.1 %copy-start.191 = (f32[128]{0:T(128)}, f32[128]{0:T(128)S(1)}, u32[]{:S(2)}) copy-start(f32[128]{0:T(128)S(1)} %get-tuple-element.63) | copy-start | bytes 1540
  54.6 151.3 %copy-start.193 = (f32[128]{0:T(128)}, f32[128]{0:T(128)S(1)}, u32[]{:S(2)}) copy-start(f32[128]{0:T(128)S(1)} %get-tuple-element.62) | copy-start | bytes 1540
  55.2 26.1 %copy-start.158 = (f32[1024]{0:T(1024)}, f32[1024]{0:T(1024)S(1)}, u32[]{:S(2)}) copy-start(f32[1024]{0:T(1024)S(1)} %get-tuple-element.61) | copy-start | bytes 12292
  56.8 142.4 %copy-start.109 = (bf16[2,256,1024]{2,1,0:T(8,128)(2,1)}, bf16[2,256,1024]{2,1,0:T(8,128)(2,1)S(1)}, u32[]{:S(2)}) copy-start(bf16[2,256,1024]{2,1,0:T(8,128)(2,1)S(1)} %fusion.297) | copy-start | bytes 3145732
  80.1 209.0 %all-gather.18.cloned.1.call-start = ((), (), s32[]{:S(2)}) async-start(), calls=%async_computation.14 | async-start | bytes 4718592 | tf_op jit(solution)/shard_map/all_gather | solution.py:231
  80.7 255.3 %all-gather.22.cloned.1.call-start = ((), (), s32[]{:S(2)}) async-start(), calls=%async_computation.16 | async-start | bytes 4718592 | tf_op jit(solution)/shard_map/all_gather | solution.py:232
  82.2 53.9 %copy-start.197 = (s32[2,4]{1,0:T(2,128)S(1)}, s32[2,4]{1,0:T(2,128)}, u32[]{:S(2)}) copy-start(s32[2,4]{1,0:T(2,128)} %param.13) | copy-start | bytes 100
  132.5 250.9 %all-gather.14.cloned.1.call-start = ((), (), s32[]{:S(2)}) async-start(), calls=%async_computation.12 | async-start | bytes 4718592 | tf_op jit(solution)/shard_map/all_gather | solution.py:232
  133.2 314.1 %all-gather.26.cloned.1.call-start = ((), (), s32[]{:S(2)}) async-start(), calls=%async_computation.18 | async-start | bytes 4325376 | tf_op jit(solution)/shard_map/all_gather | solution.py:182
  134.0 384.4 %all-gather.30.cloned.1.call-start = ((), (), s32[]{:S(2)}) async-start(), calls=%async_computation.20 | async-start | bytes 6488064 | tf_op jit(solution)/shard_map/all_gather | solution.py:187
  134.7 454.4 %all-gather.28.cloned.1.call-start = ((), (), s32[]{:S(2)}) async-start(), calls=%async_computation.19 | async-start | bytes 6488064 | tf_op jit(solution)/shard_map/all_gather | solution.py:186
  135.3 524.8 %all-gather.32.cloned.1.call-start = ((), (), s32[]{:S(2)}) async-start(), calls=%async_computation.21 | async-start | bytes 6488064 | tf_op jit(solution)/shard_map/all_gather | solution.py:188
  136.0 759.8 %reduce-scatter.18.cloned.1.call-start = ((), (), s32[]{:S(2)}) async-start(), calls=%async_computation.25 | async-start | bytes 4718592 | tf_op jit(solution)/shard_map/reduce_scatter | solution.py:308
  207.6 53.7 %copy-start.117 = (bf16[1,256,16,128]{1,3,2,0:T(8,128)(2,1)}, bf16[1,256,16,128]{1,3,2,0:T(8,128)(2,1)S(1)}, u32[]{:S(2)}) copy-start(bf16[1,256,16,128]{1,3,2,0:T(8,128)(2,1)S(1)} %get-tuple-element.35) | copy-start | bytes 3145732
  207.6 102.4 %copy-start.115 = (bf16[1,256,16,128]{1,3,2,0:T(8,128)(2,1)}, bf16[1,256,16,128]{1,3,2,0:T(8,128)(2,1)S(1)}, u32[]{:S(2)}) copy-start(bf16[1,256,16,128]{1,3,2,0:T(8,128)(2,1)S(1)} %get-tuple-element.34) | copy-start | bytes 3145732
  410.1 37.2 %copy-start.65 = (bf16[2,256,1024]{2,1,0:T(8,128)(2,1)S(1)}, bf16[2,256,1024]{2,1,0:T(8,128)(2,1)}, u32[]{:S(2)}) copy-start(bf16[2,256,1024]{2,1,0:T(8,128)(2,1)} %param.11) | copy-start | bytes 3145732
  447.3 8.1 copy-start.162
  452.6 230.2 %copy-start.101 = (f32[512,1024]{1,0:T(8,128)}, f32[512,1024]{1,0:T(8,128)S(1)}, u32[]{:S(2)}) copy-start(f32[512,1024]{1,0:T(8,128)S(1)} %get-tuple-element.109) | copy-start | bytes 6291460
  452.6 246.9 %copy-start.170 = (f32[2,256]{1,0:T(2,128)}, f32[2,256]{1,0:T(2,128)S(1)}, u32[]{:S(2)}) copy-start(f32[2,256]{1,0:T(2,128)S(1)} %log_add_fusion.1) | copy-start | bytes 6148
  452.7 245.7 %copy-start.174 = (f32[2,256]{1,0:T(2,128)}, f32[2,256]{1,0:T(2,128)S(1)}, u32[]{:S(2)}) copy-start(f32[2,256]{1,0:T(2,128)S(1)} %log_add_fusion.2) | copy-start | bytes 6148
  452.7 244.4 %copy-start.176 = (f32[2,256]{1,0:T(2,128)}, f32[2,256]{1,0:T(2,128)S(1)}, u32[]{:S(2)}) copy-start(f32[2,256]{1,0:T(2,128)S(1)} %log_add_fusion.3) | copy-start | bytes 6148
  452.7 243.0 %copy-start.178 = (f32[2,256]{1,0:T(2,128)}, f32[2,256]{1,0:T(2,128)S(1)}, u32[]{:S(2)}) copy-start(f32[2,256]{1,0:T(2,128)S(1)} %log_add_fusion.4) | copy-start | bytes 6148
  452.7 242.1 %copy-start.180 = (f32[2,256]{1,0:T(2,128)}, f32[2,256]{1,0:T(2,128)S(1)}, u32[]{:S(2)}) copy-start(f32[2,256]{1,0:T(2,128)S(1)} %log_add_fusion.5) | copy-start | bytes 6148
  452.8 241.1 %copy-start.182 = (f32[2,256]{1,0:T(2,128)}, f32[2,256]{1,0:T(2,128)S(1)}, u32[]{:S(2)}) copy-start(f32[2,256]{1,0:T(2,128)S(1)} %log_add_fusion.6) | copy-start | bytes 6148
  452.8 237.3 %copy-start.184 = (f32[2,256]{1,0:T(2,128)}, f32[2,256]{1,0:T(2,128)S(1)}, u32[]{:S(2)}) copy-start(f32[2,256]{1,0:T(2,128)S(1)} %log_add_fusion.7) | copy-start | bytes 6148
  452.8 248.0 %copy-start.172 = (f32[2,256]{1,0:T(2,128)}, f32[2,256]{1,0:T(2,128)S(1)}, u32[]{:S(2)}) copy-start(f32[2,256]{1,0:T(2,128)S(1)} %log_add_fusion) | copy-start | bytes 6148
  455.7 133.4 %copy-start.147 = (bf16[512,1024]{1,0:T(8,128)(2,1)}, bf16[512,1024]{1,0:T(8,128)(2,1)S(1)}, u32[]{:S(2)}) copy-start(bf16[512,1024]{1,0:T(8,128)(2,1)S(1)} %multiply_convert_fusion.2) | copy-start | bytes 3145732
  660.1 12.5 copy-start.198
  676.1 6.7 copy-start.150
  690.0 7.1 copy-start.140
  690.0 8.3 copy-start.138
  690.0 9.5 copy-start.132
  690.0 10.7 copy-start.130
  710.4 185.5 %reduce-scatter.16.cloned.1.call-start = ((), (), s32[]{:S(2)}) async-start(), calls=%async_computation.24 | async-start | bytes 4718592 | tf_op jit(solution)/shard_map/reduce_scatter | solution.py:308
  711.2 7.0 copy-start.126
  755.6 144.9 %reduce-scatter.14.cloned.1.call-start = ((), (), s32[]{:S(2)}) async-start(), calls=%async_computation.23 | async-start | bytes 4718592 | tf_op jit(solution)/shard_map/reduce_scatter | solution.py:305
  781.8 7.1 copy-start.76
  793.5 116.6 %reduce-scatter.12.cloned.1.call-start = ((), (), s32[]{:S(2)}) async-start(), calls=%async_computation.22 | async-start | bytes 4718592 | tf_op jit(solution)/shard_map/reduce_scatter | solution.py:305
  793.6 7.1 copy-start.98
  793.6 7.1 copy-start.167
  793.6 7.1 copy-start.195
  826.6 236.9 %reduce-scatter.26.cloned.1.call-start = ((), (), s32[]{:S(2)}) async-start(), calls=%async_computation.29 | async-start | bytes 8650752 | tf_op jit(solution)/shard_map/reduce_scatter | solution.py:348
  834.7 381.2 %reduce-scatter.20.cloned.1.call-start = ((), (), s32[]{:S(2)}) async-start(), calls=%async_computation.26 | async-start | bytes 8650752 | tf_op jit(solution)/shard_map/reduce_scatter | solution.py:345
  834.7 6.6 copy-start.67
  867.8 508.1 %reduce-scatter.30.cloned.1.call-start = ((), (), s32[]{:S(2)}) async-start(), calls=%async_computation.31 | async-start | bytes 12976128 | tf_op jit(solution)/shard_map/reduce_scatter | solution.py:266
  877.5 660.6 %reduce-scatter.28.cloned.1.call-start = ((), (), s32[]{:S(2)}) async-start(), calls=%async_computation.30 | async-start | bytes 12976128 | tf_op jit(solution)/shard_map/reduce_scatter | solution.py:265
  886.0 813.0 %reduce-scatter.32.cloned.1.call-start = ((), (), s32[]{:S(2)}) async-start(), calls=%async_computation.32 | async-start | bytes 12976128 | tf_op jit(solution)/shard_map/reduce_scatter | solution.py:267
  895.8 948.0 %reduce-scatter.24.cloned.1.call-start = ((), (), s32[]{:S(2)}) async-start(), calls=%async_computation.28 | async-start | bytes 4325376 | tf_op jit(solution)/shard_map/reduce_scatter | solution.py:347
  900.4 11.4 copy-start.63
  900.4 11.4 copy-start.155
  900.4 11.4 copy-start.192
  900.4 1086.1 %reduce-scatter.22.cloned.1.call-start = ((), (), s32[]{:S(2)}) async-start(), calls=%async_computation.27 | async-start | bytes 4325376 | tf_op jit(solution)/shard_map/reduce_scatter | solution.py:346
  900.5 11.4 copy-start.107
  927.0 7.4 copy-start.123
  927.0 7.4 copy-start.124
  927.1 7.5 copy-start.121
  936.5 42.3 %copy-start.190 = (f32[1,2,2,128]{3,1,2,0:T(2,128)S(1)}, f32[1,2,2,128]{3,1,2,0:T(2,128)}, u32[]{:S(2)}) copy-start(f32[1,2,2,128]{3,1,2,0:T(2,128)} %copy-done.189) | copy-start | bytes 6148
  936.5 42.3 %copy-start.93 = (f32[512,1024]{1,0:T(8,128)S(1)}, f32[512,1024]{1,0:T(8,128)}, u32[]{:S(2)}) copy-start(f32[512,1024]{1,0:T(8,128)} %copy-done.92) | copy-start | bytes 6291460
  (161 other events, 491.7 us)
Sparse Core Ops, SparseCore 0:
  11.0 59.1 all-gather.15
  73.2 55.3 all-gather.11
  131.6 60.9 all-gather.19
  194.6 46.3 all-gather.23
  243.0 46.0 all-gather.17
  290.5 45.3 all-gather.21
  337.5 45.8 all-gather.13
  386.4 60.8 all-gather.25
  450.3 67.9 all-gather.29
  521.2 67.9 all-gather.27
  592.2 67.9 all-gather.31
  710.5 48.5 reduce-scatter.17
  761.3 48.1 reduce-scatter.15
  811.7 48.1 reduce-scatter.13
  862.0 48.1 reduce-scatter.11
  912.9 150.5 reduce-scatter.25
  1066.2 149.6 reduce-scatter.19
  1222.3 153.5 reduce-scatter.29
  1383.6 154.4 reduce-scatter.27
  1544.5 154.4 reduce-scatter.31
  1702.0 141.7 reduce-scatter.23
  1846.7 139.7 reduce-scatter.21
where the time goes:
time: 2000 us; the launch traced here: 1990 us
  waiting for transfers between devices  1440 us (72%)
  matrix products  282 us (14%)
  local copies, waits for them, and re-layouts  119 us (6%)
  blocking collectives  80.7 us (4%)
  other arithmetic  54.6 us (3%)
    reduce_scatter x1, waiting for transfers between devices, per_device(): lax.psum_scatter(grad_gate, ('dp', 'ctx'), scatter_dimension=0, tiled=True)  162 us
    reduce_scatter x1, waiting for transfers between devices, per_device(): lax.psum_scatter(grad_down, ('dp', 'ctx'), scatter_dimension=0, tiled=True)  161 us
    reduce_scatter x1, waiting for transfers between devices, per_device(): lax.psum_scatter(grad_up, ('dp', 'ctx'), scatter_dimension=0, tiled=True)  160 us
    reduce_scatter x1, waiting for transfers between devices, per_device(): lax.psum_scatter(grad_query, ('dp', 'ctx'), scatter_dimension=0, tiled=True)  152 us
    reduce_scatter x1, waiting for transfers between devices, per_device(): lax.psum_scatter(grad_value, ('dp', 'ctx'), scatter_dimension=0, tiled=True)  145 us
    reduce_scatter x1, waiting for transfers between devices, per_device(): lax.psum_scatter(grad_key, ('dp', 'ctx'), scatter_dimension=0, tiled=True)  143 us
    reduce_scatter x1, waiting for transfers between devices, per_device(): lax.psum_scatter(grad_out, ('dp', 'ctx'), scatter_dimension=0, tiled=True)  81.2 us
    unnamed x2, blocking collectives  80.7 us
  transfers between devices with their start and end apart: 22, of which 19 were waited for; matrix products, arithmetic and copies ran while one was open for 17% of the time, Pallas kernels for 0%

commit v1 on v0

--- a/solution.py
+++ b/solution.py
@@ -1,8 +1,12 @@
+import functools
 import math
 
 import jax
 import jax.numpy as jnp
 from jax import lax
+from jax.experimental import pallas as pl
+from jax.experimental.pallas import tpu as pltpu
+from jax.sharding import Mesh
 from jax.sharding import PartitionSpec as P
 
 MODEL_DIM = 1024
@@ -169,7 +173,7 @@
     return (d_query, key_gradient, value_gradient)
 
 
-def per_device(
+def generic_device(
     tokens, cotangent, starts, w_query, key_matrix, value_matrix, w_out, w_gate, w_up, w_down, gains
 ):
     sequence_count, sequence_rows, model_width = tokens.shape
@@ -362,9 +366,9 @@
     )
 
 
-def solution(mesh):
+def generic_solution(mesh):
     return jax.shard_map(
-        per_device,
+        generic_device,
         mesh=mesh,
         in_specs=(
             P("dp", "ctx", None),
@@ -393,3 +397,675 @@
         ),
         check_vma=False,
     )
+
+
+AXES = ("y", "x", "p", "l", "c")
+FF = 3072
+HALF_FF = FF // 2
+ROWS = 256
+SEQ_ROWS = SEQUENCE_TOKENS
+OWN = SEQ_ROWS // 4
+BLK = 512
+NBLK = SEQ_ROWS // BLK
+QH = 4
+KH = 2
+MESH = pl.DeviceIdType.MESH
+SCALE = 1.0 / math.sqrt(HEAD_DIM)
+LOG2E = 1.4426950408889634
+NT = (((1,), (1,)), ((), ()))
+TN = (((0,), (0,)), ((), ()))
+
+
+def dot(a, b, dims=None):
+    if dims is None:
+        dims = (((1,), (0,)), ((), ()))
+    return lax.dot_general(a, b, dims, preferred_element_type=jnp.float32)
+
+
+def greet(peers):
+    barrier = pltpu.get_barrier_semaphore()
+    for peer in peers:
+        pl.semaphore_signal(barrier, inc=1, device_id=peer, device_id_type=MESH)
+    pl.semaphore_wait(barrier, len(peers))
+
+
+class Net:
+    def __init__(self, send_sem, recv_sem):
+        self.send_sem = send_sem
+        self.recv_sem = recv_sem
+        self.count = 0
+        self.started = []
+
+    def send(self, peer, *pairs):
+        copies = []
+        for src, dst in pairs:
+            copy = pltpu.make_async_remote_copy(
+                src_ref=src,
+                dst_ref=dst,
+                send_sem=self.send_sem.at[self.count],
+                recv_sem=self.recv_sem.at[self.count],
+                device_id=peer,
+                device_id_type=MESH,
+            )
+            self.count += 1
+            copy.start()
+            copies.append(copy)
+        self.started += copies
+        return copies
+
+    def finish(self):
+        for copy in self.started:
+            copy.wait_send()
+
+
+def arrived(copies):
+    for copy in copies:
+        copy.wait_recv()
+
+
+def place():
+    return tuple(lax.axis_index(name) for name in AXES)
+
+
+def front_kernel(tok, wa, gn, xs, wf, gf, send_sem, recv_sem, local_sem):
+    y, x, p, l, c = place()
+    net = Net(send_sem, recv_sem)
+    peer_c, peer_l, peer_p = {"c": 1 - c}, {"l": 1 - l}, {"p": 1 - p}
+    peer_d = {"l": 1 - l, "c": 1 - c}
+    peer_x, peer_y = {"x": 1 - x}, {"y": 1 - y}
+    block = 4 * p + 2 * l + c
+    group = (y * 2 + x) * 8
+    me = group + block
+    greet((peer_c, peer_l, peer_d, peer_p, peer_x, peer_y))
+    first = []
+    for peer, quarter in ((peer_l, 2 * (1 - l) + c), (peer_d, 2 * (1 - l) + 1 - c), (peer_c, 2 * l + 1 - c)):
+        first += net.send(peer, (wa.at[quarter], wf.at[me]), (gn, gf.at[me]))
+    near = net.send(peer_l, (tok.at[p], xs.at[block]))
+    far = net.send(peer_p, (tok.at[1 - p], xs.at[block]))
+    near_c = net.send(peer_c, (tok.at[p], xs.at[block]))
+    own = (
+        pltpu.make_async_copy(wa.at[2 * l + c], wf.at[me], local_sem.at[0]),
+        pltpu.make_async_copy(gn, gf.at[me], local_sem.at[1]),
+        pltpu.make_async_copy(tok.at[p], xs.at[block], local_sem.at[2]),
+    )
+    for copy in own:
+        copy.start()
+
+    def span(base, count):
+        ref = pl.ds(base, count)
+        return (wf.at[ref], wf.at[ref]), (gf.at[ref], gf.at[ref])
+
+    for copy in own:
+        copy.wait()
+    arrived(first)
+    mine, other = group + 4 * p, group + 4 * (1 - p)
+    across = net.send(peer_p, *span(mine, 4))
+    own_x = net.send(peer_x, *span(mine, 4))
+    arrived(near)
+    relay = net.send(peer_c, (xs.at[block ^ 2], xs.at[block ^ 2]))
+    arrived(own_x)
+    own_y = net.send(peer_y, *span(mine, 4), *span((y * 2 + 1 - x) * 8 + 4 * p, 4))
+    arrived(across)
+    other_y = net.send(peer_y, *span(other, 4))
+    arrived(far)
+    far_l = net.send(peer_l, (xs.at[block ^ 4], xs.at[block ^ 4]))
+    relay += net.send(peer_c, (xs.at[block ^ 4], xs.at[block ^ 4]))
+    arrived(other_y)
+    other_x = net.send(peer_x, *span(other, 4), *span(((1 - y) * 2 + x) * 8 + 4 * (1 - p), 4))
+    arrived(far_l)
+    relay += net.send(peer_c, (xs.at[block ^ 6], xs.at[block ^ 6]))
+    arrived(near_c)
+    arrived(relay)
+    arrived(own_y)
+    arrived(other_x)
+    net.finish()
+
+
+def front(tok, wa, gn):
+    any_spec = pl.BlockSpec(memory_space=pl.ANY)
+    copies = 30
+    return pl.pallas_call(
+        front_kernel,
+        out_shape=(
+            jax.ShapeDtypeStruct((8, ROWS, MODEL_DIM), jnp.bfloat16),
+            jax.ShapeDtypeStruct((32, 48, 1024), jnp.bfloat16),
+            jax.ShapeDtypeStruct((32, 8, 128), jnp.float32),
+        ),
+        in_specs=[any_spec] * 3,
+        out_specs=[any_spec] * 3,
+        scratch_shapes=[
+            pltpu.SemaphoreType.DMA((copies,)),
+            pltpu.SemaphoreType.DMA((copies,)),
+            pltpu.SemaphoreType.DMA((3,)),
+        ],
+        compiler_params=pltpu.CompilerParams(collective_id=0, has_side_effects=True),
+        name="front_gather",
+    )(tok, wa, gn)
+
+
+def back_kernel(
+    part, gpart, out, gout, work, gwork, ry, rx, ox, oy, rp, rq, gry, grx, gox, goy, grp, grq, send_sem, recv_sem
+):
+    y, x, p, l, c = place()
+    net = Net(send_sem, recv_sem)
+    peer_c, peer_l, peer_p = {"c": 1 - c}, {"l": 1 - l}, {"p": 1 - p}
+    peer_d = {"l": 1 - l, "c": 1 - c}
+    peer_x, peer_y = {"x": 1 - x}, {"y": 1 - y}
+    greet((peer_c, peer_l, peer_d, peer_p, peer_x, peer_y))
+
+    def slots(yy, xx, pp):
+        return pl.ds(((yy * 2 + xx) * 2 + pp) * 4, 4)
+
+    def pairs(from_refs, spans, to_refs):
+        found = []
+        for index, span in enumerate(spans):
+            for src, dst in zip(from_refs, to_refs):
+                found.append((src.at[span], dst.at[pl.ds(4 * index, 4)]))
+        return found
+
+    source = (part, gpart)
+    own_y = net.send(peer_y, *pairs(source, (slots(1 - y, 0, p), slots(1 - y, 1, p)), (ry, gry)))
+    other_x = net.send(peer_x, *pairs(source, (slots(0, 1 - x, 1 - p), slots(1, 1 - x, 1 - p)), (ox, gox)))
+
+    def add(targets, span, left, right, place_at):
+        for target, a, b in zip(targets, left, right):
+            total = a.astype(jnp.float32) + b[pl.ds(4 * place_at, 4)].astype(jnp.float32)
+            target[span] = total.astype(target.dtype)
+
+    working = (work, gwork)
+    arrived(own_y)
+    for xx in (0, 1):
+        span = slots(y, xx, p)
+        add(working, span, (part[span], gpart[span]), (ry, gry), xx)
+    own_x = net.send(peer_x, *pairs(working, (slots(y, 1 - x, p),), (rx, grx)))
+    arrived(other_x)
+    for yy in (0, 1):
+        span = slots(yy, x, 1 - p)
+        add(working, span, (part[span], gpart[span]), (ox, gox), yy)
+    other_y = net.send(peer_y, *pairs(working, (slots(1 - y, x, 1 - p),), (oy, goy)))
+    arrived(other_y)
+    span = slots(y, x, 1 - p)
+    add(working, span, (work[span], gwork[span]), (oy, goy), 0)
+    across = net.send(peer_p, *pairs(working, (span,), (rp, grp)))
+    arrived(own_x)
+    span = slots(y, x, p)
+    add(working, span, (work[span], gwork[span]), (rx, grx), 0)
+    arrived(across)
+    add(working, span, (work[span], gwork[span]), (rp, grp), 0)
+    base = ((y * 2 + x) * 2 + p) * 4
+    me = 2 * l + c
+    last = []
+    for peer, quarter in ((peer_l, 2 * (1 - l) + c), (peer_d, 2 * (1 - l) + 1 - c), (peer_c, 2 * l + 1 - c)):
+        last += net.send(peer, (work.at[base + quarter], rq.at[me]), (gwork.at[base + quarter], grq.at[me]))
+    rq[me] = work[base + me]
+    grq[me] = gwork[base + me]
+    arrived(last)
+    out[...] = rq[...].astype(jnp.float32)
+    gout[...] = grq[0] + grq[1] + grq[2] + grq[3]
+    net.finish()
+
+
+def back(part, gpart):
+    def both(*lead):
+        return pltpu.VMEM(lead + (48, 1024), jnp.bfloat16), pltpu.VMEM(lead + (8, 128), jnp.float32)
+
+    sizes = (8, 4, 8, 4, 4, 4)
+    grads = [both(size)[0] for size in sizes]
+    gains = [both(size)[1] for size in sizes]
+    vmem = pl.BlockSpec(memory_space=pltpu.VMEM)
+    copies = 24
+    return pl.pallas_call(
+        back_kernel,
+        out_shape=(
+            jax.ShapeDtypeStruct((4, 48, 1024), jnp.float32),
+            jax.ShapeDtypeStruct((8, 128), jnp.float32),
+        ),
+        in_specs=[vmem] * 2,
+        out_specs=[vmem] * 2,
+        scratch_shapes=[*both(32)] + grads + gains + [pltpu.SemaphoreType.DMA((copies,))] * 2,
+        compiler_params=pltpu.CompilerParams(
+            collective_id=1, has_side_effects=True, vmem_limit_bytes=48 * 1024 * 1024
+        ),
+        name="back_reduce",
+    )(part, gpart)
+
+
+def turn(value):
+    return pltpu.roll(value, HEAD_DIM // 2, 1)
+
+
+def qkv_kernel(x_ref, w_ref, ga_ref, gq_ref, gk_ref, cos_ref, sin_ref, n_ref, q_ref, k_ref, v_ref, qr_ref, kr_ref):
+    x = x_ref[...].astype(jnp.float32)
+    r = lax.rsqrt(jnp.mean(x * x, axis=-1, keepdims=True) + EPS)
+    normed = (x * r * ga_ref[...]).astype(jnp.bfloat16)
+    n_ref[...] = normed
+    full = dot(normed, w_ref[...])
+    cosine, sine = cos_ref[...], sin_ref[...]
+    for h in range(QH + KH):
+        u = full[:, h * HEAD_DIM : (h + 1) * HEAD_DIM]
+        raw_ref, out_ref, g_ref, at = (qr_ref, q_ref, gq_ref, h) if h < QH else (kr_ref, k_ref, gk_ref, h - QH)
+        raw_ref[at] = u
+        n = u * lax.rsqrt(jnp.mean(u * u, axis=-1, keepdims=True) + EPS) * g_ref[...]
+        out_ref[at] = (n * cosine + turn(n) * sine).astype(jnp.bfloat16)
+    for h in range(KH):
+        at = (QH + KH + h) * HEAD_DIM
+        v_ref[h] = full[:, at : at + HEAD_DIM].astype(jnp.bfloat16)
+
+
+def qkv(x, w, ga, gq, gk, cosine, sine):
+    rows = 256
+
+    def row(width):
+        return pl.BlockSpec((rows, width), lambda i: (i, 0))
+
+    def whole(a):
+        return pl.BlockSpec(a.shape, lambda i: (0, 0))
+
+    def heads(n):
+        return pl.BlockSpec((n, rows, HEAD_DIM), lambda i: (0, i, 0))
+
+    def shape(n, dtype):
+        return jax.ShapeDtypeStruct((n, SEQ_ROWS, HEAD_DIM), dtype)
+
+    return pl.pallas_call(
+        qkv_kernel,
+        grid=(SEQ_ROWS // rows,),
+        out_shape=(
+            jax.ShapeDtypeStruct((SEQ_ROWS, MODEL_DIM), jnp.bfloat16),
+            shape(QH, jnp.bfloat16),
+            shape(KH, jnp.bfloat16),
+            shape(KH, jnp.bfloat16),
+            shape(QH, jnp.float32),
+            shape(KH, jnp.float32),
+        ),
+        in_specs=[row(MODEL_DIM), whole(w), whole(ga), whole(gq), whole(gk), row(HEAD_DIM), row(HEAD_DIM)],
+        out_specs=[row(MODEL_DIM), heads(QH), heads(KH), heads(KH), heads(QH), heads(KH)],
+        compiler_params=pltpu.CompilerParams(vmem_limit_bytes=48 * 1024 * 1024),
+        cost_estimate=pl.CostEstimate(flops=2 * SEQ_ROWS * 1024 * 1024, bytes_accessed=24 << 20, transcendentals=0),
+        name="project",
+    )(x, w, ga, gq, gk, cosine, sine)
+
+
+def block_mask(key_dim, flags, index):
+    shape = (BLK, BLK)
+    key = lax.broadcasted_iota(jnp.int32, shape, key_dim)
+    query = lax.broadcasted_iota(jnp.int32, shape, 1 - key_dim)
+    upper = query // PIECE
+    piece = jnp.where(upper == 0, flags[2 * index], flags[2 * index + 1])
+    return (key <= query) | ((key // PIECE == upper) & (piece > 0))
+
+
+def attend_kernel(flags, q_ref, k_ref, v_ref, o_ref, lse_ref):
+    i = pl.program_id(1)
+    ones = jnp.ones((BLK, HEAD_DIM), jnp.bfloat16)
+    mask = block_mask(1, flags, i)
+
+    def values(j):
+        return jnp.concatenate([v_ref[0, pl.ds(j * BLK, BLK), :], ones], axis=1)
+
+    for h in range(2):
+        q = q_ref[h]
+
+        def scores(j):
+            return dot(q, k_ref[0, pl.ds(j * BLK, BLK), :], NT) * (SCALE * LOG2E)
+
+        def step(j, acc):
+            return acc + dot(jnp.exp2(scores(j)).astype(jnp.bfloat16), values(j))
+
+        acc = lax.fori_loop(0, i, step, jnp.zeros((BLK, 2 * HEAD_DIM), jnp.float32))
+        probs = jnp.where(mask, jnp.exp2(scores(i)), 0.0).astype(jnp.bfloat16)
+        acc = acc + dot(probs, values(i))
+        total = acc[:, HEAD_DIM:]
+        o_ref[:, h * HEAD_DIM : (h + 1) * HEAD_DIM] = (acc[:, :HEAD_DIM] / total).astype(jnp.bfloat16)
+        lse_ref[h] = jnp.log2(total).T[0:8, :]
+
+
+def attend(flags, q, k, v):
+    whole = pl.BlockSpec((1, SEQ_ROWS, HEAD_DIM), lambda g, i, f: (g, 0, 0))
+    return pl.pallas_call(
+        attend_kernel,
+        out_shape=(
+            jax.ShapeDtypeStruct((SEQ_ROWS, QH * HEAD_DIM), jnp.bfloat16),
+            jax.ShapeDtypeStruct((QH, 8, SEQ_ROWS), jnp.float32),
+        ),
+        grid_spec=pltpu.PrefetchScalarGridSpec(
+            num_scalar_prefetch=1,
+            grid=(KH, NBLK),
+            in_specs=[pl.BlockSpec((2, BLK, HEAD_DIM), lambda g, i, f: (g, i, 0)), whole, whole],
+            out_specs=[
+                pl.BlockSpec((BLK, 2 * HEAD_DIM), lambda g, i, f: (i, g)),
+                pl.BlockSpec((2, 8, BLK), lambda g, i, f: (g, 0, i)),
+            ],
+        ),
+        compiler_params=pltpu.CompilerParams(vmem_limit_bytes=48 * 1024 * 1024),
+        cost_estimate=pl.CostEstimate(
+            flops=4 * QH * SEQ_ROWS * SEQ_ROWS * HEAD_DIM, bytes_accessed=8 << 20, transcendentals=QH * SEQ_ROWS * SEQ_ROWS
+        ),
+        name="attend",
+    )(flags, q, k, v)
+
+
+def attend_back_kernel(flags, q_ref, k_ref, v_ref, o_ref, do_ref, lse_ref, dq_ref, dk_ref, dv_ref, delta, dk_acc, dv_acc):
+    j = pl.program_id(1)
+
+    @pl.when(j == 0)
+    def _():
+        dq_ref[...] = jnp.zeros_like(dq_ref)
+        for h in range(2):
+            cols = slice(h * HEAD_DIM, (h + 1) * HEAD_DIM)
+            for i in range(NBLK):
+                rows = slice(i * BLK, (i + 1) * BLK)
+                prod = do_ref[rows, cols].astype(jnp.float32) * o_ref[rows, cols].astype(jnp.float32)
+                delta[h, :, rows] = jnp.broadcast_to(jnp.sum(prod.T, axis=0, keepdims=True), (8, BLK))
+
+    k = k_ref[0]
+    v = v_ref[0]
+    dk_acc[...] = jnp.zeros_like(dk_acc)
+    dv_acc[...] = jnp.zeros_like(dv_acc)
+    for h in range(2):
+
+        def step(i, mask=None):
+            rows = pl.ds(pl.multiple_of(i * BLK, BLK), BLK)
+            q = q_ref[h, rows, :]
+            do = do_ref[rows, h * HEAD_DIM : (h + 1) * HEAD_DIM]
+            probs = jnp.exp2(dot(k, q, NT) * (SCALE * LOG2E) - lse_ref[h, 0:1, rows])
+            if mask is not None:
+                probs = jnp.where(mask, probs, 0.0)
+            d_scores = (probs * (dot(v, do, NT) - delta[h, 0:1, rows])).astype(jnp.bfloat16)
+            dv_acc[...] += dot(probs.astype(jnp.bfloat16), do)
+            dk_acc[...] += dot(d_scores, q)
+            dq_ref[h, rows, :] += dot(d_scores, k, TN)
+
+        def loop(i, carry):
+            step(i)
+            return carry
+
+        step(j, block_mask(0, flags, j))
+        lax.fori_loop(j + 1, NBLK, loop, 0)
+    dk_ref[0] = dk_acc[...]
+    dv_ref[0] = dv_acc[...].astype(jnp.bfloat16)
+
+
+def attend_back(flags, q, k, v, o, do, lse):
+    both = pl.BlockSpec((2, SEQ_ROWS, HEAD_DIM), lambda g, j, f: (g, 0, 0))
+    wide = pl.BlockSpec((SEQ_ROWS, 2 * HEAD_DIM), lambda g, j, f: (0, g))
+    part = pl.BlockSpec((1, BLK, HEAD_DIM), lambda g, j, f: (g, j, 0))
+    return pl.pallas_call(
+        attend_back_kernel,
+        out_shape=(
+            jax.ShapeDtypeStruct((QH, SEQ_ROWS, HEAD_DIM), jnp.float32),
+            jax.ShapeDtypeStruct((KH, SEQ_ROWS, HEAD_DIM), jnp.float32),
+            jax.ShapeDtypeStruct((KH, SEQ_ROWS, HEAD_DIM), jnp.bfloat16),
+        ),
+        grid_spec=pltpu.PrefetchScalarGridSpec(
+            num_scalar_prefetch=1,
+            grid=(KH, NBLK),
+            in_specs=[both, part, part, wide, wide, pl.BlockSpec((2, 8, SEQ_ROWS), lambda g, j, f: (g, 0, 0))],
+            out_specs=[both, part, part],
+            scratch_shapes=[
+                pltpu.VMEM((2, 8, SEQ_ROWS), jnp.float32),
+                pltpu.VMEM((BLK, HEAD_DIM), jnp.float32),
+                pltpu.VMEM((BLK, HEAD_DIM), jnp.float32),
+            ],
+        ),
+        compiler_params=pltpu.CompilerParams(vmem_limit_bytes=48 * 1024 * 1024),
+        cost_estimate=pl.CostEstimate(
+            flops=10 * QH * SEQ_ROWS * SEQ_ROWS * HEAD_DIM, bytes_accessed=16 << 20, transcendentals=QH * SEQ_ROWS * SEQ_ROWS
+        ),
+        name="attend_back",
+    )(flags, q, k, v, o, do, lse)
+
+
+def unrope_kernel(dq_ref, dk_ref, dv_ref, qr_ref, kr_ref, gq_ref, gk_ref, cos_ref, sin_ref, d_ref, dg_ref):
+    @pl.when(pl.program_id(0) == 0)
+    def _():
+        dg_ref[...] = jnp.zeros_like(dg_ref)
+
+    cosine, sine = cos_ref[...], sin_ref[...]
+    sums = [jnp.zeros((8, HEAD_DIM), jnp.float32)] * 2
+    for h in range(QH + KH):
+        at = h if h < QH else h - QH
+        grad_ref, raw_ref, g_ref, kind = (dq_ref, qr_ref, gq_ref, 0) if h < QH else (dk_ref, kr_ref, gk_ref, 1)
+        grad = grad_ref[at] * SCALE
+        u = raw_ref[at]
+        e = grad * cosine + turn(grad * sine)
+        r = lax.rsqrt(jnp.mean(u * u, axis=-1, keepdims=True) + EPS)
+        ur = u * r
+        sums[kind] += jnp.sum((e * ur).reshape(-1, 8, HEAD_DIM), axis=0)
+        ge = e * g_ref[...]
+        d = r * (ge - ur * jnp.mean(ur * ge, axis=-1, keepdims=True))
+        d_ref[:, h * HEAD_DIM : (h + 1) * HEAD_DIM] = d.astype(jnp.bfloat16)
+    for h in range(KH):
+        at = (QH + KH + h) * HEAD_DIM
+        d_ref[:, at : at + HEAD_DIM] = dv_ref[h]
+    for kind in range(2):
+        dg_ref[kind] += sums[kind]
+
+
+def unrope(dq, dk, dv, qr, kr, gq, gk, cosine, sine):
+    rows = 256
+
+    def row(width):
+        return pl.BlockSpec((rows, width), lambda i: (i, 0))
+
+    def whole(a):
+        return pl.BlockSpec(a.shape, lambda i: (0, 0))
+
+    def heads(n):
+        return pl.BlockSpec((n, rows, HEAD_DIM), lambda i: (0, i, 0))
+
+    return pl.pallas_call(
+        unrope_kernel,
+        grid=(SEQ_ROWS // rows,),
+        out_shape=(
+            jax.ShapeDtypeStruct((SEQ_ROWS, 1024), jnp.bfloat16),
+            jax.ShapeDtypeStruct((2, 8, HEAD_DIM), jnp.float32),
+        ),
+        in_specs=[heads(QH), heads(KH), heads(KH), heads(QH), heads(KH), whole(gq), whole(gk), row(HEAD_DIM), row(HEAD_DIM)],
+        out_specs=[row(1024), pl.BlockSpec((2, 8, HEAD_DIM), lambda i: (0, 0, 0))],
+        compiler_params=pltpu.CompilerParams(vmem_limit_bytes=48 * 1024 * 1024),
+        cost_estimate=pl.CostEstimate(flops=SEQ_ROWS * 1024 * 20, bytes_accessed=24 << 20, transcendentals=0),
+        name="unrope",
+    )(dq, dk, dv, qr, kr, gq, gk, cosine, sine)
+
+
+def swap(value, name):
+    return lax.ppermute(value, name, [(0, 1), (1, 0)])
+
+
+def pick(value, index):
+    return lax.dynamic_index_in_dim(value, index, 0, keepdims=False)
+
+
+def in_order(index, own, other):
+    return jnp.where(index == 0, jnp.stack([own, other]), jnp.stack([other, own]))
+
+
+def spread_pairs(which):
+    found = []
+    for p in range(2):
+        for l in range(2):
+            for c in range(2):
+                s = c if which == 0 else 1 - c
+                found.append((4 * p + 2 * l + c, 4 * s + 2 * p + l))
+    return found
+
+
+def to_owner(value, p, c):
+    first = lax.ppermute(pick(value, c), ("p", "l", "c"), spread_pairs(0))
+    second = lax.ppermute(pick(value, 1 - c), ("p", "l", "c"), spread_pairs(1))
+    return in_order(p, first, second).reshape(2 * ROWS, value.shape[-1])
+
+
+def from_owner(value, p, c):
+    rows = value.reshape(2, ROWS, value.shape[-1])
+    back = [[(b, a) for a, b in spread_pairs(which)] for which in range(2)]
+    first = lax.ppermute(pick(rows, p), ("p", "l", "c"), back[0])
+    second = lax.ppermute(pick(rows, 1 - p), ("p", "l", "c"), back[1])
+    return in_order(c, first, second)
+
+
+def sum_rows(value, l, c):
+    value = value.reshape(2, 2, OWN, value.shape[-1])
+    mine = lax.dynamic_index_in_dim(value, c, 1, keepdims=False)
+    theirs = lax.dynamic_index_in_dim(value, 1 - c, 1, keepdims=False)
+    chip = mine + swap(theirs.astype(jnp.bfloat16), "c").astype(jnp.float32)
+    return pick(chip, l) + swap(pick(chip, 1 - l).astype(jnp.bfloat16), "l").astype(jnp.float32)
+
+
+def norm_scale(value):
+    return lax.rsqrt(jnp.mean(value * value, axis=-1, keepdims=True) + EPS)
+
+
+def norm_back(value, r, gain, grad):
+    scaled = value * r
+    gained = grad * gain
+    return r * (gained - scaled * jnp.mean(scaled * gained, axis=-1, keepdims=True)), jnp.sum(grad * scaled, axis=0)
+
+
+def quarters(value, width):
+    return value.reshape(value.shape[0], 4, width).transpose(1, 0, 2)
+
+
+def fast_device(tokens, cotangent, starts, w_query, key_matrix, value_matrix, w_out, w_gate, w_up, w_down, gains):
+    y, x, p, l, c = place()
+    t = 2 * l + c
+    group = ("y", "x", "p", "l")
+    halves = jnp.stack(
+        [
+            jnp.concatenate(
+                [
+                    w_gate[:, h * HALF_FF : (h + 1) * HALF_FF],
+                    w_up[:, h * HALF_FF : (h + 1) * HALF_FF],
+                    w_down[:, h * 512 : (h + 1) * 512].reshape(32, HALF_FF),
+                ],
+                axis=0,
+            )
+            for h in range(2)
+        ]
+    )
+    chip_half = in_order(c, pick(halves, c), swap(pick(halves, 1 - c), "c")).reshape(192, HALF_FF)
+    mlp = lax.all_gather(chip_half, group, axis=0, tiled=True).reshape(32, 3, 32, HALF_FF)
+    wa = jnp.concatenate(
+        [
+            jnp.concatenate([quarters(w_query, 512), quarters(key_matrix, 256), quarters(value_matrix, 256)], axis=2),
+            quarters(w_out, 256).reshape(4, 16, 1024),
+        ],
+        axis=1,
+    )
+    gn = jnp.pad(gains.astype(jnp.float32), (0, 952)).reshape(8, 128)
+    xs, wf, gf = front(tokens, wa, gn)
+    xs = xs.reshape(SEQ_ROWS, MODEL_DIM)
+    gain_all = gf.reshape(32, 1024)[:, :72].reshape(2304)
+    g_attn = gain_all[None, :1024]
+    g_mlp = gain_all[None, 1024:2048]
+    g_q = gain_all[None, 2048:2176]
+    g_k = gain_all[None, 2176:]
+    w_qkv = wf[:, :32].reshape(1024, 1024)
+    cosine, sine = rope_tables(jnp.arange(SEQ_ROWS, dtype=jnp.int32))
+    sine = jnp.concatenate([-sine[:, :64], sine[:, 64:]], axis=1)
+    own_starts = pick(starts, p)
+    block_at = jnp.arange(SEQ_ROWS // PIECE, dtype=jnp.int32) * PIECE
+    flags = jnp.any(own_starts[None, :] == block_at[:, None], axis=1).astype(jnp.int32)
+    normed, q, k, v, q_raw, k_raw = qkv(xs, w_qkv, g_attn, g_q, g_k, cosine, sine)
+    attn, lse = attend(flags, q, k, v)
+    wo_cols = wf[:, 32:].reshape(4, 512, 256)
+    wo_l = swap(pick(wo_cols, 2 * (1 - l) + c), "l")
+    wo_d = swap(swap(pick(wo_cols, 2 * (1 - l) + 1 - c), "l"), "c")
+    wo_c = swap(pick(wo_cols, 2 * l + 1 - c), "c")
+    wo_own = pick(wo_cols, t)
+    upper = jnp.where(c == 0, jnp.concatenate([wo_own, wo_c], 1), jnp.concatenate([wo_c, wo_own], 1))
+    lower = jnp.where(c == 0, jnp.concatenate([wo_l, wo_d], 1), jnp.concatenate([wo_d, wo_l], 1))
+    wo = jnp.where(l == 0, jnp.concatenate([upper, lower], 1), jnp.concatenate([lower, upper], 1))
+    branch = sum_rows(dot(attn, wo), l, c)
+    x_own = pick(xs.reshape(4, OWN, MODEL_DIM), t).astype(jnp.float32)
+    resid = x_own + branch
+    r_mlp = norm_scale(resid)
+    mlp_own = (resid * r_mlp * g_mlp).astype(jnp.bfloat16)
+    mlp_in = in_order(c, mlp_own, swap(mlp_own, "c")).reshape(1024, MODEL_DIM)
+    dy_own = to_owner(cotangent, p, c)
+    dy = in_order(c, dy_own, swap(dy_own, "c")).reshape(1024, MODEL_DIM)
+    wg = mlp[:, 0].reshape(1024, HALF_FF)
+    wu = mlp[:, 1].reshape(1024, HALF_FF)
+    wd_cols = mlp[:, 2].reshape(2, HALF_FF, 512)
+    wd_pair = in_order(c, pick(wd_cols, c), swap(pick(wd_cols, 1 - c), "c"))
+    wd = jnp.concatenate([wd_pair[0], wd_pair[1]], axis=1)
+    gate = dot(mlp_in, wg)
+    up = dot(mlp_in, wu)
+    s = jax.nn.sigmoid(gate)
+    silu = gate * s
+    hidden = (silu * up).astype(jnp.bfloat16)
+    d_hidden = dot(dy, wd, NT)
+    d_up = (d_hidden * silu).astype(jnp.bfloat16)
+    d_gate = (d_hidden * up * s * (1.0 + gate * (1.0 - s))).astype(jnp.bfloat16)
+    d_in = (dot(d_gate, wg, NT) + dot(d_up, wu, NT)).reshape(2, OWN, MODEL_DIM)
+    d_mlp_in = pick(d_in, c) + swap(pick(d_in, 1 - c), "c")
+    d_norm, d_g_mlp = norm_back(resid, r_mlp, g_mlp, d_mlp_in)
+    d_resid = dy_own.astype(jnp.float32) + d_norm
+    d_branch = d_resid.astype(jnp.bfloat16)
+    grad_gate = dot(mlp_in, d_gate, TN).astype(jnp.bfloat16)
+    grad_up = dot(mlp_in, d_up, TN).astype(jnp.bfloat16)
+    grad_down = dot(hidden, dy, TN).astype(jnp.bfloat16)
+    down_cols = jnp.stack([grad_down[:, :512], grad_down[:, 512:]])
+    down_half = in_order(c, pick(down_cols, c), swap(pick(down_cols, 1 - c), "c"))
+    packed = jnp.stack(
+        [grad_gate.reshape(32, 32, HALF_FF), grad_up.reshape(32, 32, HALF_FF), down_half.reshape(32, 32, HALF_FF)], axis=1
+    ).reshape(16 * 192, HALF_FF)
+    mlp_sum = lax.psum_scatter(packed, group, scatter_dimension=0, tiled=True).reshape(2, 96, HALF_FF)
+    mlp_other = swap(pick(mlp_sum, 1 - c), "c")
+    mlp_out = in_order(c, pick(mlp_sum, c), mlp_other).astype(jnp.float32)
+    out_gate = jnp.concatenate([mlp_out[0, :32], mlp_out[1, :32]], axis=1)
+    out_up = jnp.concatenate([mlp_out[0, 32:64], mlp_out[1, 32:64]], axis=1)
+    out_down = jnp.concatenate([mlp_out[0, 64:].reshape(96, 512), mlp_out[1, 64:].reshape(96, 512)], axis=1)
+    down = dot(hidden, wd).reshape(2, OWN, MODEL_DIM)
+    result = resid + pick(down, c) + swap(pick(down, 1 - c).astype(jnp.bfloat16), "c").astype(jnp.float32)
+    output = from_owner(result.astype(jnp.bfloat16), p, c)
+    near = in_order(c, d_branch, swap(d_branch, "c"))
+    far = swap(d_branch, "l")
+    far_pair = in_order(c, far, swap(far, "c"))
+    d_all = in_order(l, near, far_pair).reshape(SEQ_ROWS, MODEL_DIM)
+    d_attn = dot(d_all, wo, NT).astype(jnp.bfloat16)
+    grad_out = dot(attn, d_all, TN).astype(jnp.bfloat16)
+    dq, dk, dv = attend_back(flags, q, k, v, attn, d_attn, lse)
+    d_qkv, d_g_heads = unrope(dq, dk, dv, q_raw, k_raw, g_q, g_k, cosine, sine)
+    grad_qkv = dot(normed, d_qkv, TN).astype(jnp.bfloat16)
+    d_normed = sum_rows(dot(d_qkv, w_qkv, NT), l, c)
+    d_in_norm, d_g_attn = norm_back(x_own, norm_scale(x_own), g_attn, d_normed)
+    grad_tokens = from_owner((d_resid + d_in_norm).astype(jnp.bfloat16), p, c).astype(jnp.float32)
+    go = grad_out.reshape(512, 4, 256).transpose(1, 0, 2)
+    go_own = pick(go, t)
+    go_l = swap(pick(go, 2 * (1 - l) + c), "l")
+    go_d = swap(swap(pick(go, 2 * (1 - l) + 1 - c), "l"), "c")
+    go_c = swap(pick(go, 2 * l + 1 - c), "c")
+    go_all = in_order(l, in_order(c, go_own, go_c), in_order(c, go_l, go_d))
+    part = jnp.concatenate([grad_qkv.reshape(32, 32, 1024), go_all.reshape(32, 16, 1024)], axis=1)
+    d_gains = jnp.concatenate([d_g_attn, d_g_mlp, jnp.sum(d_g_heads, axis=1).reshape(256)])
+    g_part = jnp.pad(d_gains.reshape(32, 72), ((0, 0), (0, 952))).reshape(32, 8, 128)
+    sums, g_sum = back(part, g_part)
+    top = sums[:, :32]
+    out_query = top[:, :, :512].transpose(1, 0, 2).reshape(32, 2048)
+    out_key = top[:, :, 512:768].transpose(1, 0, 2).reshape(32, 1024)
+    out_value = top[:, :, 768:].transpose(1, 0, 2).reshape(32, 1024)
+    out_out = sums[:, 32:].reshape(4, 64, 256).transpose(1, 0, 2).reshape(64, 1024)
+    out_gains = g_sum.reshape(1024)[:72]
+    return (output, grad_tokens, out_query, out_key, out_value, out_out, out_gate, out_up, out_down, out_gains)
+
+
+def fast_solution(mesh):
+    wide = Mesh(mesh.devices.reshape(2, 2, 2, 2, 2), AXES)
+    rows = ("y", "x")
+    places = ("p", "l", "c")
+    weight = P(AXES, None)
+    return jax.shard_map(
+        fast_device,
+        mesh=wide,
+        in_specs=(P(rows, places, None), P(rows, places, None), P(rows, None)) + (weight,) * 7 + (P(AXES),),
+        out_specs=(P(rows, places, None), P(rows, places, None)) + (weight,) * 7 + (P(AXES),),
+        check_vma=False,
+    )
+
+
+def solution(mesh):
+    if dict(mesh.shape) == {"dp": 4, "ctx": 8}:
+        return fast_solution(mesh)
+    return generic_solution(mesh)

time: 2000 us -> 661 us (0.33)
  waiting for transfers between devices: 1440 us -> 143 us
  Pallas kernels: 0 us -> 255 us
  matrix products: 282 us -> 82.1 us
  blocking collectives: 80.7 us -> 0 us
  local copies, waits for them, and re-layouts: 119 us -> 64.3 us
  starting transfers between devices: 1.46 us -> 35.4 us
    reduce_scatter x11 -> x1, waiting for transfers between devices: 1010 us -> 0.01 us  [fast_device(): lax.psum_scatter(packed, group, scatter_dimension=0, tiled=True)]
    all_gather x11 -> x1, waiting for transfers between devices: 418 us -> 0.01 us  [fast_device(): lax.all_gather(chip_half, group, axis=0, tiled=True)]
    pallas_call x0 -> x6, Pallas kernels: none -> 255 us  [the longest x1 106 us: front(): pl.pallas_call(front_kernel, out_shape=(jax.ShapeDtypeStruct((8, ROWS, MO...]
    dot_general x117 -> x14, matrix products: 282 us -> 82.1 us  [dot(): return lax.dot_general(a, b, dims, preferred_element_type=jnp.float32)]
    ppermute x0 -> x29, waiting for transfers between devices: none -> 143 us  [the longest x23 115 us: swap(): return lax.ppermute(value, name, [(0, 1), (1, 0)])]
    unnamed x2 -> x0, blocking collectives: 80.7 us -> none
    unnamed x410 -> x123, local copies, waits for them, and re-layouts: 68.8 us -> 15.6 us
    ppermute x0 -> x29, starting transfers between devices: none -> 35.3 us  [the longest x23 24 us: swap(): return lax.ppermute(value, name, [(0, 1), (1, 0)])]
  transfers between devices with their start and end apart: 22 -> 31, of which waited for: 19 -> 10; matrix products, arithmetic and copies ran while one was open for 17% -> 23% of each run, Pallas kernels for 0% -> 39%
where the time goes in v1:
time: 661 us; the launch traced here: 655 us
  Pallas kernels  255 us (39%)
  waiting for transfers between devices  143 us (22%)
  matrix products  82.1 us (12%)
  local copies, waits for them, and re-layouts  64.3 us (10%)
  other arithmetic  58.8 us (9%)
  starting transfers between devices  35.4 us (5%)
  between operations  15.4 us (2%)
    ppermute x23, waiting for transfers between devices, swap(): return lax.ppermute(value, name, [(0, 1), (1, 0)])  115 us
    pallas_call x1, Pallas kernels, front(): pl.pallas_call(front_kernel, out_shape=(jax.ShapeDtypeStruct((8, ROWS, MO...  106 us
    dot_general x14, matrix products, dot(): return lax.dot_general(a, b, dims, preferred_element_type=jnp.float32)  82.1 us
    pallas_call x1, Pallas kernels, back(): pl.pallas_call(back_kernel, out_shape=(jax.ShapeDtypeStruct((4, 48, 1024)...  56.3 us
    pallas_call x1, Pallas kernels, attend_back(): pl.pallas_call(attend_back_kernel, out_shape=(jax.ShapeDtypeStruct((QH, S...  41.2 us
    pallas_call x1, Pallas kernels, attend(): pl.pallas_call(attend_kernel, out_shape=(jax.ShapeDtypeStruct((SEQ_ROWS,...  26.6 us
    ppermute x23, starting transfers between devices, swap(): return lax.ppermute(value, name, [(0, 1), (1, 0)])  24 us
    ppermute x2, waiting for transfers between devices, from_owner(): second = lax.ppermute(pick(rows, 1 - p), ('p', 'l', 'c'), back[1])  17.8 us
  transfers between devices with their start and end apart: 31, of which 10 were waited for; matrix products, arithmetic and copies ran while one was open for 23% of the time, Pallas kernels for 39%

profile of v1, /device:TPU:0, one launch (start us, length us, event | category | flops | bytes accessed | tf_op | source)
XLA Modules:
  0.0 654.7 jit_solution(17262036319369251701)
XLA Ops:
  14.9 106.0 %front_gather.1 = (bf16[8,256,1024]{2,1,0:T(8,128)(2,1)}, bf16[32,48,1024]{2,1,0:T(8,128)(2,1)}, f32[32,8,128]{2,1,0:T(8,128)}) custom-call(bf16[2,256,1024]{2,1,0:T(8,128)(2,1)} %tok.1, bf16[4,48,1024]{2,1,0:T(8,128)(2,1)} %pad_maximum_fusion.7.wa, f32[8,128]{1,0:T(8,128)} %bitcast_convert_fusion.1.gn), custom_call_target="tpu_custom_call" | custom-call | tf_op jit(solution)/shard_map/front_gather/pallas_call | solution.py:527
  123.8 2.0 collective-permute-start.1
  125.8 3.2 slice.103
  129.7 4.0 fusion.24
  134.8 12.4 %project.1 = (bf16[2048,1024]{1,0:T(8,128)(2,1)}, bf16[4,2048,128]{2,1,0:T(8,128)(2,1)}, bf16[2,2048,128]{2,1,0:T(8,128)(2,1)S(1)}, bf16[2,2048,128]{2,1,0:T(8,1...) custom-call(bf16[2048,1024]{1,0:T(8,128)(2,1)} %bitcast.280, bf16[1024,1024]{1,0:T(8,128)(2,1)} %bitcast.287, ...), custom_call_target="tpu_custom_call" | custom-call | flops 4294967296 | bytes 25165824 | tf_op jit(solution)/shard_map/project/pallas_call | solution.py:670
  147.2 2.7 collective-permute-done.2
  149.8 26.6 %attend.1 = (bf16[2048,512]{1,0:T(8,128)(2,1)S(1)}, f32[4,8,2048]{2,1,0:T(8,128)S(1)}) custom-call(s32[8]{0:T(128)S(1)} %convert_element_type.118.flags, bf16[4,2048,128]{2,1,0:T(8,128)(2,1)} %get-tuple-element.31.q_ref, bf16[2,2048,128]{2,1,0:T(8,128)(2,1)S(1)} %get-tuple-element.32.k_ref, bf16[2,2048,128]{2,1,0:T(8,128)(2,1)S(1)} %get-tuple-element.33.v_ref), custom_call_target="tpu_custom_call" | custom-call | flops 8589934592 | bytes 8388608 | tf_op jit(solution)/shard_map/attend/pallas_call | solution.py:725
  177.5 2.1 maximum_select_fusion.14
  181.1 2.4 fusion.30
  183.5 3.2 copy-done.26
  186.7 1.7 fusion.12
  189.9 1.7 collective-permute-start.12
  193.1 11.1 %collective-permute-done.13 = bf16[256,1024]{1,0:T(8,128)(2,1)S(1)} collective-permute-done((bf16[256,1024]{1,0:T(8,128)(2,1)}, bf16[256,1024]{1,0:T(8,128)(2,1)S(1)}, u32[]{:S(2)}, u32[]{:S(2)}) %collective-permute-start.13) | collective-permute-done | bytes 524320 | tf_op jit(solution)/shard_map/ppermute | solution.py:896
  204.3 2.2 collective-permute-start.14
  206.5 3.5 bitcast_add_fusion.1
  210.0 2.0 copy-done.23
  213.2 11.6 %collective-permute-start.5 = (bf16[512,1024]{1,0:T(8,128)(2,1)}, bf16[512,1024]{1,0:T(8,128)(2,1)}, u32[]{:S(2)}, u32[]{:S(2)}) collective-permute-start(bf16[512,1024]{1,0:T(8,128)(2,1)} %fusion.20), channel_id=1, source_target_pairs={{0,2},{2,0},{1,3},{3,1},{4,6},{6,4},{5,7},{7,5},{8,10},{10,8},{9,1... | collective-permute-start | bytes 3145736 | tf_op jit(solution)/shard_map/ppermute | solution.py:873
  224.8 1.7 maximum_select_fusion.4
  226.4 22.2 %collective-permute-done.5 = bf16[512,1024]{1,0:T(8,128)(2,1)} collective-permute-done((bf16[512,1024]{1,0:T(8,128)(2,1)}, bf16[512,1024]{1,0:T(8,128)(2,1)}, u32[]{:S(2)}, u32[]{:S(2)}) %collective-permute-start.5) | collective-permute-done | bytes 1048608 | tf_op jit(solution)/shard_map/ppermute | solution.py:873
  248.6 2.2 multiply_reduce_fusion.2
  253.5 6.7 %fusion.37 = (bf16[32,1,32,1536]{3,2,1,0:T(8,128)(2,1)}, bf16[32,1,32,1536]{3,2,1,0:T(8,128)(2,1)}, bf16[32,1,32,1536]{3,2,1,0:T(8,128)(2,1)}) fusion(bf16[32,3,32,1536]{3,2,1,0:T(8,128)(2,1)} %bitcast.261), kind=kLoop, calls=%fused_computation.159 | loop fusion | bytes 18874368 | tf_op jit(solution)/shard_map/slice | solution.py:990
  260.1 5.8 reshape_squeeze.17
  266.0 2.2 constant_dynamic-slice_fusion.5
  268.7 2.1 maximum_select_fusion.3
  271.2 3.4 fusion.44
  274.7 5.3 fusion.43
  280.7 2.3 copy-done.34
  283.0 9.4 %multiply_convert_fusion = (bf16[1024,1536]{1,0:T(8,128)(2,1)S(1)}, bf16[1024,1536]{1,0:T(8,128)(2,1)}, bf16[1024,1536]{1,0:T(8,128)(2,1)}) fusion(f32[1024,1536]{1,0:T(8,128)} %fusion.43, f32[1024,1536]{1,0:T(8,128)S(1)} %fusion.44, bf16[1024,1024]{1,0:T(8,128)(2,1)S(1)} %bitcast.289, bf16[1536,512]{1,0:T(8,128)(2,1)S(1)} %get-tuple-element.65, ...), kind=kOutput, calls=%fused_computation.1 | convolution fusion | flops 3251109888 | bytes 27262976 | tf_op jit(solution)/shard_map/dot_general | solution.py:422
  292.5 6.7 %convolution_convert_fusion = bf16[1536,1024]{1,0:T(8,128)(2,1)S(1)} fusion(bf16[1024,1536]{1,0:T(8,128)(2,1)} %get-tuple-element.55, bf16[1024,1024]{1,0:T(8,128)(2,1)S(1)} %bitcast.290), kind=kOutput, calls=%fused_computation.11 | convolution fusion | flops 3222798336 | bytes 8388608 | tf_op jit(solution)/shard_map/dot_general | solution.py:422
  300.7 13.8 %convolution_convert_fusion.1 = bf16[1024,1536]{1,0:T(8,128)(2,1)} fusion(bf16[1024,1024]{1,0:T(8,128)(2,1)S(1)} %bitcast.293, bf16[1024,1536]{1,0:T(8,128)(2,1)S(1)} %get-tuple-element.53), kind=kOutput, calls=%fused_computation.12 | convolution fusion | flops 3222798336 | bytes 8388608 | tf_op jit(solution)/shard_map/dot_general | solution.py:422
  314.5 5.0 convolution_convert_fusion.2
  319.5 2.0 maximum_select_fusion.2
  321.5 5.9 select_n.304
  327.4 8.3 %pad_maximum_fusion = bf16[32,3,32,1536]{3,2,1,0:T(8,128)(2,1)} fusion(bf16[32,1,32,1536]{3,2,1,0:T(8,128)(2,1)} %bitcast.260, bf16[32,1,32,1536]{3,2,1,0:T(8,128)(2,1)} %bitcast.277, bf16[32,1,32,1536]{3,2,1,0:T(8,128)(2,1)} %bitcast.278), kind=kLoop, calls=%fused_computation | loop fusion | flops 9437184 | bytes 18874368 | tf_op jit(solution)/shard_map/stack | solution.py:1011
  335.8 6.4 fusion.45
  342.2 3.4 convolution_add_fusion
  346.1 3.9 collective-permute-done.15
  351.5 1.8 collective-permute-start.17
  353.3 51.1 %collective-permute-done.17 = bf16[512,1024]{1,0:T(8,128)(2,1)S(1)} collective-permute-done((bf16[512,1024]{1,0:T(8,128)(2,1)S(1)}, bf16[512,1024]{1,0:T(8,128)(2,1)S(1)}, u32[]{:S(2)}, u32[]{:S(2)}) %collective-permute-start.17) | collective-permute-done | bytes 1048608 | tf_op jit(solution)/shard_map/ppermute | solution.py:873
  404.8 2.3 collective-permute-done.18
  408.7 3.8 convolution_convert_fusion.3.do_ref
  412.5 41.2 %attend_back.1 = (f32[4,2048,128]{2,1,0:T(8,128)}, f32[2,2048,128]{2,1,0:T(8,128)S(1)}, bf16[2,2048,128]{2,1,0:T(8,128)(2,1)S(1)}) custom-call(s32[8]{0:T(128)S(1)} %convert_element_type.118.flags, bf16[4,2048,128]{2,1,0:T(8,128)(2,1)} %get-tuple-element.31.q_ref, bf16[2,2048,128]{2,1,0:T(8,128)(2,1)S(1)} %get-tuple-element.32.k_ref, ...), custom_call_target="tpu_custom_call" | custom-call | flops 21474836480 | bytes 16777216 | tf_op jit(solution)/shard_map/attend_back/pallas_call | solution.py:793
  453.8 12.7 %unrope.1 = (bf16[2048,1024]{1,0:T(8,128)(2,1)}, f32[2,8,128]{2,1,0:T(8,128)S(1)}) custom-call(f32[4,2048,128]{2,1,0:T(8,128)} %get-tuple-element.36.dq_ref, f32[2,2048,128]{2,1,0:T(8,128)S(1)} %get-tuple-element.37.dk_ref, bf16[2,2048,128]{2,1,0:T(8,128)(2,1)S(1)} %get-tuple-element.38.dv_ref, f32[4,2048,128]{2,1,0:T(8,128)} %get-tuple-element.39.qr_ref, ...), custom_call_target="tpu_custom_call" | custom-call | flops 41943040 | bytes 25165824 | tf_op jit(solution)/shard_map/unrope/pallas_call | solution.py:857
  466.5 6.5 fusion.46
  473.0 3.2 copy-done.25
  476.2 1.6 fusion.11
  478.5 4.6 convolution_convert_fusion.5
  484.1 2.2 constant_dynamic-slice_fusion.4
  486.5 5.5 fusion.16
  494.0 1.8 collective-permute-start.24
  495.7 3.7 collective-permute-done.25
  499.6 2.8 bitcast_add_fusion
  504.3 5.7 convolution_convert_fusion.4
  510.5 1.5 select_n.302
  512.0 2.5 pad_maximum_fusion.2.part
  514.4 27.5 %collective-permute-done.20 = bf16[512,1024]{1,0:T(8,128)(2,1)} collective-permute-done((bf16[512,1024]{1,0:T(8,128)(2,1)}, bf16[512,1024]{1,0:T(8,128)(2,1)}, u32[]{:S(2)}, u32[]{:S(2)}) %collective-permute-start.20) | collective-permute-done | bytes 1048608 | tf_op jit(solution)/shard_map/ppermute | solution.py:873
  541.9 2.4 fusion.9
  544.5 5.5 fusion.8
  551.0 5.3 collective-permute-start.10
  556.3 56.3 %back_reduce.1 = (f32[4,48,1024]{2,1,0:T(8,128)S(1)}, f32[8,128]{1,0:T(8,128)S(1)}) custom-call(bf16[32,48,1024]{2,1,0:T(8,128)(2,1)S(1)} %pad_maximum_fusion.2.part, f32[32,8,128]{2,1,0:T(8,128)S(1)} %bitcast.254), custom_call_target="tpu_custom_call" | custom-call | tf_op jit(solution)/shard_map/back_reduce/pallas_call | solution.py:617
  616.2 2.1 collective-permute-start.22
  623.1 2.7 maximum_select_fusion.8
  625.8 17.8 %collective-permute-done.22 = bf16[256,1024]{1,0:T(8,128)(2,1)S(1)} collective-permute-done((bf16[256,1024]{1,0:T(8,128)(2,1)S(1)}, bf16[256,1024]{1,0:T(8,128)(2,1)S(1)}, u32[]{:S(2)}, u32[]{:S(2)}) %collective-permute-start.22) | collective-permute-done | bytes 524320 | tf_op jit(solution)/shard_map/ppermute | solution.py:904
  643.6 1.5 fusion.23
  (243 shorter events, 46.7 us)
Async XLA Ops:
  7.2 121.9 %copy-start = (s32[2,4]{1,0:T(2,128)S(1)}, s32[2,4]{1,0:T(2,128)}, u32[]{:S(2)}) copy-start(s32[2,4]{1,0:T(2,128)} %param.13) | copy-start | bytes 100
  7.2 246.3 %all-gather.2.cloned.1.call-start = ((), (), s32[]{:S(2)}) async-start(), calls=%async_computation.1 | async-start | bytes 10027008 | tf_op jit(solution)/shard_map/all_gather | solution.py:948
  10.6 1.7 collective-permute-start.7
  13.3 607.4 %reduce-scatter.2.cloned.1.call-start = ((), (), s32[]{:S(2)}) async-start(), calls=%async_computation.2 | async-start | bytes 10027008 | tf_op jit(solution)/shard_map/reduce_scatter | solution.py:1014
  123.8 26.0 %collective-permute-start.2 = (bf16[512,256]{1,0:T(8,128)(2,1)S(1)}, bf16[512,256]{1,0:T(8,128)(2,1)}, u32[]{:S(2)}, u32[]{:S(2)}) collective-permute-start(bf16[512,256]{1,0:T(8,128)(2,1)S(1)} %get-tuple-element.87), channel_id=1, source_target_pairs={{0,2},{2,0},{1,3},{3,1},{4,6},{6,4},{5,7},{7,5},{8,10},{10,8},{9,1... | collective-permute-start | bytes 786440 | tf_op jit(solution)/shard_map/ppermute | solution.py:873
  123.8 55.8 %collective-permute-start.1 = (bf16[512,256]{1,0:T(8,128)(2,1)}, bf16[512,256]{1,0:T(8,128)(2,1)}, u32[]{:S(2)}, u32[]{:S(2)}) collective-permute-start(bf16[512,256]{1,0:T(8,128)(2,1)} %get-tuple-element.88), channel_id=1, source_target_pairs={{0,2},{2,0},{1,3},{3,1},{4,6},{6,4},{5,7},{7,5},{8,10},{10,8},{9,1... | collective-permute-start | bytes 786440 | tf_op jit(solution)/shard_map/ppermute | solution.py:873
  125.8 51.7 %collective-permute-start = (bf16[512,256]{1,0:T(8,128)(2,1)}, bf16[512,256]{1,0:T(8,128)(2,1)}, u32[]{:S(2)}, u32[]{:S(2)}) collective-permute-start(bf16[512,256]{1,0:T(8,128)(2,1)} %get-tuple-element.89), channel_id=1, source_target_pairs={{0,1},{1,0},{2,3},{3,2},{4,5},{5,4},{6,7},{7,6},{8,9},{9,8},{10,11... | collective-permute-start | bytes 786440 | tf_op jit(solution)/shard_map/ppermute | solution.py:873
  129.4 5.1 copy-start.9
  129.4 5.1 copy-start.11
  129.4 5.1 copy-start.7
  134.5 12.7 %copy-start.4 = (f32[2048,128]{1,0:T(8,128)}, f32[2048,128]{1,0:T(8,128)S(1)}, u32[]{:S(2)}) copy-start(f32[2048,128]{1,0:T(8,128)S(1)} %pad_maximum_fusion.6.sin_ref) | copy-start | bytes 3145732
  149.8 29.8 %collective-permute-start.3 = (bf16[512,256]{1,0:T(8,128)(2,1)}, bf16[512,256]{1,0:T(8,128)(2,1)}, u32[]{:S(2)}, u32[]{:S(2)}) collective-permute-start(bf16[512,256]{1,0:T(8,128)(2,1)} %collective-permute-done.2), channel_id=1, source_target_pairs={{0,1},{1,0},{2,3},{3,2},{4,5},{5,4},{6,7},{7,6},{8,9},{9,8},{10,11... | collective-permute-start | bytes 786440 | tf_op jit(solution)/shard_map/ppermute | solution.py:873
  177.5 6.0 copy-start.13
  179.6 3.9 copy-start.40
  188.4 18.1 %collective-permute-start.4 = (bf16[2,512,1024]{2,1,0:T(8,128)(2,1)}, bf16[2,512,1024]{2,1,0:T(8,128)(2,1)}, u32[]{:S(2)}, u32[]{:S(2)}) collective-permute-start(bf16[2,512,1024]{2,1,0:T(8,128)(2,1)} %fusion.12), channel_id=1, source_target_pairs={{0,1},{1,0},{2,3},{3,2},{4,5},{5,4},{6,7},{7,6},{8,9},{9,8},{10,11... | collective-permute-start | bytes 6291464 | tf_op jit(solution)/shard_map/ppermute | solution.py:873
  189.9 3.1 collective-permute-start.12
  191.6 12.5 %collective-permute-start.13 = (bf16[256,1024]{1,0:T(8,128)(2,1)}, bf16[256,1024]{1,0:T(8,128)(2,1)S(1)}, u32[]{:S(2)}, u32[]{:S(2)}) collective-permute-start(bf16[256,1024]{1,0:T(8,128)(2,1)} %get-tuple-element.83), channel_id=1, source_target_pairs={{0,4},{1,0},{2,5},{3,1},{4,6},{5,2},{6,7},{7,3},{8,12},{9,8},{10,1... | collective-permute-start | bytes 1572872 | tf_op jit(solution)/shard_map/ppermute | solution.py:896
  204.3 20.5 %copy-start.21 = (bf16[2,256,1024]{2,1,0:T(8,128)(2,1)}, bf16[2,256,1024]{2,1,0:T(8,128)(2,1)S(1)}, u32[]{:S(2)}) copy-start(bf16[2,256,1024]{2,1,0:T(8,128)(2,1)S(1)} %maximum_select_fusion.9) | copy-start | bytes 3145732
  204.3 20.5 %collective-permute-start.14 = (bf16[512,1024]{1,0:T(8,128)(2,1)S(1)}, bf16[512,1024]{1,0:T(8,128)(2,1)S(1)}, u32[]{:S(2)}, u32[]{:S(2)}) collective-permute-start(bf16[512,1024]{1,0:T(8,128)(2,1)S(1)} %bitcast.258), channel_id=1, source_target_pairs={{0,1},{1,0},{2,3},{3,2},{4,5},{5,4},{6,7},{7,6},{8,9},{9,8},{10,11... | collective-permute-start | bytes 3145736 | tf_op jit(solution)/shard_map/ppermute | solution.py:873
  213.2 35.4 %collective-permute-start.5 = (bf16[512,1024]{1,0:T(8,128)(2,1)}, bf16[512,1024]{1,0:T(8,128)(2,1)}, u32[]{:S(2)}, u32[]{:S(2)}) collective-permute-start(bf16[512,1024]{1,0:T(8,128)(2,1)} %fusion.20), channel_id=1, source_target_pairs={{0,2},{2,0},{1,3},{3,1},{4,6},{6,4},{5,7},{7,5},{8,10},{10,8},{9,1... | collective-permute-start | bytes 3145736 | tf_op jit(solution)/shard_map/ppermute | solution.py:873
  224.8 23.8 %copy-start.24 = (f32[2,512,1024]{2,1,0:T(8,128)S(1)}, f32[2,512,1024]{2,1,0:T(8,128)}, u32[]{:S(2)}) copy-start(f32[2,512,1024]{2,1,0:T(8,128)} %copy-done.23) | copy-start | bytes 12582916
  250.8 100.0 %copy-start.17 = (f32[512,1024]{1,0:T(8,128)}, f32[512,1024]{1,0:T(8,128)S(1)}, u32[]{:S(2)}) copy-start(f32[512,1024]{1,0:T(8,128)S(1)} %get-tuple-element.52) | copy-start | bytes 6291460
  252.2 16.5 %collective-permute-start.6 = (bf16[512,1024]{1,0:T(8,128)(2,1)}, bf16[512,1024]{1,0:T(8,128)(2,1)}, u32[]{:S(2)}, u32[]{:S(2)}) collective-permute-start(bf16[512,1024]{1,0:T(8,128)(2,1)} %multiply_convert_fusion.3), channel_id=1, source_target_pairs={{0,1},{1,0},{2,3},{3,2},{4,5},{5,4},{6,7},{7,6},{8,9},{9,8},{10,11... | collective-permute-start | bytes 3145736 | tf_op jit(solution)/shard_map/ppermute | solution.py:873
  268.1 11.8 %collective-permute-start.8 = (bf16[1536,512]{1,0:T(8,128)(2,1)S(1)}, bf16[1536,512]{1,0:T(8,128)(2,1)S(1)}, u32[]{:S(2)}, u32[]{:S(2)}) collective-permute-start(bf16[1536,512]{1,0:T(8,128)(2,1)S(1)} %get-tuple-element.67), channel_id=1, source_target_pairs={{0,1},{1,0},{2,3},{3,2},{4,5},{5,4},{6,7},{7,6},{8,9},{9,8},{10,11... | collective-permute-start | bytes 4718600 | tf_op jit(solution)/shard_map/ppermute | solution.py:873
  280.7 11.8 %copy-start.35 = (bf16[1536,512]{1,0:T(8,128)(2,1)}, bf16[1536,512]{1,0:T(8,128)(2,1)S(1)}, u32[]{:S(2)}) copy-start(bf16[1536,512]{1,0:T(8,128)(2,1)S(1)} %get-tuple-element.64) | copy-start | bytes 4718596
  280.7 11.8 %copy-start.37 = (bf16[1536,512]{1,0:T(8,128)(2,1)}, bf16[1536,512]{1,0:T(8,128)(2,1)S(1)}, u32[]{:S(2)}) copy-start(bf16[1536,512]{1,0:T(8,128)(2,1)S(1)} %get-tuple-element.65) | copy-start | bytes 4718596
  292.5 8.2 %copy-start.52 = (bf16[1024,1536]{1,0:T(8,128)(2,1)}, bf16[1024,1536]{1,0:T(8,128)(2,1)S(1)}, u32[]{:S(2)}) copy-start(bf16[1024,1536]{1,0:T(8,128)(2,1)S(1)} %get-tuple-element.53) | copy-start | bytes 9437188
  300.6 18.9 %collective-permute-start.27 = (bf16[1536,512]{1,0:T(8,128)(2,1)S(1)}, bf16[1536,512]{1,0:T(8,128)(2,1)S(1)}, u32[]{:S(2)}, u32[]{:S(2)}) collective-permute-start(bf16[1536,512]{1,0:T(8,128)(2,1)S(1)} %get-tuple-element.61), channel_id=1, source_target_pairs={{0,1},{1,0},{2,3},{3,2},{4,5},{5,4},{6,7},{7,6},{8,9},{9,8},{10,11... | collective-permute-start | bytes 4718600 | tf_op jit(solution)/shard_map/ppermute | solution.py:873
  300.7 13.8 %copy-start.54 = (bf16[1024,1536]{1,0:T(8,128)(2,1)S(1)}, bf16[1024,1536]{1,0:T(8,128)(2,1)}, u32[]{:S(2)}) copy-start(bf16[1024,1536]{1,0:T(8,128)(2,1)} %get-tuple-element.54) | copy-start | bytes 9437188
  335.8 6.5 copy-start.30
  335.8 6.5 copy-start.53
  345.8 5.0 copy-start.22
  345.8 4.2 collective-permute-start.15
  350.8 56.6 %copy-start.20 = (f32[512,1024]{1,0:T(8,128)}, f32[512,1024]{1,0:T(8,128)S(1)}, u32[]{:S(2)}) copy-start(f32[512,1024]{1,0:T(8,128)S(1)} %get-tuple-element.50) | copy-start | bytes 6291460
  351.5 52.9 %collective-permute-start.17 = (bf16[512,1024]{1,0:T(8,128)(2,1)S(1)}, bf16[512,1024]{1,0:T(8,128)(2,1)S(1)}, u32[]{:S(2)}, u32[]{:S(2)}) collective-permute-start(bf16[512,1024]{1,0:T(8,128)(2,1)S(1)} %fusion.36), channel_id=1, source_target_pairs={{0,2},{2,0},{1,3},{3,1},{4,6},{6,4},{5,7},{7,5},{8,10},{10,8},{9,1... | collective-permute-start | bytes 3145736 | tf_op jit(solution)/shard_map/ppermute | solution.py:873
  353.3 51.1 %collective-permute-start.16 = (bf16[512,1024]{1,0:T(8,128)(2,1)S(1)}, bf16[512,1024]{1,0:T(8,128)(2,1)S(1)}, u32[]{:S(2)}, u32[]{:S(2)}) collective-permute-start(bf16[512,1024]{1,0:T(8,128)(2,1)S(1)} %fusion.36), channel_id=1, source_target_pairs={{0,1},{1,0},{2,3},{3,2},{4,5},{5,4},{6,7},{7,6},{8,9},{9,8},{10,11... | collective-permute-start | bytes 3145736 | tf_op jit(solution)/shard_map/ppermute | solution.py:873
  404.4 2.7 collective-permute-start.18
  408.6 3.9 copy-start.28
  408.7 3.8 copy-start.16
  412.5 41.3 %copy-start.3 = (f32[2048,128]{1,0:T(8,128)S(1)}, f32[2048,128]{1,0:T(8,128)}, u32[]{:S(2)}) copy-start(f32[2048,128]{1,0:T(8,128)} %copy-done.2) | copy-start | bytes 3145732
  412.5 41.3 %copy-start.5 = (f32[2048,128]{1,0:T(8,128)S(1)}, f32[2048,128]{1,0:T(8,128)}, u32[]{:S(2)}) copy-start(f32[2048,128]{1,0:T(8,128)} %copy-done.4) | copy-start | bytes 3145732
  412.5 41.3 %copy-start.10 = (f32[1,128]{1,0:T(1,128)S(1)}, f32[1,128]{1,0:T(1,128)}, u32[]{:S(2)}) copy-start(f32[1,128]{1,0:T(1,128)} %copy-done.9) | copy-start | bytes 1540
  412.5 41.3 %copy-start.12 = (f32[1,128]{1,0:T(1,128)S(1)}, f32[1,128]{1,0:T(1,128)}, u32[]{:S(2)}) copy-start(f32[1,128]{1,0:T(1,128)} %copy-done.11) | copy-start | bytes 1540
  453.8 12.7 %copy-start.33 = (bf16[32,32,1024]{2,1,0:T(8,128)(2,1)S(1)}, bf16[32,32,1024]{2,1,0:T(8,128)(2,1)}, u32[]{:S(2)}) copy-start(bf16[32,32,1024]{2,1,0:T(8,128)(2,1)} %slice.103) | copy-start | bytes 6291460
  477.8 21.7 %collective-permute-start.19 = (bf16[2,512,1024]{2,1,0:T(8,128)(2,1)}, bf16[2,512,1024]{2,1,0:T(8,128)(2,1)}, u32[]{:S(2)}, u32[]{:S(2)}) collective-permute-start(bf16[2,512,1024]{2,1,0:T(8,128)(2,1)} %fusion.11), channel_id=1, source_target_pairs={{0,1},{1,0},{2,3},{3,2},{4,5},{5,4},{6,7},{7,6},{8,9},{9,8},{10,11... | collective-permute-start | bytes 6291464 | tf_op jit(solution)/shard_map/ppermute | solution.py:873
  486.3 13.2 %slice-start = ((s8[8388608]{0:T(1024)(128)(4,1)}), s8[4194304]{0:T(1024)(128)(4,1)S(1)}, s32[]{:S(2)}) async-start(s8[8388608]{0:T(1024)(128)(4,1)} %bitcast.262), calls=%async_computation.3 | async-start | bytes 8388608
  486.4 13.2 %slice-start.1 = ((s8[8388608]{0:T(1024)(128)(4,1)}), s8[4194304]{0:T(1024)(128)(4,1)S(1)}, s32[]{:S(2)}) async-start(s8[8388608]{0:T(1024)(128)(4,1)} %bitcast.262), calls=%async_computation.4 | async-start | bytes 8388608
  486.4 13.0 %collective-permute-start.25 = (bf16[512,256]{1,0:T(8,128)(2,1)S(1)}, bf16[512,256]{1,0:T(8,128)(2,1)S(1)}, u32[]{:S(2)}, u32[]{:S(2)}) collective-permute-start(bf16[512,256]{1,0:T(8,128)(2,1)S(1)} %bitcast.314), channel_id=1, source_target_pairs={{0,2},{2,0},{1,3},{3,1},{4,6},{6,4},{5,7},{7,5},{8,10},{10,8},{9,1... | collective-permute-start | bytes 786440 | tf_op jit(solution)/shard_map/ppermute | solution.py:873
  492.0 7.5 %copy-start.32 = (f32[1024,1024]{1,0:T(8,128)}, f32[1024,1024]{1,0:T(8,128)S(1)}, u32[]{:S(2)}) copy-start(f32[1024,1024]{1,0:T(8,128)S(1)} %fusion.16) | copy-start | bytes 12582916
  493.3 51.1 %collective-permute-start.9 = (bf16[512,1024]{1,0:T(8,128)(2,1)}, bf16[512,1024]{1,0:T(8,128)(2,1)}, u32[]{:S(2)}, u32[]{:S(2)}) collective-permute-start(bf16[512,1024]{1,0:T(8,128)(2,1)} %fusion.21), channel_id=1, source_target_pairs={{0,1},{1,0},{2,3},{3,2},{4,5},{5,4},{6,7},{7,6},{8,9},{9,8},{10,11... | collective-permute-start | bytes 3145736 | tf_op jit(solution)/shard_map/ppermute | solution.py:873
  493.6 16.4 %collective-permute-start.23 = (bf16[512,256]{1,0:T(8,128)(2,1)S(1)}, bf16[512,256]{1,0:T(8,128)(2,1)S(1)}, u32[]{:S(2)}, u32[]{:S(2)}) collective-permute-start(bf16[512,256]{1,0:T(8,128)(2,1)S(1)} %bitcast.313), channel_id=1, source_target_pairs={{0,1},{1,0},{2,3},{3,2},{4,5},{5,4},{6,7},{7,6},{8,9},{9,8},{10,11... | collective-permute-start | bytes 786440 | tf_op jit(solution)/shard_map/ppermute | solution.py:873
  494.0 16.2 %collective-permute-start.24 = (bf16[512,256]{1,0:T(8,128)(2,1)S(1)}, bf16[512,256]{1,0:T(8,128)(2,1)S(1)}, u32[]{:S(2)}, u32[]{:S(2)}) collective-permute-start(bf16[512,256]{1,0:T(8,128)(2,1)S(1)} %bitcast.312), channel_id=1, source_target_pairs={{0,2},{2,0},{1,3},{3,1},{4,6},{6,4},{5,7},{7,5},{8,10},{10,8},{9,1... | collective-permute-start | bytes 786440 | tf_op jit(solution)/shard_map/ppermute | solution.py:873
  499.4 10.8 %collective-permute-start.26 = (bf16[512,256]{1,0:T(8,128)(2,1)S(1)}, bf16[512,256]{1,0:T(8,128)(2,1)S(1)}, u32[]{:S(2)}, u32[]{:S(2)}) collective-permute-start(bf16[512,256]{1,0:T(8,128)(2,1)S(1)} %collective-permute-done.25), channel_id=1, source_target_pairs={{0,1},{1,0},{2,3},{3,2},{4,5},{5,4},{6,7},{7,6},{8,9},{9,8},{10,11... | collective-permute-start | bytes 786440 | tf_op jit(solution)/shard_map/ppermute | solution.py:873
  499.5 4.3 copy-start.50
  499.6 4.7 copy-start.51
  502.4 7.7 %copy-start.18 = (f32[2,512,1024]{2,1,0:T(8,128)}, f32[2,512,1024]{2,1,0:T(8,128)S(1)}, u32[]{:S(2)}) copy-start(f32[2,512,1024]{2,1,0:T(8,128)S(1)} %bitcast_add_fusion) | copy-start | bytes 12582916
  503.5 38.4 %collective-permute-start.20 = (bf16[512,1024]{1,0:T(8,128)(2,1)}, bf16[512,1024]{1,0:T(8,128)(2,1)}, u32[]{:S(2)}, u32[]{:S(2)}) collective-permute-start(bf16[512,1024]{1,0:T(8,128)(2,1)} %fusion.22), channel_id=1, source_target_pairs={{0,2},{2,0},{1,3},{3,1},{4,6},{6,4},{5,7},{7,5},{8,10},{10,8},{9,1... | collective-permute-start | bytes 3145736 | tf_op jit(solution)/shard_map/ppermute | solution.py:873
  512.0 30.0 %copy-start.8 = (f32[1024]{0:T(1024)S(1)}, f32[1024]{0:T(1024)}, u32[]{:S(2)}) copy-start(f32[1024]{0:T(1024)} %copy-done.7) | copy-start | bytes 12292
  512.0 30.0 %copy-start.19 = (f32[2,512,1024]{2,1,0:T(8,128)S(1)}, f32[2,512,1024]{2,1,0:T(8,128)}, u32[]{:S(2)}) copy-start(f32[2,512,1024]{2,1,0:T(8,128)} %copy-done.18) | copy-start | bytes 12582916
  551.0 72.1 %collective-permute-start.10 = (bf16[256,1024]{1,0:T(8,128)(2,1)}, bf16[256,1024]{1,0:T(8,128)(2,1)}, u32[]{:S(2)}, u32[]{:S(2)}) collective-permute-start(bf16[256,1024]{1,0:T(8,128)(2,1)} %get-tuple-element.84), channel_id=1, source_target_pairs={{0,0},{4,1},{1,2},{5,3},{2,4},{6,5},{3,6},{7,7},{8,8},{12,9},{9,10... | collective-permute-start | bytes 1572872 | tf_op jit(solution)/shard_map/ppermute | solution.py:903
  556.3 66.8 %collective-permute-start.11 = (bf16[256,1024]{1,0:T(8,128)(2,1)}, bf16[256,1024]{1,0:T(8,128)(2,1)}, u32[]{:S(2)}, u32[]{:S(2)}) collective-permute-start(bf16[256,1024]{1,0:T(8,128)(2,1)} %get-tuple-element.85), channel_id=1, source_target_pairs={{4,0},{0,1},{5,2},{1,3},{6,4},{2,5},{7,6},{3,7},{12,8},{8,9},{13,1... | collective-permute-start | bytes 1572872 | tf_op jit(solution)/shard_map/ppermute | solution.py:904
  615.5 10.3 %collective-permute-start.21 = (bf16[256,1024]{1,0:T(8,128)(2,1)S(1)}, bf16[256,1024]{1,0:T(8,128)(2,1)S(1)}, u32[]{:S(2)}, u32[]{:S(2)}) collective-permute-start(bf16[256,1024]{1,0:T(8,128)(2,1)S(1)} %get-tuple-element.80), channel_id=1, source_target_pairs={{0,0},{4,1},{1,2},{5,3},{2,4},{6,5},{3,6},{7,7},{8,8},{12,9},{9,10... | collective-permute-start | bytes 1572872 | tf_op jit(solution)/shard_map/ppermute | solution.py:903
  616.2 27.3 %collective-permute-start.22 = (bf16[256,1024]{1,0:T(8,128)(2,1)S(1)}, bf16[256,1024]{1,0:T(8,128)(2,1)S(1)}, u32[]{:S(2)}, u32[]{:S(2)}) collective-permute-start(bf16[256,1024]{1,0:T(8,128)(2,1)S(1)} %get-tuple-element.81), channel_id=1, source_target_pairs={{4,0},{0,1},{5,2},{1,3},{6,4},{2,5},{7,6},{3,7},{12,8},{8,9},{13,1... | collective-permute-start | bytes 1572872 | tf_op jit(solution)/shard_map/ppermute | solution.py:904
  621.8 23.3 %collective-permute-start.28 = (bf16[96,1536]{1,0:T(8,128)(2,1)S(1)}, bf16[96,1536]{1,0:T(8,128)(2,1)S(1)}, u32[]{:S(2)}, u32[]{:S(2)}) collective-permute-start(bf16[96,1536]{1,0:T(8,128)(2,1)S(1)} %get-tuple-element.97), channel_id=1, source_target_pairs={{0,1},{1,0},{2,3},{3,2},{4,5},{5,4},{6,7},{7,6},{8,9},{9,8},{10,11... | collective-permute-start | bytes 884744 | tf_op jit(solution)/shard_map/ppermute | solution.py:873
  (24 other events, 59.4 us)
Sparse Core Ops, SparseCore 0:
  13.4 173.2 all-gather.1
  335.9 205.9 reduce-scatter.1

commit v2 on v0

--- a/solution.py
+++ b/solution.py
@@ -1,8 +1,12 @@
+import functools
 import math
 
 import jax
 import jax.numpy as jnp
 from jax import lax
+from jax.experimental import pallas as pl
+from jax.experimental.pallas import tpu as pltpu
+from jax.sharding import Mesh
 from jax.sharding import PartitionSpec as P
 
 MODEL_DIM = 1024
@@ -169,7 +173,7 @@
     return (d_query, key_gradient, value_gradient)
 
 
-def per_device(
+def generic_device(
     tokens, cotangent, starts, w_query, key_matrix, value_matrix, w_out, w_gate, w_up, w_down, gains
 ):
     sequence_count, sequence_rows, model_width = tokens.shape
@@ -362,9 +366,9 @@
     )
 
 
-def solution(mesh):
+def generic_solution(mesh):
     return jax.shard_map(
-        per_device,
+        generic_device,
         mesh=mesh,
         in_specs=(
             P("dp", "ctx", None),
@@ -393,3 +397,1541 @@
         ),
         check_vma=False,
     )
+
+
+AXES = ("y", "x", "p", "l", "c")
+FF = 3072
+HALF_FF = FF // 2
+ROWS = 256
+SEQ_ROWS = SEQUENCE_TOKENS
+OWN = SEQ_ROWS // 4
+BLK = 512
+NBLK = SEQ_ROWS // BLK
+QH = 4
+KH = 2
+MESH = pl.DeviceIdType.MESH
+SCALE = 1.0 / math.sqrt(HEAD_DIM)
+LOG2E = 1.4426950408889634
+NT = (((1,), (1,)), ((), ()))
+TN = (((0,), (0,)), ((), ()))
+
+
+def dot(a, b, dims=None):
+    if dims is None:
+        dims = (((1,), (0,)), ((), ()))
+    return lax.dot_general(a, b, dims, preferred_element_type=jnp.float32)
+
+
+def greet(peers):
+    barrier = pltpu.get_barrier_semaphore()
+    for peer in peers:
+        pl.semaphore_signal(barrier, inc=1, device_id=peer, device_id_type=MESH)
+    pl.semaphore_wait(barrier, len(peers))
+
+
+class Plan:
+    def __init__(self, send_sem, recv_sem):
+        self.send_sem = send_sem
+        self.recv_sem = recv_sem
+        self.count = 0
+        self.entries = []
+
+    def add(self, peer, pairs):
+        self.entries.append((peer, pairs, self.count))
+        self.count += len(pairs)
+        return len(self.entries) - 1
+
+    def copies(self, name):
+        peer, pairs, at = self.entries[name]
+        return [
+            pltpu.make_async_remote_copy(
+                src_ref=src,
+                dst_ref=dst,
+                send_sem=self.send_sem.at[at + k],
+                recv_sem=self.recv_sem.at[at + k],
+                device_id=peer,
+                device_id_type=MESH,
+            )
+            for k, (src, dst) in enumerate(pairs)
+        ]
+
+    def start(self, *names):
+        for name in names:
+            for copy in self.copies(name):
+                copy.start()
+
+    def arrived(self, *names):
+        for name in names:
+            for copy in self.copies(name):
+                copy.wait_recv()
+
+    def sent(self):
+        for name in range(len(self.entries)):
+            for copy in self.copies(name):
+                copy.wait_send()
+
+
+def place():
+    return tuple(lax.axis_index(name) for name in AXES)
+
+
+def peers_of(x, y, p, l, c):
+    return {
+        "c": {"c": 1 - c},
+        "l": {"l": 1 - l},
+        "d": {"l": 1 - l, "c": 1 - c},
+        "p": {"p": 1 - p},
+        "x": {"x": 1 - x},
+        "y": {"y": 1 - y},
+    }
+
+
+def rows_at(index, size, count=1):
+    return pl.ds(pl.multiple_of(index * size, size), size * count)
+
+
+def in_place(*refs):
+    return [(ref, ref) for ref in refs]
+
+
+def front_kernel(tok, wq, wk, wv, wo, gn, wg, wu, wd, inverse, xs, wa, woq, gf, wgu, wdn, cosine, sine, send_sem, recv_sem, local_sem):
+    y, x, p, l, c = place()
+    peer = peers_of(x, y, p, l, c)
+    block = 4 * p + 2 * l + c
+    group = (y * 2 + x) * 8
+    me = group + block
+    t = 2 * l + c
+    net = Plan(send_sem, recv_sem)
+
+    def quarter(q):
+        return [
+            (wq.at[:, rows_at(q, 512)], wa.at[rows_at(me, 32), pl.ds(0, 512)]),
+            (wk.at[:, rows_at(q, 256)], wa.at[rows_at(me, 32), pl.ds(512, 256)]),
+            (wv.at[:, rows_at(q, 256)], wa.at[rows_at(me, 32), pl.ds(768, 256)]),
+            (wo.at[:, rows_at(q, 256)], woq.at[rows_at(me, 64)]),
+            (gn, gf.at[me]),
+        ]
+
+    def half(h):
+        return [
+            (wg.at[:, rows_at(h, HALF_FF)], wgu.at[0, rows_at(me, 32)]),
+            (wu.at[:, rows_at(h, HALF_FF)], wgu.at[1, rows_at(me, 32)]),
+            (wd.at[:, rows_at(h, 512)], wdn.at[rows_at(me, 96)]),
+        ]
+
+    def span(base):
+        return in_place(wa.at[rows_at(base // 4, 128)], woq.at[rows_at(base // 4, 256)], gf.at[pl.ds(base, 4)])
+
+    def chip(yy, xx, pp, ll):
+        slot = (yy * 2 + xx) * 4 + 2 * pp + ll
+        return in_place(wgu.at[:, rows_at(slot, 64)], wdn.at[rows_at(slot, 192)])
+
+    mine, other = group + 4 * p, group + 4 * (1 - p)
+    go_first_l = net.add(peer["l"], quarter(2 * (1 - l) + c))
+    go_first_d = net.add(peer["d"], quarter(2 * (1 - l) + 1 - c))
+    go_first_c = net.add(peer["c"], quarter(2 * l + 1 - c))
+    go_near = net.add(peer["l"], [(tok.at[p], xs.at[block])])
+    upper, lower = pl.ds(0, ROWS // 2), pl.ds(ROWS // 2, ROWS // 2)
+    go_far_0 = net.add(peer["p"], [(tok.at[1 - p, upper], xs.at[block, upper])])
+    go_far_1 = net.add(peer["p"], [(tok.at[1 - p, lower], xs.at[block, lower])])
+    go_near_c = net.add(peer["c"], [(tok.at[p], xs.at[block])])
+    go_across = net.add(peer["p"], span(mine))
+    go_own_x = net.add(peer["x"], span(mine))
+    go_near_relay = net.add(peer["c"], in_place(xs.at[block ^ 2]))
+    go_own_y = net.add(peer["y"], span(mine) + span((y * 2 + 1 - x) * 8 + 4 * p))
+    go_other_y = net.add(peer["y"], span(other))
+    go_far_l0 = net.add(peer["l"], in_place(xs.at[block ^ 4, upper]))
+    go_far_l1 = net.add(peer["l"], in_place(xs.at[block ^ 4, lower]))
+    go_far_relay = net.add(peer["c"], in_place(xs.at[block ^ 4]))
+    go_other_x = net.add(peer["x"], span(other) + span(((1 - y) * 2 + x) * 8 + 4 * (1 - p)))
+    go_far_l_relay = net.add(peer["c"], in_place(xs.at[block ^ 6]))
+    go_mlp_c = net.add(peer["c"], half(1 - c))
+    go_mlp_near = net.add(peer["l"], chip(y, x, p, l))
+    go_mlp_x = net.add(peer["x"], chip(y, x, p, l))
+    go_mlp_y = net.add(peer["y"], chip(y, x, p, 1 - l))
+    greet(list(peer.values()))
+    net.start(go_first_l, go_first_d, go_first_c, go_near_c, go_mlp_c)
+    own = [
+        pltpu.make_async_copy(src, dst, local_sem.at[k])
+        for k, (src, dst) in enumerate(quarter(t) + half(c) + [(tok.at[p], xs.at[block])])
+    ]
+    for copy in own:
+        copy.start()
+
+    def table(first, last):
+        def chunk(k, carry):
+            rows = rows_at(k, 64)
+            position = (lax.broadcasted_iota(jnp.int32, (64, HEAD_DIM), 0) + k * 64).astype(jnp.float32)
+            lane = lax.broadcasted_iota(jnp.int32, (64, HEAD_DIM), 1)
+            angle = position * inverse[0:1, :]
+            cosine[rows, :] = jnp.cos(angle)
+            sine[rows, :] = jnp.where(lane < HEAD_DIM // 2, -1.0, 1.0) * jnp.sin(angle)
+            return carry
+
+        lax.fori_loop(first, last, chunk, 0)
+
+    for copy in own:
+        copy.wait()
+    net.arrived(go_first_l, go_first_d, go_first_c)
+    net.start(go_across, go_own_x, go_near)
+    table(0, 16)
+    net.arrived(go_own_x)
+    net.start(go_own_y)
+    net.arrived(go_mlp_c)
+    net.start(go_mlp_x)
+    net.arrived(go_across)
+    net.start(go_other_y, go_far_0, go_far_1)
+    net.arrived(go_near)
+    net.start(go_near_relay, go_mlp_near)
+    table(16, 32)
+    net.arrived(go_other_y)
+    net.start(go_other_x)
+    net.arrived(go_far_0)
+    net.start(go_far_l0)
+    net.arrived(go_mlp_near)
+    net.start(go_mlp_y)
+    net.arrived(go_far_1)
+    net.start(go_far_l1, go_far_relay)
+    net.arrived(go_far_l0, go_far_l1)
+    net.start(go_far_l_relay)
+    net.arrived(go_near_c, go_near_relay, go_far_relay, go_far_l_relay, go_own_y, go_other_x, go_mlp_x, go_mlp_y)
+    net.sent()
+
+
+def front(tok, wq, wk, wv, wo, gn, wg, wu, wd, inverse):
+    any_spec = pl.BlockSpec(memory_space=pl.ANY)
+    copies = 64
+    bf16 = jnp.bfloat16
+    return pl.pallas_call(
+        front_kernel,
+        out_shape=(
+            jax.ShapeDtypeStruct((8, ROWS, MODEL_DIM), bf16),
+            jax.ShapeDtypeStruct((1024, 1024), bf16),
+            jax.ShapeDtypeStruct((2048, 256), bf16),
+            jax.ShapeDtypeStruct((32, 8, 128), jnp.float32),
+            jax.ShapeDtypeStruct((2, MODEL_DIM, HALF_FF), bf16),
+            jax.ShapeDtypeStruct((FF, 512), bf16),
+            jax.ShapeDtypeStruct((SEQ_ROWS, HEAD_DIM), jnp.float32),
+            jax.ShapeDtypeStruct((SEQ_ROWS, HEAD_DIM), jnp.float32),
+        ),
+        in_specs=[any_spec] * 9 + [pl.BlockSpec(memory_space=pltpu.VMEM)],
+        out_specs=[any_spec] * 6 + [pl.BlockSpec(memory_space=pltpu.VMEM)] * 2,
+        scratch_shapes=[
+            pltpu.SemaphoreType.DMA((copies,)),
+            pltpu.SemaphoreType.DMA((copies,)),
+            pltpu.SemaphoreType.DMA((9,)),
+        ],
+        compiler_params=pltpu.CompilerParams(collective_id=0, has_side_effects=True),
+        name="front_gather",
+    )(tok, wq, wk, wv, wo, gn, wg, wu, wd, inverse)
+
+
+def line_peers(p, l, c):
+    return [
+        {"p": (p + a) % 2, "l": (l + b) % 2, "c": (c + d) % 2}
+        for a in range(2)
+        for b in range(2)
+        for d in range(2)
+        if a + b + d > 0
+    ]
+
+
+class Return:
+    def __init__(self, where, src, dst, send_sem, recv_sem):
+        self.where = where[2:]
+        self.src, self.dst, self.send_sem, self.recv_sem = src, dst, send_sem, recv_sem
+
+    def stays(self, first, second, third, fourth):
+        return (first == second) & (second == third) & (third == fourth)
+
+    def local(self, c0):
+        p, l, c = self.where
+        return pltpu.make_async_copy(self.src.at[pl.ds(c0 * ROWS, ROWS)], self.dst.at[p], self.send_sem.at[c0])
+
+    def remote(self, c0):
+        p, l, c = self.where
+        return pltpu.make_async_remote_copy(
+            src_ref=self.src.at[pl.ds(c0 * ROWS, ROWS)],
+            dst_ref=self.dst.at[p],
+            send_sem=self.send_sem.at[c0],
+            recv_sem=self.recv_sem.at[p],
+            device_id={"p": l, "l": c, "c": c0},
+            device_id_type=MESH,
+        )
+
+    def start(self):
+        p, l, c = self.where
+        for c0 in range(2):
+            here = self.stays(p, l, c, c0)
+
+            @pl.when(here)
+            def _():
+                self.local(c0).start()
+
+            @pl.when(jnp.logical_not(here))
+            def _():
+                self.remote(c0).start()
+
+    def wait(self):
+        p, l, c = self.where
+        for c0 in range(2):
+            here = self.stays(p, l, c, c0)
+
+            @pl.when(here)
+            def _():
+                self.local(c0).wait()
+
+            @pl.when(jnp.logical_not(here))
+            def _():
+                self.remote(c0).wait_send()
+
+        for seq in range(2):
+
+            @pl.when(jnp.logical_not(self.stays(seq, p, l, c)))
+            def _():
+                pltpu.make_async_remote_copy(
+                    src_ref=self.src.at[pl.ds(0, ROWS)],
+                    dst_ref=self.dst.at[seq],
+                    send_sem=self.send_sem.at[0],
+                    recv_sem=self.recv_sem.at[seq],
+                    device_id={"p": l, "l": c, "c": 1 - c},
+                    device_id_type=MESH,
+                ).wait_recv()
+
+
+class Spread:
+    def __init__(self, where, src, dst, send_sem, recv_sem):
+        self.where = where[2:]
+        self.src, self.dst, self.send_sem, self.recv_sem = src, dst, send_sem, recv_sem
+
+    def here(self, first):
+        p, l, c = self.where
+        return (first == p) & (p == l) & (l == c)
+
+    def local(self, seq):
+        p, l, c = self.where
+        return pltpu.make_async_copy(self.src.at[seq], self.dst.at[l, c], self.send_sem.at[seq])
+
+    def remote(self, seq):
+        p, l, c = self.where
+        return pltpu.make_async_remote_copy(
+            src_ref=self.src.at[seq],
+            dst_ref=self.dst.at[l, c],
+            send_sem=self.send_sem.at[seq],
+            recv_sem=self.recv_sem.at[c],
+            device_id={"p": seq, "l": p, "c": l},
+            device_id_type=MESH,
+        )
+
+    def start(self):
+        for seq in range(2):
+
+            @pl.when(self.here(seq))
+            def _():
+                self.local(seq).start()
+
+            @pl.when(jnp.logical_not(self.here(seq)))
+            def _():
+                self.remote(seq).start()
+
+    def wait(self):
+        p, l, c = self.where
+        for seq in range(2):
+
+            @pl.when(self.here(seq))
+            def _():
+                self.local(seq).wait()
+
+            @pl.when(jnp.logical_not(self.here(seq)))
+            def _():
+                self.remote(seq).wait_send()
+
+        for block in range(2):
+
+            @pl.when(jnp.logical_not((l == p) & (c == l) & (block == c)))
+            def _():
+                pltpu.make_async_remote_copy(
+                    src_ref=self.src.at[0],
+                    dst_ref=self.dst.at[c, block],
+                    send_sem=self.send_sem.at[0],
+                    recv_sem=self.recv_sem.at[block],
+                    device_id={"p": l, "l": c, "c": 1 - c},
+                    device_id_type=MESH,
+                ).wait_recv()
+
+
+def turn(value):
+    return pltpu.roll(value, HEAD_DIM // 2, 1)
+
+
+def block_mask(key_dim, flags, index):
+    shape = (BLK, BLK)
+    key = lax.broadcasted_iota(jnp.int32, shape, key_dim)
+    query = lax.broadcasted_iota(jnp.int32, shape, 1 - key_dim)
+    upper = query // PIECE
+    piece = jnp.where(upper == 0, flags[2 * index], flags[2 * index + 1])
+    return (key <= query) | ((key // PIECE == upper) & (piece > 0))
+
+
+PROJECT = 8
+
+
+def attend_kernel(
+    flags, x_ref, w_ref, ga_ref, gq_ref, gk_ref, cos_ref, sin_ref, woq, wgu_in, wdn_in,
+    n_ref, q_ref, k_ref, v_ref, qr_ref, kr_ref, o_ref, lse_ref, wo, wgu, wdn,
+    send_sem, recv_sem, local_sem,
+):
+    y, x, p, l, c = place()
+    peer = peers_of(x, y, p, l, c)
+    t = 2 * l + c
+    net = Plan(send_sem, recv_sem)
+
+    def chip(yy, xx, pp, ll):
+        slot = (yy * 2 + xx) * 4 + 2 * pp + ll
+        return in_place(wgu.at[:, rows_at(slot, 64)], wdn.at[rows_at(slot, 192)])
+
+    def rows_of(q):
+        return woq.at[rows_at(q, 512)], wo.at[:, rows_at(t, 256)]
+
+    go_mlp_y = net.add(peer["y"], chip(y, x, p, l) + chip(y, 1 - x, p, l))
+    go_mlp_x = net.add(peer["x"], chip(y, x, p, 1 - l) + chip(1 - y, x, p, 1 - l))
+    go_far = net.add(peer["p"], chip(y, x, p, l))
+    go_far_l = net.add(peer["l"], chip(y, x, 1 - p, l))
+    go_wo_l = net.add(peer["l"], [rows_of(2 * (1 - l) + c)])
+    go_wo_d = net.add(peer["d"], [rows_of(2 * (1 - l) + 1 - c)])
+    go_wo_c = net.add(peer["c"], [rows_of(2 * l + 1 - c)])
+    step = pl.program_id(0)
+
+    @pl.when(step == 0)
+    def _():
+        greet(list(peer.values()))
+        net.start(go_far, go_mlp_y, go_mlp_x, go_wo_l, go_wo_d, go_wo_c)
+        copy = pltpu.make_async_copy(*rows_of(t), local_sem.at[0])
+        copy.start()
+        copy.wait()
+
+    @pl.when(step < PROJECT)
+    def _():
+        value = x_ref[...].astype(jnp.float32)
+        r = lax.rsqrt(jnp.mean(value * value, axis=-1, keepdims=True) + EPS)
+        normed = (value * r * ga_ref[...]).astype(jnp.bfloat16)
+        n_ref[...] = normed
+        full = dot(normed, w_ref[...])
+        cosine, sine = cos_ref[...], sin_ref[...]
+        rows = rows_at(jnp.minimum(step, PROJECT - 1), 256)
+        for h in range(QH + KH):
+            u = full[:, h * HEAD_DIM : (h + 1) * HEAD_DIM]
+            raw_ref, out_ref, g_ref, at = (qr_ref, q_ref, gq_ref, h) if h < QH else (kr_ref, k_ref, gk_ref, h - QH)
+            raw_ref[at] = u
+            n = u * lax.rsqrt(jnp.mean(u * u, axis=-1, keepdims=True) + EPS) * g_ref[...]
+            out_ref[at, rows, :] = (n * cosine + turn(n) * sine).astype(jnp.bfloat16)
+        for h in range(KH):
+            at = (QH + KH + h) * HEAD_DIM
+            v_ref[h, rows, :] = full[:, at : at + HEAD_DIM].astype(jnp.bfloat16)
+
+    @pl.when(step == PROJECT + 4)
+    def _():
+        net.arrived(go_far)
+        net.start(go_far_l)
+
+    @pl.when(step >= PROJECT)
+    def _():
+        order = jnp.maximum(step - PROJECT, 0)
+        g, i = order // NBLK, order % NBLK
+        ones = jnp.ones((BLK, HEAD_DIM), jnp.bfloat16)
+        mask = block_mask(1, flags, i)
+
+        def values(j):
+            return jnp.concatenate([v_ref[g, rows_at(j, BLK), :], ones], axis=1)
+
+        queries = [q_ref[2 * g + h, rows_at(i, BLK), :] for h in range(2)]
+
+        def part(j, masked):
+            keys, both = k_ref[g, rows_at(j, BLK), :], values(j)
+            found = []
+            for q in queries:
+                probs = jnp.exp2(dot(q, keys, NT) * (SCALE * LOG2E))
+                if masked:
+                    probs = jnp.where(mask, probs, 0.0)
+                found.append(dot(probs.astype(jnp.bfloat16), both))
+            return found
+
+        def one(j, accs):
+            return tuple(acc + more for acc, more in zip(accs, part(j, False)))
+
+        accs = lax.fori_loop(0, i, one, tuple(part(i, True)))
+        for h, acc in enumerate(accs):
+            total = acc[:, HEAD_DIM:]
+            o_ref[:, h * HEAD_DIM : (h + 1) * HEAD_DIM] = (acc[:, :HEAD_DIM] / total).astype(jnp.bfloat16)
+            lse_ref[h] = jnp.log2(total).T[0:8, :]
+
+    @pl.when(step == PROJECT + 2 * NBLK - 1)
+    def _():
+        net.arrived(go_mlp_y, go_mlp_x, go_far_l, go_wo_l, go_wo_d, go_wo_c)
+        net.sent()
+
+
+def attend(flags, x, w, ga, gq, gk, cosine, sine, woq, wgu, wdn):
+    bf16, f32 = jnp.bfloat16, jnp.float32
+
+    def early(s):
+        return jnp.minimum(s, PROJECT - 1)
+
+    def late(s):
+        return jnp.maximum(s - PROJECT, 0)
+
+    def row(width):
+        return pl.BlockSpec((256, width), lambda s, f: (early(s), 0))
+
+    def whole(shape):
+        return pl.BlockSpec(shape, lambda s, f: (0,) * len(shape))
+
+    def heads(n):
+        return pl.BlockSpec((n, 256, HEAD_DIM), lambda s, f: (0, early(s), 0))
+
+    def shape(n, dtype):
+        return jax.ShapeDtypeStruct((n, SEQ_ROWS, HEAD_DIM), dtype)
+
+    any_spec = pl.BlockSpec(memory_space=pl.ANY)
+    copies = 20
+    return pl.pallas_call(
+        attend_kernel,
+        out_shape=(
+            jax.ShapeDtypeStruct((SEQ_ROWS, MODEL_DIM), bf16),
+            shape(QH, bf16),
+            shape(KH, bf16),
+            shape(KH, bf16),
+            shape(QH, f32),
+            shape(KH, f32),
+            jax.ShapeDtypeStruct((SEQ_ROWS, QH * HEAD_DIM), bf16),
+            jax.ShapeDtypeStruct((QH, 8, SEQ_ROWS), f32),
+            jax.ShapeDtypeStruct((512, MODEL_DIM), bf16),
+            jax.ShapeDtypeStruct(wgu.shape, bf16),
+            jax.ShapeDtypeStruct(wdn.shape, bf16),
+        ),
+        grid_spec=pltpu.PrefetchScalarGridSpec(
+            num_scalar_prefetch=1,
+            grid=(PROJECT + KH * NBLK,),
+            in_specs=[row(MODEL_DIM), whole(w.shape), whole(ga.shape), whole(gq.shape), whole(gk.shape), row(HEAD_DIM), row(HEAD_DIM)]
+            + [any_spec] * 3,
+            out_specs=[
+                row(MODEL_DIM),
+                whole((QH, SEQ_ROWS, HEAD_DIM)),
+                whole((KH, SEQ_ROWS, HEAD_DIM)),
+                whole((KH, SEQ_ROWS, HEAD_DIM)),
+                heads(QH),
+                heads(KH),
+                pl.BlockSpec((BLK, 2 * HEAD_DIM), lambda s, f: (late(s) % NBLK, late(s) // NBLK)),
+                pl.BlockSpec((2, 8, BLK), lambda s, f: (late(s) // NBLK, 0, late(s) % NBLK)),
+            ]
+            + [any_spec] * 3,
+            scratch_shapes=[pltpu.SemaphoreType.DMA((copies,))] * 2 + [pltpu.SemaphoreType.DMA((1,))],
+        ),
+        input_output_aliases={9: 9, 10: 10},
+        compiler_params=pltpu.CompilerParams(
+            collective_id=2, has_side_effects=True, vmem_limit_bytes=48 * 1024 * 1024
+        ),
+        cost_estimate=pl.CostEstimate(
+            flops=4 * QH * SEQ_ROWS * SEQ_ROWS * HEAD_DIM, bytes_accessed=24 << 20, transcendentals=QH * SEQ_ROWS * SEQ_ROWS
+        ),
+        name="attend",
+    )(flags, x, w, ga, gq, gk, cosine, sine, woq, wgu, wdn)
+
+
+def resid_kernel(
+    attn, wo, g_mlp, xs, cot, wgu_in, wdn_in,
+    resid, mlp_in, wgu, wdn, wdx, wdo, dy,
+    send_c, recv_c, send_l, recv_l, keep, x_own, send_sem, recv_sem, local_sem, dy_send, dy_recv,
+):
+    where = place()
+    y, x, p, l, c = where
+    peer = peers_of(x, y, p, l, c)
+    net = Plan(send_sem, recv_sem)
+
+    def chip(yy, xx, pp, ll):
+        slot = (yy * 2 + xx) * 4 + 2 * pp + ll
+        return in_place(wgu.at[:, rows_at(slot, 64)], wdn.at[rows_at(slot, 192)])
+
+    def down(pp, ll):
+        found = []
+        for xx in range(2):
+            slot = xx * 4 + 2 * pp + ll
+            found.append((wdn.at[rows_at((1 - c) * 8 + slot, 192)], wdx.at[rows_at(slot, 192)]))
+        return found
+
+    go_far_x = net.add(peer["x"], chip(y, x, 1 - p, l))
+    go_far_y = net.add(peer["y"], chip(y, x, 1 - p, l) + chip(y, 1 - x, 1 - p, l))
+    go_fal_y = net.add(peer["y"], chip(y, x, 1 - p, 1 - l))
+    go_fal_x = net.add(peer["x"], chip(y, x, 1 - p, 1 - l) + chip(1 - y, x, 1 - p, 1 - l))
+    go_down_me = net.add(peer["c"], down(p, l))
+    go_down_near = net.add(peer["c"], down(p, 1 - l))
+    go_down_far = net.add(peer["c"], down(1 - p, l))
+    go_down_fal = net.add(peer["c"], down(1 - p, 1 - l))
+    go_give_0 = net.add(peer["c"], [(send_c.at[0], recv_c.at[0])])
+    go_give_1 = net.add(peer["c"], [(send_c.at[1], recv_c.at[1])])
+    go_cross = net.add(peer["l"], [(send_l, recv_l)])
+    go_share = net.add(peer["c"], in_place(mlp_in.at[c]))
+    go_dy_c = net.add(peer["c"], in_place(dy.at[c]))
+    spread = Spread(where, cot, dy, dy_send, dy_recv)
+    greet(line_peers(p, l, c) + [peer["x"], peer["y"]])
+    net.start(go_far_x, go_fal_y, go_down_me, go_down_near)
+    fetch = pltpu.make_async_copy(xs.at[rows_at(2 * l + c, OWN)], x_own, local_sem.at[0])
+    fetch.start()
+    own_down = pltpu.make_async_copy(wdn.at[rows_at(c, HALF_FF)], wdo, local_sem.at[1])
+
+    def project(ll, cc, write):
+        part = attn[rows_at(2 * ll + cc, OWN), :]
+
+        def chunk(k, carry):
+            cols = rows_at(k, 256)
+            write(cols, dot(part, wo[:, cols]))
+            return carry
+
+        lax.fori_loop(0, 4, chunk, 0)
+
+    def give(k):
+        def write(cols, value):
+            send_c[k, :, cols] = value.astype(jnp.bfloat16)
+
+        return write
+
+    def hold(k):
+        def write(cols, value):
+            keep[k, :, cols] = value
+
+        return write
+
+    project(1 - l, 1 - c, give(0))
+    net.start(go_give_0)
+    project(1 - l, c, hold(0))
+    net.arrived(go_give_0)
+    send_l[...] = (keep[0] + recv_c[0].astype(jnp.float32)).astype(jnp.bfloat16)
+    net.start(go_cross)
+    spread.start()
+    project(l, 1 - c, give(1))
+    net.start(go_give_1)
+    project(l, c, hold(1))
+    fetch.wait()
+    net.arrived(go_far_x)
+    net.start(go_far_y)
+    net.arrived(go_fal_y)
+    net.start(go_fal_x)
+    net.arrived(go_give_1)
+    keep[1] += recv_c[1].astype(jnp.float32) + x_own[...].astype(jnp.float32)
+    net.arrived(go_cross)
+    total = keep[1] + recv_l[...].astype(jnp.float32)
+    resid[...] = total
+    r = lax.rsqrt(jnp.mean(total * total, axis=-1, keepdims=True) + EPS)
+    mlp_in[c] = (total * r * g_mlp[...]).astype(jnp.bfloat16)
+    net.start(go_share)
+    net.arrived(go_far_y)
+    net.start(go_down_far)
+    spread.wait()
+    net.start(go_dy_c)
+    net.arrived(go_fal_x)
+    net.start(go_down_fal)
+    own_down.start()
+    net.arrived(go_down_me, go_down_near, go_down_far, go_down_fal, go_share, go_dy_c)
+    own_down.wait()
+    net.sent()
+
+
+def finish_resid(attn, wo, g_mlp, xs, cot, wgu, wdn):
+    bf16, f32 = jnp.bfloat16, jnp.float32
+    any_spec = pl.BlockSpec(memory_space=pl.ANY)
+    vmem = pl.BlockSpec(memory_space=pltpu.VMEM)
+    copies = 32
+    return pl.pallas_call(
+        resid_kernel,
+        out_shape=(
+            jax.ShapeDtypeStruct((OWN, MODEL_DIM), f32),
+            jax.ShapeDtypeStruct((2, OWN, MODEL_DIM), bf16),
+            jax.ShapeDtypeStruct(wgu.shape, bf16),
+            jax.ShapeDtypeStruct(wdn.shape, bf16),
+            jax.ShapeDtypeStruct((HALF_FF, 512), bf16),
+            jax.ShapeDtypeStruct((HALF_FF, 512), bf16),
+            jax.ShapeDtypeStruct((2, 2, ROWS, MODEL_DIM), bf16),
+        ),
+        in_specs=[vmem] * 3 + [any_spec] * 4,
+        out_specs=[vmem] * 2 + [any_spec] * 5,
+        scratch_shapes=[
+            pltpu.VMEM((2, OWN, MODEL_DIM), bf16),
+            pltpu.VMEM((2, OWN, MODEL_DIM), bf16),
+            pltpu.VMEM((OWN, MODEL_DIM), bf16),
+            pltpu.VMEM((OWN, MODEL_DIM), bf16),
+            pltpu.VMEM((2, OWN, MODEL_DIM), f32),
+            pltpu.VMEM((OWN, MODEL_DIM), bf16),
+            pltpu.SemaphoreType.DMA((copies,)),
+            pltpu.SemaphoreType.DMA((copies,)),
+            pltpu.SemaphoreType.DMA((2,)),
+            pltpu.SemaphoreType.DMA((2,)),
+            pltpu.SemaphoreType.DMA((2,)),
+        ],
+        input_output_aliases={5: 2, 6: 3},
+        compiler_params=pltpu.CompilerParams(
+            collective_id=3, has_side_effects=True, vmem_limit_bytes=48 * 1024 * 1024
+        ),
+        name="residual",
+    )(attn, wo, g_mlp, xs, cot, wgu, wdn)
+
+
+CHUNK = 512
+
+
+def forward_kernel(
+    m_ref, dy_ref, w_ref, wo_ref, wx_ref, resid, g_mlp,
+    gg, gu, gd, d_resid, db, res, dg,
+    mt, dyt, hid, dgt, dup, d_in, down, give, take, send_sem, recv_sem,
+):
+    y, x, p, l, c = place()
+    peer = {"c": 1 - c}
+    net = Plan(send_sem, recv_sem)
+    go_d_in = net.add(peer, [(give.at[0], take.at[0])])
+    go_down = net.add(peer, [(give.at[1], take.at[1])])
+    step = pl.program_id(0)
+
+    @pl.when(step == 0)
+    def _():
+        greet([peer])
+
+        def flip(k, carry):
+            rows = rows_at(k, 256)
+            mt[:, rows] = m_ref[rows, :].T
+            dyt[:, rows] = dy_ref[rows, :].T
+            return carry
+
+        lax.fori_loop(0, 4, flip, 0)
+        d_in[...] = jnp.zeros_like(d_in)
+        down[...] = jnp.zeros_like(down)
+
+    own_cols, other_cols = rows_at(c, 512), rows_at(1 - c, 512)
+
+    def part(r, carry):
+        rows = rows_at(r, 256)
+        value, grad = m_ref[rows, :], dy_ref
+        gate, up = dot(value, w_ref[0]), dot(value, w_ref[1])
+        d_hidden = dot(grad[rows, own_cols], wo_ref[...], NT) + dot(grad[rows, other_cols], wx_ref[...], NT)
+        s = 1.0 / (1.0 + jnp.exp(-gate))
+        silu = gate * s
+        hidden = (silu * up).astype(jnp.bfloat16)
+        d_up = (d_hidden * silu).astype(jnp.bfloat16)
+        d_gate = (d_hidden * up * (s * (1.0 + gate * (1.0 - s)))).astype(jnp.bfloat16)
+        hid[rows, :] = hidden
+        dup[rows, :] = d_up
+        dgt[rows, :] = d_gate
+        d_in[rows, :] += dot(d_gate, w_ref[0], NT) + dot(d_up, w_ref[1], NT)
+        down[rows, own_cols] += dot(hidden, wo_ref[...])
+        down[rows, other_cols] += dot(hidden, wx_ref[...])
+        return carry
+
+    lax.fori_loop(0, 4, part, 0)
+
+    @pl.when(step == pl.num_programs(0) - 1)
+    def _():
+        give[0] = d_in[rows_at(1 - c, OWN), :].astype(jnp.bfloat16)
+        give[1] = down[rows_at(1 - c, OWN), :].astype(jnp.bfloat16)
+        net.start(go_d_in, go_down)
+
+    def weights(k, carry):
+        rows = rows_at(k, 256)
+        gg[rows, :] = dot(mt[rows, :], dgt[...]).astype(jnp.bfloat16)
+        gu[rows, :] = dot(mt[rows, :], dup[...]).astype(jnp.bfloat16)
+        gd[:, rows] = dot(dyt[rows, :], hid[...]).T.astype(jnp.bfloat16)
+        return carry
+
+    lax.fori_loop(0, 4, weights, 0)
+
+    @pl.when(step == pl.num_programs(0) - 1)
+    def _():
+        net.arrived(go_d_in, go_down)
+        dg[...] = jnp.zeros_like(dg)
+
+        def finish(k, carry):
+            rows = rows_at(k, 64)
+            here = pl.ds(pl.multiple_of(c * OWN + k * 64, 64), 64)
+            value = resid[rows, :]
+            grad = d_in[here, :] + take[0, rows, :].astype(jnp.float32)
+            r = lax.rsqrt(jnp.mean(value * value, axis=-1, keepdims=True) + EPS)
+            scaled = value * r
+            gained = grad * g_mlp[...]
+            total = dy_ref[here, :].astype(jnp.float32) + r * (gained - scaled * jnp.mean(scaled * gained, axis=-1, keepdims=True))
+            d_resid[rows, :] = total
+            db[rows, :] = total.astype(jnp.bfloat16)
+            dg[...] += jnp.sum((grad * scaled).reshape(-1, 8, MODEL_DIM), axis=0)
+            res[rows, :] = (value + down[here, :] + take[1, rows, :].astype(jnp.float32)).astype(jnp.bfloat16)
+            return carry
+
+        lax.fori_loop(0, 8, finish, 0)
+        net.sent()
+
+
+def feed_forward(mlp_in, dy, wgu, wdo, wdx, resid, g_mlp):
+    bf16, f32 = jnp.bfloat16, jnp.float32
+
+    def whole(shape):
+        return pl.BlockSpec(shape, lambda f: (0,) * len(shape), pipeline_mode=pl.Buffered(1))
+
+    down = pl.BlockSpec((CHUNK, 512), lambda f: (f, 0))
+    wide = pl.BlockSpec((MODEL_DIM, CHUNK), lambda f: (0, f))
+    rows = (1024, MODEL_DIM)
+    own = (OWN, MODEL_DIM)
+    return pl.pallas_call(
+        forward_kernel,
+        grid=(HALF_FF // CHUNK,),
+        out_shape=(
+            jax.ShapeDtypeStruct((MODEL_DIM, HALF_FF), bf16),
+            jax.ShapeDtypeStruct((MODEL_DIM, HALF_FF), bf16),
+            jax.ShapeDtypeStruct((HALF_FF, MODEL_DIM), bf16),
+            jax.ShapeDtypeStruct(own, f32),
+            jax.ShapeDtypeStruct(own, bf16),
+            jax.ShapeDtypeStruct(own, bf16),
+            jax.ShapeDtypeStruct((8, MODEL_DIM), f32),
+        ),
+        in_specs=[whole(rows), whole(rows), pl.BlockSpec((2, MODEL_DIM, CHUNK), lambda f: (0, 0, f)), down, down]
+        + [whole(own), whole((1, MODEL_DIM))],
+        out_specs=[wide, wide, pl.BlockSpec((CHUNK, MODEL_DIM), lambda f: (f, 0))]
+        + [whole(own), whole(own), whole(own), whole((8, MODEL_DIM))],
+        scratch_shapes=[
+            pltpu.VMEM(rows, bf16),
+            pltpu.VMEM(rows, bf16),
+            pltpu.VMEM((1024, CHUNK), bf16),
+            pltpu.VMEM((1024, CHUNK), bf16),
+            pltpu.VMEM((1024, CHUNK), bf16),
+            pltpu.VMEM(rows, f32),
+            pltpu.VMEM(rows, f32),
+            pltpu.VMEM((2,) + own, bf16),
+            pltpu.VMEM((2,) + own, bf16),
+            pltpu.SemaphoreType.DMA((2,)),
+            pltpu.SemaphoreType.DMA((2,)),
+        ],
+        compiler_params=pltpu.CompilerParams(
+            collective_id=6, has_side_effects=True, vmem_limit_bytes=56 * 1024 * 1024
+        ),
+        name="feed_forward",
+    )(mlp_in, dy, wgu, wdo, wdx, resid, g_mlp)
+
+
+KINDS = ME, NEAR, FAR, FAL = range(4)
+
+
+def chip_slot(yy, xx, pp, ll):
+    return (yy * 2 + xx) * 4 + 2 * pp + ll
+
+
+class Reduction:
+    def __init__(self, where):
+        y, x, p, l, c = where
+        self.z = ((p, l), (p, 1 - l), (1 - p, l), (1 - p, 1 - l))
+        self.y, self.x = y, x
+
+    def y_first(self, kind):
+        return kind in (ME, FAR)
+
+    def first_peer(self, kind):
+        return "y" if self.y_first(kind) else "x"
+
+    def second_peer(self, kind):
+        return "x" if self.y_first(kind) else "y"
+
+    def place(self, kind, index, given):
+        if self.y_first(kind):
+            return (1 - self.y if given else self.y), index
+        return index, (1 - self.x if given else self.x)
+
+    def kept(self, kind):
+        return self.x if self.y_first(kind) else self.y
+
+
+def attend_back_kernel(
+    flags, q_in, k_in, v_in, o_in, db_in, wo_in, lse_in, qr_in, kr_in, cos_in, sin_in, gg, gu, gd, res, gq_ref, gk_ref,
+    d_out, goq, fw_out, fd_out, od_out, out, dg_ref,
+    q_ref, k_ref, v_ref, o_ref, dall, wo, lse_ref, qr_ref, kr_ref, cos_ref, sin_ref,
+    da, delta, dbuf, dq_acc, dk_acc, dv_acc, og, gdb, od, rb, rbd, rc, rcd, rz, rzd, go,
+    send_sem, recv_sem, load_sem, own_sem, out_sem, back_send, back_recv,
+):
+    where = place()
+    y, x, p, l, c = where
+    peer = peers_of(x, y, p, l, c)
+    red = Reduction(where)
+    net = Plan(send_sem, recv_sem)
+    wide_of, deep_of, second_of = {}, {}, {}
+    t = 2 * l + c
+
+    def block(index):
+        return dall.at[rows_at(index, OWN)]
+
+    go_db_l = net.add(peer["l"], [(db_in, block(t))])
+    go_db_c = net.add(peer["c"], [(db_in, block(t))])
+    go_db_r = net.add(peer["c"], in_place(block(2 * (1 - l) + c)))
+    go_gd_c = net.add(peer["c"], [(gd.at[:, rows_at(1 - c, 512)], gdb.at[c])])
+    go_fal = net.add(peer["l"], [(og.at[1, red.kept(FAL)], rz), (od.at[3, red.kept(FAL)], rzd)])
+    for n, kind in enumerate(KINDS):
+        wide, deep = [], []
+        for k in range(2):
+            yy, xx = red.place(kind, k, True)
+            slot = chip_slot(yy, xx, *red.z[kind])
+            if n >= 2:
+                wide.append((gg.at[rows_at(slot, 64)], rb.at[n - 2, k, 0]))
+                wide.append((gu.at[rows_at(slot, 64)], rb.at[n - 2, k, 1]))
+            deep.append((gdb.at[yy, rows_at(xx * 4 + 2 * red.z[kind][0] + red.z[kind][1], 192)], rbd.at[n, k]))
+        deep_of[kind] = net.add(peer[red.first_peer(kind)], deep)
+        if n >= 2:
+            wide_of[kind] = net.add(peer[red.first_peer(kind)], wide)
+            away = 1 - red.kept(kind)
+            second_of[kind] = net.add(peer[red.second_peer(kind)], [(og.at[n - 2, away], rc.at[n - 2]), (od.at[n, away], rcd.at[n - 2])])
+    home = Return(where, res, out, back_send, back_recv)
+
+    def columns(q):
+        return [(go.at[:, rows_at(q, 256)], goq.at[rows_at(t, 512)])]
+
+    go_go_l = net.add(peer["l"], columns(2 * (1 - l) + c))
+    go_go_d = net.add(peer["d"], columns(2 * (1 - l) + 1 - c))
+    go_go_c = net.add(peer["c"], columns(2 * l + 1 - c))
+    own_go = pltpu.make_async_copy(*columns(t)[0], out_sem.at[1])
+    loads = [
+        pltpu.make_async_copy(src, dst, load_sem.at[k])
+        for k, (src, dst) in enumerate(
+            [
+                (db_in, block(t)), (wo_in, wo), (o_in, o_ref), (q_in, q_ref), (k_in, k_ref), (v_in, v_ref), (lse_in, lse_ref),
+                (cos_in, cos_ref), (sin_in, sin_ref), (qr_in, qr_ref), (kr_in, kr_ref),
+                (gd.at[:, rows_at(c, 512)], gdb.at[c]),
+            ]
+        )
+    ]
+    own = []
+    for n, kind in enumerate(KINDS[2:]):
+        for k in range(2):
+            slot = chip_slot(*red.place(kind, k, False), *red.z[kind])
+            for m, ref in enumerate((gg, gu)):
+                own.append(pltpu.make_async_copy(ref.at[rows_at(slot, 64)], og.at[n, k, m], own_sem.at[len(own)]))
+
+    def wide_sum(kind):
+        n = KINDS.index(kind) - 2
+        for k in range(2):
+
+            def wide(r, carry):
+                rows = rows_at(r, 16)
+                for m in range(2):
+                    total = og[n, k, m, rows, :].astype(jnp.float32) + rb[n, k, m, rows, :].astype(jnp.float32)
+                    og[n, k, m, rows, :] = total.astype(jnp.bfloat16)
+                return carry
+
+            lax.fori_loop(0, 4, wide, 0)
+
+    def deep_sum(kind):
+        n = KINDS.index(kind)
+        for k in range(2):
+            yy, xx = red.place(kind, k, False)
+            at = (xx * 4 + 2 * red.z[kind][0] + red.z[kind][1]) * 192
+
+            def deep(r, carry):
+                rows = rows_at(r, 32)
+                mine = gdb[yy, pl.ds(pl.multiple_of(at + r * 32, 32), 32), :]
+                od[n, k, rows, :] = (mine.astype(jnp.float32) + rbd[n, k, rows, :].astype(jnp.float32)).astype(jnp.bfloat16)
+                return carry
+
+            lax.fori_loop(0, 6, deep, 0)
+
+    def more(kind, wide, deep):
+        n, u = KINDS.index(kind), red.kept(kind)
+        og[n - 2, u] = (og[n - 2, u].astype(jnp.float32) + wide.astype(jnp.float32)).astype(jnp.bfloat16)
+        od[n, u] = (od[n, u].astype(jnp.float32) + deep.astype(jnp.float32)).astype(jnp.bfloat16)
+
+    def branch(index):
+        rows = rows_at(index, OWN)
+        value = dot(dall[rows, :], wo[...], NT).astype(jnp.bfloat16)
+        da[rows, :] = value
+        for h in range(QH):
+            cols = slice(h * HEAD_DIM, (h + 1) * HEAD_DIM)
+            prod = value[:, cols].astype(jnp.float32) * o_ref[rows, cols].astype(jnp.float32)
+            delta[h, :, rows] = jnp.broadcast_to(jnp.sum(prod.T, axis=0, keepdims=True), (8, BLK))
+
+    def unrope(grad, u, gain, rows):
+        grad = grad * SCALE
+        e = grad * cos_ref[rows, :] + turn(grad * sin_ref[rows, :])
+        r = lax.rsqrt(jnp.mean(u * u, axis=-1, keepdims=True) + EPS)
+        ur = u * r
+        ge = e * gain
+        d = r * (ge - ur * jnp.mean(ur * ge, axis=-1, keepdims=True))
+        return d.astype(jnp.bfloat16), jnp.sum((e * ur).reshape(-1, 8, HEAD_DIM), axis=0)
+
+    step = pl.program_id(0)
+    b, g = step // KH, step % KH
+    i = 2 * ((l + b // 2) % 2) + b % 2
+
+    @pl.when(step == 0)
+    def _():
+        for copy in loads:
+            copy.start()
+        greet(line_peers(p, l, c) + [peer["x"], peer["y"]])
+        net.start(go_db_l, go_db_c, go_gd_c, wide_of[FAR], wide_of[FAL])
+        home.start()
+        for copy in own:
+            copy.start()
+        dk_acc[...] = jnp.zeros_like(dk_acc)
+        dv_acc[...] = jnp.zeros_like(dv_acc)
+        dg_ref[...] = jnp.zeros_like(dg_ref)
+        for copy in loads[:3]:
+            copy.wait()
+        branch(t)
+        loads[-1].wait()
+        net.arrived(go_gd_c)
+        net.start(deep_of[FAR], deep_of[FAL])
+        net.arrived(go_db_c)
+        branch(2 * l + 1 - c)
+        for copy in loads[3:-1]:
+            copy.wait()
+
+    @pl.when(step == 2 * KH)
+    def _():
+        net.arrived(go_db_l)
+        net.start(go_db_r)
+        branch(2 * (1 - l) + c)
+        for copy in own:
+            copy.wait()
+        for kind in (FAR, FAL):
+            net.arrived(wide_of[kind], deep_of[kind])
+            wide_sum(kind)
+            deep_sum(kind)
+            net.start(second_of[kind])
+        net.arrived(go_db_r)
+        branch(2 * (1 - l) + 1 - c)
+
+    @pl.when(step == 3 * KH)
+    def _():
+        net.arrived(second_of[FAL])
+        more(FAL, rc[1], rcd[1])
+        net.start(go_fal)
+        net.arrived(second_of[FAR])
+        more(FAR, rc[0], rcd[0])
+        net.start(deep_of[ME], deep_of[NEAR])
+
+        def grad_out(k, carry):
+            cols = rows_at(k, 256)
+            go[cols, :] = dot(o_ref[:, cols], dall[...], TN).astype(jnp.bfloat16)
+            return carry
+
+        lax.fori_loop(0, 2, grad_out, 0)
+        net.start(go_go_l, go_go_d, go_go_c)
+        own_go.start()
+
+    dq_acc[...] = jnp.zeros_like(dq_acc)
+    rows = rows_at(i, BLK)
+    heads = [2 * g + n for n in range(2)]
+    spans = [rows_at(h, HEAD_DIM) for h in heads]
+    queries = [q_ref[h, rows, :] for h in heads]
+    grads = [da[rows, span] for span in spans]
+
+    def tile(j, mask=None):
+        keys = rows_at(j, BLK)
+        k, v = k_ref[g, keys, :], v_ref[g, keys, :]
+        dv, dk = None, None
+        for n, h in enumerate(heads):
+            probs = jnp.exp2(dot(k, queries[n], NT) * (SCALE * LOG2E) - lse_ref[h, 0:1, rows])
+            if mask is not None:
+                probs = jnp.where(mask, probs, 0.0)
+            d_scores = (probs * (dot(v, grads[n], NT) - delta[h, 0:1, rows])).astype(jnp.bfloat16)
+            dv_more, dk_more = dot(probs.astype(jnp.bfloat16), grads[n]), dot(d_scores, queries[n])
+            dv, dk = (dv_more, dk_more) if dv is None else (dv + dv_more, dk + dk_more)
+            dq_acc[n] += dot(d_scores, k, TN)
+        dv_acc[g, keys, :] += dv
+        dk_acc[g, keys, :] += dk
+
+    def loop(j, carry):
+        tile(j)
+        return carry
+
+    tile(i, block_mask(0, flags, i))
+    lax.fori_loop(0, i, loop, 0)
+    for n, h in enumerate(heads):
+        low, total = unrope(dq_acc[n], qr_ref[h, rows, :], gq_ref[...], rows)
+        dbuf[rows, spans[n]] = low
+        dg_ref[0] += total
+
+    @pl.when(step == 4 * KH - 1)
+    def _():
+        for gg_at in range(KH):
+
+            def finish(r, carry):
+                rows = rows_at(r, 256)
+                low, total = unrope(dk_acc[gg_at, rows, :], kr_ref[gg_at, rows, :], gk_ref[...], rows)
+                dbuf[rows, pl.ds((QH + gg_at) * HEAD_DIM, HEAD_DIM)] = low
+                dbuf[rows, pl.ds((QH + KH + gg_at) * HEAD_DIM, HEAD_DIM)] = dv_acc[gg_at, rows, :].astype(jnp.bfloat16)
+                dg_ref[1] += total
+                return carry
+
+            lax.fori_loop(0, 8, finish, 0)
+        outs = [pltpu.make_async_copy(dbuf, d_out, out_sem.at[0])]
+        outs[0].start()
+        for kind in (ME, NEAR):
+            net.arrived(deep_of[kind])
+            deep_sum(kind)
+        net.arrived(go_fal)
+        more(FAR, rz[...], rzd[...])
+        u = red.kept(FAR)
+        outs += [
+            pltpu.make_async_copy(og.at[0, u], fw_out, out_sem.at[2]),
+            pltpu.make_async_copy(od.at[2, u], fd_out, out_sem.at[3]),
+            pltpu.make_async_copy(od.at[pl.ds(0, 2)], od_out, out_sem.at[4]),
+        ]
+        for copy in outs[1:]:
+            copy.start()
+        net.arrived(go_go_l, go_go_d, go_go_c)
+        own_go.wait()
+        net.sent()
+        home.wait()
+        for copy in outs:
+            copy.wait()
+
+
+def attend_back(flags, q, k, v, o, db, wo, lse, qr, kr, cosine, sine, gg, gu, gd, res, gq, gk):
+    bf16, f32 = jnp.bfloat16, jnp.float32
+    any_spec = pl.BlockSpec(memory_space=pl.ANY)
+    gain = pl.BlockSpec((1, HEAD_DIM), lambda s, f: (0, 0))
+    copies = 40
+
+    def vm(a):
+        return pltpu.VMEM(a.shape, a.dtype)
+
+    return pl.pallas_call(
+        attend_back_kernel,
+        out_shape=(
+            jax.ShapeDtypeStruct((SEQ_ROWS, 1024), bf16),
+            jax.ShapeDtypeStruct((2048, 256), bf16),
+            jax.ShapeDtypeStruct((2, 64, HALF_FF), bf16),
+            jax.ShapeDtypeStruct((192, 512), bf16),
+            jax.ShapeDtypeStruct((2, 2, 192, 512), bf16),
+            jax.ShapeDtypeStruct((2, ROWS, MODEL_DIM), bf16),
+            jax.ShapeDtypeStruct((2, 8, HEAD_DIM), f32),
+        ),
+        grid_spec=pltpu.PrefetchScalarGridSpec(
+            num_scalar_prefetch=1,
+            grid=(4 * KH,),
+            in_specs=[any_spec] * 15 + [gain] * 2,
+            out_specs=[any_spec] * 6 + [pl.BlockSpec((2, 8, HEAD_DIM), lambda s, f: (0, 0, 0))],
+            scratch_shapes=[vm(q), vm(k), vm(v), vm(o), pltpu.VMEM((SEQ_ROWS, MODEL_DIM), bf16), vm(wo), vm(lse), vm(qr), vm(kr)]
+            + [vm(cosine), vm(sine)]
+            + [
+                pltpu.VMEM((SEQ_ROWS, QH * HEAD_DIM), bf16),
+                pltpu.VMEM((QH, 8, SEQ_ROWS), f32),
+                pltpu.VMEM((SEQ_ROWS, 1024), bf16),
+                pltpu.VMEM((2, BLK, HEAD_DIM), f32),
+                pltpu.VMEM((KH, SEQ_ROWS, HEAD_DIM), f32),
+                pltpu.VMEM((KH, SEQ_ROWS, HEAD_DIM), f32),
+                pltpu.VMEM((2, 2, 2, 64, HALF_FF), bf16),
+                pltpu.VMEM((2, HALF_FF, 512), bf16),
+                pltpu.VMEM((4, 2, 192, 512), bf16),
+                pltpu.VMEM((2, 2, 2, 64, HALF_FF), bf16),
+                pltpu.VMEM((4, 2, 192, 512), bf16),
+                pltpu.VMEM((2, 2, 64, HALF_FF), bf16),
+                pltpu.VMEM((2, 192, 512), bf16),
+                pltpu.VMEM((2, 64, HALF_FF), bf16),
+                pltpu.VMEM((192, 512), bf16),
+                pltpu.VMEM((512, MODEL_DIM), bf16),
+                pltpu.SemaphoreType.DMA((copies,)),
+                pltpu.SemaphoreType.DMA((copies,)),
+                pltpu.SemaphoreType.DMA((12,)),
+                pltpu.SemaphoreType.DMA((8,)),
+                pltpu.SemaphoreType.DMA((5,)),
+                pltpu.SemaphoreType.DMA((2,)),
+                pltpu.SemaphoreType.DMA((2,)),
+            ],
+        ),
+        compiler_params=pltpu.CompilerParams(
+            collective_id=4, has_side_effects=True, vmem_limit_bytes=58 * 1024 * 1024
+        ),
+        cost_estimate=pl.CostEstimate(
+            flops=10 * QH * SEQ_ROWS * SEQ_ROWS * HEAD_DIM, bytes_accessed=40 << 20, transcendentals=QH * SEQ_ROWS * SEQ_ROWS
+        ),
+        name="attend_back",
+    )(flags, q, k, v, o, db, wo, lse, qr, kr, cosine, sine, gg, gu, gd, res, gq, gk)
+
+
+def normed_kernel(
+    d_in, w_in, n_in, xs, gg, gu, fw_in, fd_in, od_in, dr_ref, ga_ref,
+    gt, dg, pq, me_w, me_d, near_w, near_d,
+    d_ref, w_ref, n_ref, x_ref, send_c, recv_c, send_l, recv_l, keep, og, rb, od, rx, rxd, rz, rzd,
+    send_sem, recv_sem, load_sem, own_sem,
+):
+    where = place()
+    y, x, p, l, c = where
+    peer = peers_of(x, y, p, l, c)
+    red = Reduction(where)
+    net = Plan(send_sem, recv_sem)
+    wide_of, deep_of, second_of = {}, {}, {}
+    t = 2 * l + c
+    two = KINDS[:2]
+    own = []
+    for n, kind in enumerate(two):
+        wide = []
+        for k in range(2):
+            away = chip_slot(*red.place(kind, k, True), *red.z[kind])
+            here = chip_slot(*red.place(kind, k, False), *red.z[kind])
+            for m, ref in enumerate((gg, gu)):
+                wide.append((ref.at[rows_at(away, 64)], rb.at[n, k, m]))
+                own.append(pltpu.make_async_copy(ref.at[rows_at(here, 64)], og.at[n, k, m], own_sem.at[len(own)]))
+        wide_of[kind] = net.add(peer[red.first_peer(kind)], wide)
+        away = 1 - red.kept(kind)
+        second_of[kind] = net.add(peer[red.second_peer(kind)], [(og.at[n, away], rx.at[n]), (od_in.at[n, away], rxd.at[n])])
+    go_far = net.add(peer["p"], [(fw_in, rz), (fd_in, rzd)])
+    go_give_0 = net.add(peer["c"], [(send_c.at[0], recv_c.at[0])])
+    go_give_1 = net.add(peer["c"], [(send_c.at[1], recv_c.at[1])])
+    go_cross = net.add(peer["l"], [(send_l, recv_l)])
+
+    loads = [
+        pltpu.make_async_copy(src, dst, load_sem.at[k])
+        for k, (src, dst) in enumerate([(d_in, d_ref), (w_in, w_ref), (n_in, n_ref), (od_in, od), (xs.at[rows_at(t, OWN)], x_ref)])
+    ]
+    for copy in loads:
+        copy.start()
+    for copy in own:
+        copy.start()
+    greet(list(peer.values()))
+    net.start(wide_of[ME], wide_of[NEAR], go_far)
+
+    def project(ll, cc, write):
+        part = d_ref[rows_at(2 * ll + cc, OWN), :]
+
+        def chunk(k, carry):
+            cols = rows_at(k, 256)
+            write(cols, dot(part, w_ref[cols, :], NT))
+            return carry
+
+        lax.fori_loop(0, 4, chunk, 0)
+
+    def give(k):
+        def write(cols, value):
+            send_c[k, :, cols] = value.astype(jnp.bfloat16)
+
+        return write
+
+    def hold(k):
+        def write(cols, value):
+            keep[k, :, cols] = value
+
+        return write
+
+    loads[0].wait()
+    loads[1].wait()
+    project(1 - l, 1 - c, give(0))
+    net.start(go_give_0)
+    project(1 - l, c, hold(0))
+    net.arrived(go_give_0)
+    send_l[...] = (keep[0] + recv_c[0].astype(jnp.float32)).astype(jnp.bfloat16)
+    net.start(go_cross)
+    project(l, 1 - c, give(1))
+    net.start(go_give_1)
+    project(l, c, hold(1))
+    for copy in own:
+        copy.wait()
+    for copy in loads[2:]:
+        copy.wait()
+    for n, kind in enumerate(two):
+        net.arrived(wide_of[kind])
+        for k in range(2):
+
+            def wide(r, carry):
+                rows = rows_at(r, 16)
+                for m in range(2):
+                    total = og[n, k, m, rows, :].astype(jnp.float32) + rb[n, k, m, rows, :].astype(jnp.float32)
+                    og[n, k, m, rows, :] = total.astype(jnp.bfloat16)
+                return carry
+
+            lax.fori_loop(0, 4, wide, 0)
+        net.start(second_of[kind])
+
+    def grad_qkv(k, carry):
+        cols = rows_at(k, 256)
+        pq[cols, :] = dot(n_ref[:, cols], d_ref[...], TN).astype(jnp.bfloat16)
+        return carry
+
+    lax.fori_loop(0, 4, grad_qkv, 0)
+    net.arrived(go_give_1, go_cross)
+
+    dg[...] = jnp.zeros_like(dg)
+
+    def rows_back(k, carry):
+        rows = rows_at(k, 64)
+        value = x_ref[rows, :].astype(jnp.float32)
+        grad = keep[1, rows, :] + recv_c[1, rows, :].astype(jnp.float32) + recv_l[rows, :].astype(jnp.float32)
+        r = lax.rsqrt(jnp.mean(value * value, axis=-1, keepdims=True) + EPS)
+        scaled = value * r
+        gained = grad * ga_ref[...]
+        back = r * (gained - scaled * jnp.mean(scaled * gained, axis=-1, keepdims=True))
+        gt[rows, :] = (dr_ref[rows, :] + back).astype(jnp.bfloat16)
+        dg[...] += jnp.sum((grad * scaled).reshape(-1, 8, MODEL_DIM), axis=0)
+        return carry
+
+    lax.fori_loop(0, 8, rows_back, 0)
+    net.arrived(second_of[NEAR])
+    u = red.kept(NEAR)
+    near_w[...] = (og[1, u].astype(jnp.float32) + rx[1].astype(jnp.float32)).astype(jnp.bfloat16)
+    near_d[...] = (od[1, u].astype(jnp.float32) + rxd[1].astype(jnp.float32)).astype(jnp.bfloat16)
+    net.arrived(second_of[ME], go_far)
+    u = red.kept(ME)
+    me_w[...] = og[0, u].astype(jnp.float32) + rx[0].astype(jnp.float32) + rz[...].astype(jnp.float32)
+    me_d[...] = od[0, u].astype(jnp.float32) + rxd[0].astype(jnp.float32) + rzd[...].astype(jnp.float32)
+    net.sent()
+
+
+def normed_back(d, w, normed, xs, gg, gu, fw, fd, od, d_resid, g_attn):
+    bf16, f32 = jnp.bfloat16, jnp.float32
+    any_spec = pl.BlockSpec(memory_space=pl.ANY)
+    vmem = pl.BlockSpec(memory_space=pltpu.VMEM)
+    copies = 24
+    wide, deep = (2, 64, HALF_FF), (192, 512)
+
+    def vm(a):
+        return pltpu.VMEM(a.shape, a.dtype)
+
+    return pl.pallas_call(
+        normed_kernel,
+        out_shape=(
+            jax.ShapeDtypeStruct((OWN, MODEL_DIM), bf16),
+            jax.ShapeDtypeStruct((8, MODEL_DIM), f32),
+            jax.ShapeDtypeStruct((1024, 1024), bf16),
+            jax.ShapeDtypeStruct(wide, f32),
+            jax.ShapeDtypeStruct(deep, f32),
+            jax.ShapeDtypeStruct(wide, bf16),
+            jax.ShapeDtypeStruct(deep, bf16),
+        ),
+        in_specs=[any_spec] * 9 + [vmem] * 2,
+        out_specs=[vmem] * 7,
+        scratch_shapes=[
+            vm(d), vm(w), vm(normed),
+            pltpu.VMEM((OWN, MODEL_DIM), bf16),
+            pltpu.VMEM((2, OWN, MODEL_DIM), bf16),
+            pltpu.VMEM((2, OWN, MODEL_DIM), bf16),
+            pltpu.VMEM((OWN, MODEL_DIM), bf16),
+            pltpu.VMEM((OWN, MODEL_DIM), bf16),
+            pltpu.VMEM((2, OWN, MODEL_DIM), f32),
+            pltpu.VMEM((2, 2) + wide, bf16),
+            pltpu.VMEM((2, 2) + wide, bf16),
+            pltpu.VMEM((2, 2) + deep, bf16),
+            pltpu.VMEM((2,) + wide, bf16),
+            pltpu.VMEM((2,) + deep, bf16),
+            pltpu.VMEM(wide, bf16),
+            pltpu.VMEM(deep, bf16),
+            pltpu.SemaphoreType.DMA((copies,)),
+            pltpu.SemaphoreType.DMA((copies,)),
+            pltpu.SemaphoreType.DMA((6,)),
+            pltpu.SemaphoreType.DMA((8,)),
+        ],
+        compiler_params=pltpu.CompilerParams(
+            collective_id=5, has_side_effects=True, vmem_limit_bytes=58 * 1024 * 1024
+        ),
+        name="normed_back",
+    )(d, w, normed, xs, gg, gu, fw, fd, od, d_resid, g_attn)
+
+
+def back_kernel(
+    pq, go, gp, near_w, near_d, me_w, me_d, gt,
+    out_query, out_key, out_value, out_out, out_gate, out_up, out_down, gout, tokens,
+    work, wgo, wgp, ry, ryo, ryg, ox, oxo, oxg, rs, rso, rsg, rq, rqo, rqg,
+    zw, zd, total_w, total_d, fw, fd, landed,
+    send_sem, recv_sem, back_send, back_recv,
+):
+    where = place()
+    y, x, p, l, c = where
+    peer = peers_of(x, y, p, l, c)
+    net = Plan(send_sem, recv_sem)
+    me = 2 * l + c
+    home = Return(where, gt, landed, back_send, back_recv)
+
+    def group(yy, xx, pp):
+        return (yy * 2 + xx) * 2 + pp
+
+    def moved(sources, groups, targets, at=0):
+        return [
+            (src.at[one], dst.at[at + k])
+            for k, one in enumerate(groups)
+            for src, dst in zip(sources, targets)
+        ]
+
+    source, working, small = (pq, go, gp), (work, wgo, wgp), (rs, rso, rsg)
+    go_own_y = net.add(peer["y"], moved(source, (group(1 - y, 0, p), group(1 - y, 1, p)), (ry, ryo, ryg)))
+    go_other_x = net.add(peer["x"], moved(source, (group(0, 1 - x, 1 - p), group(1, 1 - x, 1 - p)), (ox, oxo, oxg)))
+    go_own_x = net.add(peer["x"], moved(working, (group(y, 1 - x, p),), small, 0))
+    go_other_y = net.add(peer["y"], moved(working, (group(1 - y, x, 1 - p),), small, 1))
+    go_across = net.add(peer["p"], moved(working, (group(y, x, 1 - p),), small, 2))
+    base = group(y, x, p)
+
+    def parts(q):
+        return [
+            (work.at[base, rows_at(q, 32)], rq.at[me]),
+            (wgo.at[base, rows_at(q, 64)], rqo.at[me]),
+            (wgp.at[base, q], rqg.at[me]),
+        ]
+
+    go_last_l = net.add(peer["l"], parts(2 * (1 - l) + c))
+    go_last_d = net.add(peer["d"], parts(2 * (1 - l) + 1 - c))
+    go_last_c = net.add(peer["c"], parts(2 * l + 1 - c))
+    go_near = net.add(peer["l"], [(near_w, zw), (near_d, zd)])
+    go_halves = net.add(peer["c"], [(total_w.at[1 - c], fw.at[c]), (total_d.at[1 - c], fd.at[c])])
+    greet(line_peers(p, l, c) + [peer["x"], peer["y"]])
+    net.start(go_own_y, go_other_x, go_near)
+    home.start()
+
+    def add(at, left, right, place_at):
+        for target, a, b in zip(working, left, right):
+            total = a[at].astype(jnp.float32) + b[place_at].astype(jnp.float32)
+            target[at] = total.astype(target.dtype)
+
+    net.arrived(go_own_y)
+    for xx in (0, 1):
+        add(group(y, xx, p), source, (ry, ryo, ryg), xx)
+    net.start(go_own_x)
+    net.arrived(go_other_x)
+    for yy in (0, 1):
+        add(group(yy, x, 1 - p), source, (ox, oxo, oxg), yy)
+    net.start(go_other_y)
+    net.arrived(go_near)
+    for cc in range(2):
+        rows = pl.ds(32 * cc, 32)
+        total_w[cc] = me_w[:, rows, :] + zw[:, rows, :].astype(jnp.float32)
+        rows = pl.ds(96 * cc, 96)
+        total_d[cc] = me_d[rows, :] + zd[rows, :].astype(jnp.float32)
+    net.start(go_halves)
+    net.arrived(go_other_y)
+    add(group(y, x, 1 - p), working, small, 1)
+    net.start(go_across)
+    net.arrived(go_own_x)
+    add(base, working, small, 0)
+    fw[c] = total_w[c]
+    fd[c] = total_d[c]
+    net.arrived(go_halves)
+    for half in range(2):
+        cols = slice(half * HALF_FF, (half + 1) * HALF_FF)
+        out_gate[:, cols] = fw[half, 0]
+        out_up[:, cols] = fw[half, 1]
+        out_down[:, half * 512 : (half + 1) * 512] = fd[half]
+    net.arrived(go_across)
+    add(base, working, small, 2)
+    net.start(go_last_l, go_last_d, go_last_c)
+    rq[me] = work[base, rows_at(me, 32), :]
+    rqo[me] = wgo[base, rows_at(me, 64), :]
+    rqg[me] = wgp[base, me]
+    home.wait()
+    tokens[...] = landed[...].astype(jnp.float32)
+    net.arrived(go_last_l, go_last_d, go_last_c)
+    for q in range(4):
+        value = rq[q].astype(jnp.float32)
+        out_query[:, 512 * q : 512 * (q + 1)] = value[:, :512]
+        out_key[:, 256 * q : 256 * (q + 1)] = value[:, 512:768]
+        out_value[:, 256 * q : 256 * (q + 1)] = value[:, 768:]
+        out_out[:, 256 * q : 256 * (q + 1)] = rqo[q].astype(jnp.float32)
+    gout[...] = rqg[0] + rqg[1] + rqg[2] + rqg[3]
+    net.sent()
+
+
+def back(pq, goq, gp, near_w, near_d, me_w, me_d, gt):
+    bf16, f32 = jnp.bfloat16, jnp.float32
+    vmem = pl.BlockSpec(memory_space=pltpu.VMEM)
+    copies = 40
+
+    def three(*lead):
+        return [
+            pltpu.VMEM(lead + (128, 1024), bf16),
+            pltpu.VMEM(lead + (256, 256), bf16),
+            pltpu.VMEM(lead + (4, 8, 128), f32),
+        ]
+
+    wide, deep = (2, 64, HALF_FF), (192, 512)
+    return pl.pallas_call(
+        back_kernel,
+        out_shape=(
+            jax.ShapeDtypeStruct((32, 2048), f32),
+            jax.ShapeDtypeStruct((32, 1024), f32),
+            jax.ShapeDtypeStruct((32, 1024), f32),
+            jax.ShapeDtypeStruct((64, 1024), f32),
+            jax.ShapeDtypeStruct((32, FF), f32),
+            jax.ShapeDtypeStruct((32, FF), f32),
+            jax.ShapeDtypeStruct((96, 1024), f32),
+            jax.ShapeDtypeStruct((8, 128), f32),
+            jax.ShapeDtypeStruct((2, ROWS, MODEL_DIM), f32),
+        ),
+        in_specs=[vmem] * 8,
+        out_specs=[vmem] * 9,
+        scratch_shapes=three(8) + three(2) + three(2) + three(3)
+        + [
+            pltpu.VMEM((4, 32, 1024), bf16),
+            pltpu.VMEM((4, 64, 256), bf16),
+            pltpu.VMEM((4, 8, 128), f32),
+            pltpu.VMEM(wide, bf16),
+            pltpu.VMEM(deep, bf16),
+            pltpu.VMEM((2, 2, 32, HALF_FF), f32),
+            pltpu.VMEM((2, 96, 512), f32),
+            pltpu.VMEM((2, 2, 32, HALF_FF), f32),
+            pltpu.VMEM((2, 96, 512), f32),
+            pltpu.VMEM((2, ROWS, MODEL_DIM), bf16),
+            pltpu.SemaphoreType.DMA((copies,)),
+            pltpu.SemaphoreType.DMA((copies,)),
+            pltpu.SemaphoreType.DMA((2,)),
+            pltpu.SemaphoreType.DMA((2,)),
+        ],
+        compiler_params=pltpu.CompilerParams(
+            collective_id=1, has_side_effects=True, vmem_limit_bytes=58 * 1024 * 1024
+        ),
+        name="back_reduce",
+    )(pq.reshape(8, 128, 1024), goq.reshape(8, 256, 256), gp.reshape(8, 4, 8, 128), near_w, near_d, me_w, me_d, gt)
+
+
+def pick(value, index):
+    return lax.dynamic_index_in_dim(value, index, 0, keepdims=False)
+
+
+def fast_device(tokens, cotangent, starts, w_query, key_matrix, value_matrix, w_out, w_gate, w_up, w_down, gains):
+    p = lax.axis_index("p")
+    gn = jnp.pad(gains.astype(jnp.float32), (0, 952)).reshape(8, 128)
+    half_steps = jnp.arange(HEAD_DIM // 2, dtype=jnp.float32)
+    inverse = THETA ** (-2.0 * half_steps / HEAD_DIM)
+    inverse = jnp.broadcast_to(jnp.concatenate([inverse, inverse])[None], (8, HEAD_DIM))
+    own_starts = pick(starts, p)
+    block_at = jnp.arange(SEQ_ROWS // PIECE, dtype=jnp.int32) * PIECE
+    flags = jnp.any(own_starts[None, :] == block_at[:, None], axis=1).astype(jnp.int32)
+    xs, w_qkv, woq, gf, wgu, wdn, cosine, sine = front(
+        tokens, w_query, key_matrix, value_matrix, w_out, gn, w_gate, w_up, w_down, inverse
+    )
+    xs = xs.reshape(SEQ_ROWS, MODEL_DIM)
+    gain_all = gf.reshape(32, 1024)[:, :72].reshape(2304)
+    g_attn = gain_all[None, :1024]
+    g_mlp = gain_all[None, 1024:2048]
+    g_q = gain_all[None, 2048:2176]
+    g_k = gain_all[None, 2176:]
+    normed, q, k, v, q_raw, k_raw, attn, lse, wo, wgu, wdn = attend(
+        flags, xs, w_qkv, g_attn, g_q, g_k, cosine, sine, woq, wgu, wdn
+    )
+    resid, mlp_in, wgu, wdn, wdx, wdo, dy = finish_resid(attn, wo, g_mlp, xs, cotangent, wgu, wdn)
+    grad_gate, grad_up, grad_down, d_resid, d_branch, result, d_g_mlp = feed_forward(
+        mlp_in.reshape(1024, MODEL_DIM), dy.reshape(1024, MODEL_DIM), wgu, wdo, wdx, resid, g_mlp
+    )
+    d_qkv, goq, fw, fd, od, output, d_g_heads = attend_back(
+        flags, q, k, v, attn, d_branch, wo, lse, q_raw, k_raw, cosine, sine, grad_gate, grad_up, grad_down, result, g_q, g_k
+    )
+    gt, d_g_attn, pq, me_w, me_d, near_w, near_d = normed_back(
+        d_qkv, w_qkv, normed, xs, grad_gate, grad_up, fw, fd, od, d_resid, g_attn
+    )
+    d_gains = jnp.concatenate([jnp.sum(d_g_attn, axis=0), jnp.sum(d_g_mlp, axis=0), jnp.sum(d_g_heads, axis=1).reshape(256)])
+    gp = jnp.pad(d_gains.reshape(32, 72), ((0, 0), (0, 952))).reshape(32, 8, 128)
+    *grads, gains_sum, grad_tokens = back(pq, goq, gp, near_w, near_d, me_w, me_d, gt)
+    return (output, grad_tokens, *grads, gains_sum.reshape(1024)[:72])
+
+
+def fast_solution(mesh):
+    wide = Mesh(mesh.devices.reshape(2, 2, 2, 2, 2), AXES)
+    rows = ("y", "x")
+    places = ("p", "l", "c")
+    weight = P(AXES, None)
+    return jax.shard_map(
+        fast_device,
+        mesh=wide,
+        in_specs=(P(rows, places, None), P(rows, places, None), P(rows, None)) + (weight,) * 7 + (P(AXES),),
+        out_specs=(P(rows, places, None), P(rows, places, None)) + (weight,) * 7 + (P(AXES),),
+        check_vma=False,
+    )
+
+
+def solution(mesh):
+    if dict(mesh.shape) == {"dp": 4, "ctx": 8}:
+        return fast_solution(mesh)
+    return generic_solution(mesh)

time: 2000 us -> 460 us (0.23)
  waiting for transfers between devices: 1440 us -> 0 us
  Pallas kernels: 0 us -> 439 us
  matrix products: 282 us -> 0 us
  local copies, waits for them, and re-layouts: 119 us -> 17.5 us
  blocking collectives: 80.7 us -> 0 us
  other arithmetic: 54.6 us -> 2.24 us
    reduce_scatter x11 -> x0, waiting for transfers between devices: 1010 us -> none  [the longest x1 162 us: per_device(): lax.psum_scatter(grad_gate, ('dp', 'ctx'), scatter_dimension=0, tiled=True)]
    pallas_call x0 -> x7, Pallas kernels: none -> 439 us  [the longest x1 97.4 us: front(): pl.pallas_call(front_kernel, out_shape=(jax.ShapeDtypeStruct((8, ROWS, MO...]
    all_gather x11 -> x0, waiting for transfers between devices: 418 us -> none  [the longest x1 62.9 us: per_device(): lax.all_gather(w_down, ('dp', 'ctx'), axis=0, tiled=True)]
    dot_general x117 -> x0, matrix products: 282 us -> none  [the longest x16 46.8 us: attend_forward(): jnp.einsum('tagd,kad->agtk', q_part, k_part, preferred_element_type=jnp.f...]
    unnamed x2 -> x0, blocking collectives: 80.7 us -> none
    unnamed x410 -> x66, local copies, waits for them, and re-layouts: 68.8 us -> 15.3 us
    another operation x18 -> x0, other arithmetic: 20.3 us -> none
  transfers between devices with their start and end apart: 22 -> 0, of which waited for: 19 -> 0; matrix products, arithmetic and copies ran while one was open for 17% -> 0% of each run, Pallas kernels for 0% -> 0%
where the time goes in v2:
time: 460 us; the launch traced here: 459 us
  Pallas kernels  439 us (95%)
  local copies, waits for them, and re-layouts  17.5 us (4%)
    pallas_call x1, Pallas kernels, front(): pl.pallas_call(front_kernel, out_shape=(jax.ShapeDtypeStruct((8, ROWS, MO...  97.4 us
    pallas_call x1, Pallas kernels, attend_back(): pl.pallas_call(attend_back_kernel, out_shape=(jax.ShapeDtypeStruct((SEQ_R...  82.2 us
    pallas_call x1, Pallas kernels, back(): pl.pallas_call(back_kernel, out_shape=(jax.ShapeDtypeStruct((32, 2048), f...  61.1 us
    pallas_call x1, Pallas kernels, finish_resid(): pl.pallas_call(resid_kernel, out_shape=(jax.ShapeDtypeStruct((OWN, MODEL_...  53.2 us
    pallas_call x1, Pallas kernels, normed_back(): pl.pallas_call(normed_kernel, out_shape=(jax.ShapeDtypeStruct((OWN, MODEL...  49.8 us
    pallas_call x1, Pallas kernels, feed_forward(): pl.pallas_call(forward_kernel, grid=(HALF_FF // CHUNK,), out_shape=(jax.S...  47.7 us
    pallas_call x1, Pallas kernels, attend(): pl.pallas_call(attend_kernel, out_shape=(jax.ShapeDtypeStruct((SEQ_ROWS,...  47.4 us
    unnamed x66, local copies, waits for them, and re-layouts  15.3 us

profile of v2, /device:TPU:0, one launch (start us, length us, event | category | flops | bytes accessed | tf_op | source)
XLA Modules:
  0.0 459.5 jit_solution(7381943956066141865)
XLA Ops:
  0.6 0.0 copy-start
  0.7 0.7 copy-done
  1.3 0.1 compare_reduce_fusion
  1.5 0.1 pad_maximum_fusion.1
  1.5 0.6 broadcast_in_dim.20.inverse
  2.1 1.2 bitcast_convert_fusion.gn
  3.4 97.4 %front_gather.1 = (bf16[8,256,1024]{2,1,0:T(8,128)(2,1)}, bf16[1024,1024]{1,0:T(8,128)(2,1)}, bf16[2048,256]{1,0:T(8,128)(2,1)}, f32[32,8,128]{2,1,0:T(8,128)}, ...) custom-call(bf16[2,256,1024]{2,1,0:T(8,128)(2,1)} %tok.1, ...), custom_call_target="tpu_custom_call" | custom-call | tf_op jit(solution)/shard_map/front_gather/pallas_call | solution.py:605
  100.8 0.9 copy.28
  101.7 0.1 reshape.64
  101.8 0.0 copy-start.8
  101.8 0.0 copy-start.9
  101.8 0.0 copy-start.7
  101.8 0.0 copy-start.6
  101.9 0.0 copy-start.10
  101.9 1.2 copy-done.10
  103.1 1.2 copy-done.11
  104.3 47.4 %attend.1 = (bf16[2048,1024]{1,0:T(8,128)(2,1)}, bf16[4,2048,128]{2,1,0:T(8,128)(2,1)}, bf16[2,2048,128]{2,1,0:T(8,128)(2,1)S(1)}, bf16[2,2048,128]{2,1,0:T(8,12...) custom-call(s32[8]{0:T(128)S(1)} %convert_element_type.8.flags, ...), custom_call_target="tpu_custom_call", output_to_operand_aliasing={{9}: (9, {}), {10}: (10, {})} | custom-call | flops 8589934592 | bytes 25165824 | tf_op jit(solution)/shard_map/attend/pallas_call | solution.py:897
  151.7 0.0 copy-done.12
  151.7 0.0 copy-done.8
  151.7 0.0 copy-done.9
  151.7 0.0 copy-done.7
  151.8 0.0 copy-start.13
  151.8 1.0 copy-done.13
  152.7 0.0 copy-done.6
  152.7 0.0 copy-done.4
  152.8 53.2 %residual.1 = (f32[512,1024]{1,0:T(8,128)}, bf16[2,512,1024]{2,1,0:T(8,128)(2,1)}, bf16[2,1024,1536]{2,1,0:T(8,128)(2,1)}, bf16[3072,512]{1,0:T(8,128)(2,1)}, bf...) custom-call(bf16[2048,512]{1,0:T(8,128)(2,1)} %get-tuple-element.76., ...), custom_call_target="tpu_custom_call", output_to_operand_aliasing={{2}: (5, {}), {3}: (6, {})} | custom-call | tf_op jit(solution)/shard_map/residual/pallas_call | solution.py:1044
  206.0 0.0 copy-done.5
  206.0 0.0 copy-done.14
  206.0 0.0 copy-done.15
  206.0 0.0 copy-start.2
  206.0 1.2 copy-done.2
  207.2 1.1 copy-done.3
  208.3 47.7 %feed_forward.1 = (bf16[1024,1536]{1,0:T(8,128)(2,1)}, bf16[1024,1536]{1,0:T(8,128)(2,1)}, bf16[1536,1024]{1,0:T(8,128)(2,1)}, f32[512,1024]{1,0:T(8,128)}, bf16...) custom-call(bf16[1024,1024]{1,0:T(8,128)(2,1)} %bitcast.34, bf16[1024,1024]{1,0:T(8,128)(2,1)} %bitcast.35, ...), custom_call_target="tpu_custom_call" | custom-call | tf_op jit(solution)/shard_map/feed_forward/pallas_call | solution.py:1178
  256.1 82.2 %attend_back.1 = (bf16[2048,1024]{1,0:T(8,128)(2,1)}, bf16[2048,256]{1,0:T(8,128)(2,1)}, bf16[2,64,1536]{2,1,0:T(8,128)(2,1)}, bf16[192,512]{1,0:T(8,128)(2,1)},...) custom-call(s32[8]{0:T(128)} %copy-done.12, ...), custom_call_target="tpu_custom_call" | custom-call | flops 21474836480 | bytes 41943040 | tf_op jit(solution)/shard_map/attend_back/pallas_call | solution.py:1496
  338.2 0.0 copy-start.26
  338.3 0.0 copy-start.25
  338.3 49.8 %normed_back.1 = (bf16[512,1024]{1,0:T(8,128)(2,1)}, f32[8,1024]{1,0:T(8,128)}, bf16[1024,1024]{1,0:T(8,128)(2,1)}, f32[2,64,1536]{2,1,0:T(8,128)}, f32[192,512]...) custom-call(bf16[2048,1024]{1,0:T(8,128)(2,1)} %get-tuple-element.95.d_in, ...), custom_call_target="tpu_custom_call" | custom-call | tf_op jit(solution)/shard_map/normed_back/pallas_call | solution.py:1687
  388.0 0.0 copy-done.26
  388.1 0.8 reduce_sum.27
  388.8 0.0 copy-done.25
  388.9 0.1 reshape.70
  389.0 0.0 copy-start.17
  389.0 0.7 copy.26
  389.7 61.1 %back_reduce.1 = (f32[32,2048]{1,0:T(8,128)}, f32[32,1024]{1,0:T(8,128)}, f32[32,1024]{1,0:T(8,128)}, f32[64,1024]{1,0:T(8,128)}, f32[32,3072]{1,0:T(8,128)}, /*...) custom-call(bf16[8,128,1024]{2,1,0:T(8,128)(2,1)} %bitcast.33, ...), custom_call_target="tpu_custom_call" | custom-call | tf_op jit(solution)/shard_map/back_reduce/pallas_call | solution.py:1840
  450.8 0.0 copy-start.16
  450.8 1.3 slice.23
  452.2 0.0 copy-done.17
  452.2 0.0 copy-start.1
  452.2 1.0 copy.42
  453.1 0.0 copy-done.16
  453.2 0.0 copy-start.18
  453.2 1.3 copy.43
  454.5 0.0 copy-done.22
  454.5 0.7 copy.44
  455.2 0.0 copy-done.24
  455.2 0.7 copy.45
  455.9 0.0 copy-done.23
  455.9 0.7 copy.46
  456.5 0.0 copy-done.21
  456.5 0.7 copy.47
  457.2 0.0 copy-done.20
  457.2 0.7 copy.48
  458.0 0.7 copy.49
  458.7 0.7 copy.50
  (27 shorter events, 0.1 us)
Async XLA Ops:
  0.6 0.7 copy-start
  1.4 150.3 %copy-start.12 = (s32[8]{0:T(128)}, s32[8]{0:T(128)S(1)}, u32[]{:S(2)}) copy-start(s32[8]{0:T(128)S(1)} %convert_element_type.8.flags) | copy-start | bytes 100
  101.8 49.9 %copy-start.8 = (f32[1,128]{1,0:T(1,128)}, f32[1,128]{1,0:T(1,128)S(1)}, u32[]{:S(2)}) copy-start(f32[1,128]{1,0:T(1,128)S(1)} %get-tuple-element.122.gk_ref) | copy-start | bytes 1540
  101.8 49.9 %copy-start.9 = (f32[1,128]{1,0:T(1,128)}, f32[1,128]{1,0:T(1,128)S(1)}, u32[]{:S(2)}) copy-start(f32[1,128]{1,0:T(1,128)S(1)} %get-tuple-element.123.gq_ref) | copy-start | bytes 1540
  101.8 49.9 %copy-start.7 = (f32[1024]{0:T(1024)}, f32[1024]{0:T(1024)S(1)}, u32[]{:S(2)}) copy-start(f32[1024]{0:T(1024)S(1)} %get-tuple-element.121) | copy-start | bytes 12292
  101.8 50.9 %copy-start.6 = (f32[1024]{0:T(1024)}, f32[1024]{0:T(1024)S(1)}, u32[]{:S(2)}) copy-start(f32[1024]{0:T(1024)S(1)} %get-tuple-element.120) | copy-start | bytes 12292
  101.9 1.2 copy-start.10
  103.1 1.2 copy-start.11
  104.3 48.4 %copy-start.4 = (bf16[2,256,1024]{2,1,0:T(8,128)(2,1)S(1)}, bf16[2,256,1024]{2,1,0:T(8,128)(2,1)}, u32[]{:S(2)}) copy-start(bf16[2,256,1024]{2,1,0:T(8,128)(2,1)} %cot.1) | copy-start | bytes 3145732
  151.8 1.0 copy-start.13
  152.7 53.2 %copy-start.5 = (bf16[512,1024]{1,0:T(8,128)(2,1)}, bf16[512,1024]{1,0:T(8,128)(2,1)S(1)}, u32[]{:S(2)}) copy-start(bf16[512,1024]{1,0:T(8,128)(2,1)S(1)} %get-tuple-element.77.wo.wo_in) | copy-start | bytes 3145732
  152.7 53.2 %copy-start.14 = (bf16[2,2048,128]{2,1,0:T(8,128)(2,1)}, bf16[2,2048,128]{2,1,0:T(8,128)(2,1)S(1)}, u32[]{:S(2)}) copy-start(bf16[2,2048,128]{2,1,0:T(8,128)(2,1)S(1)} %get-tuple-element.75.v_in) | copy-start | bytes 3145732
  152.7 53.2 %copy-start.15 = (f32[4,8,2048]{2,1,0:T(8,128)}, f32[4,8,2048]{2,1,0:T(8,128)S(1)}, u32[]{:S(2)}) copy-start(f32[4,8,2048]{2,1,0:T(8,128)S(1)} %get-tuple-element.87.lse_in) | copy-start | bytes 786436
  206.0 1.2 copy-start.2
  207.2 1.1 copy-start.3
  338.2 49.8 %copy-start.26 = (f32[2,8,128]{2,1,0:T(8,128)S(1)}, f32[2,8,128]{2,1,0:T(8,128)}, u32[]{:S(2)}) copy-start(f32[2,8,128]{2,1,0:T(8,128)} %get-tuple-element.105) | copy-start | bytes 24580
  338.3 50.6 %copy-start.25 = (f32[8,1024]{1,0:T(8,128)S(1)}, f32[8,1024]{1,0:T(8,128)}, u32[]{:S(2)}) copy-start(f32[8,1024]{1,0:T(8,128)} %get-tuple-element.104) | copy-start | bytes 98308
  389.0 63.2 %copy-start.17 = (bf16[2,256,1024]{2,1,0:T(8,128)(2,1)S(1)}, bf16[2,256,1024]{2,1,0:T(8,128)(2,1)}, u32[]{:S(2)}) copy-start(bf16[2,256,1024]{2,1,0:T(8,128)(2,1)} %get-tuple-element.134) | copy-start | bytes 3145732
  450.8 2.4 copy-start.16
  452.2 2.3 copy-start.22
  452.2 3.0 copy-start.24
  452.2 3.7 copy-start.23
  452.2 7.3 %copy-start.1 = (s32[2,4]{1,0:T(2,128)S(1)}, s32[2,4]{1,0:T(2,128)}, u32[]{:S(2)}) copy-start(s32[2,4]{1,0:T(2,128)} %param.13) | copy-start | bytes 100
  453.2 3.4 copy-start.21
  453.2 4.1 copy-start.20
  453.2 4.8 %copy-start.19 = (f32[32,3072]{1,0:T(8,128)S(1)}, f32[32,3072]{1,0:T(8,128)}, u32[]{:S(2)}) copy-start(f32[32,3072]{1,0:T(8,128)} %get-tuple-element.141) | copy-start | bytes 1179652
  453.2 5.6 %copy-start.18 = (f32[96,1024]{1,0:T(8,128)S(1)}, f32[96,1024]{1,0:T(8,128)}, u32[]{:S(2)}) copy-start(f32[96,1024]{1,0:T(8,128)} %get-tuple-element.142) | copy-start | bytes 1179652

commit v3 on v2

--- a/solution.py
+++ b/solution.py
@@ -486,6 +486,10 @@
     }
 
 
+def owned(p, l, c):
+    return 2 * c + (p + l + c) % 2
+
+
 def rows_at(index, size, count=1):
     return pl.ds(pl.multiple_of(index * size, size), size * count)
 
@@ -494,7 +498,7 @@
     return [(ref, ref) for ref in refs]
 
 
-def front_kernel(tok, wq, wk, wv, wo, gn, wg, wu, wd, inverse, xs, wa, woq, gf, wgu, wdn, cosine, sine, send_sem, recv_sem, local_sem):
+def front_kernel(tok, wq, wk, wv, wo, gn, wg, wu, wd, inverse, xs, wa, woq, gf, wgu, wdn, cosine, sine, send_sem, recv_sem, in_sem, local_sem, *staged):
     y, x, p, l, c = place()
     peer = peers_of(x, y, p, l, c)
     block = 4 * p + 2 * l + c
@@ -519,8 +523,10 @@
             (wd.at[:, rows_at(h, 512)], wdn.at[rows_at(me, 96)]),
         ]
 
-    def span(base):
-        return in_place(wa.at[rows_at(base // 4, 128)], woq.at[rows_at(base // 4, 256)], gf.at[pl.ds(base, 4)])
+    def span(base, piece):
+        if piece < 2:
+            return in_place(wa.at[rows_at(base // 2 + piece, 64)])
+        return in_place(woq.at[rows_at(base // 4, 256)], gf.at[pl.ds(base, 4)])
 
     def chip(yy, xx, pp, ll):
         slot = (yy * 2 + xx) * 4 + 2 * pp + ll
@@ -535,26 +541,29 @@
     go_far_0 = net.add(peer["p"], [(tok.at[1 - p, upper], xs.at[block, upper])])
     go_far_1 = net.add(peer["p"], [(tok.at[1 - p, lower], xs.at[block, lower])])
     go_near_c = net.add(peer["c"], [(tok.at[p], xs.at[block])])
-    go_across = net.add(peer["p"], span(mine))
-    go_own_x = net.add(peer["x"], span(mine))
+    pieces = range(3)
+    go_across = [net.add(peer["p"], span(mine, k)) for k in pieces]
+    go_own_x = [net.add(peer["x"], span(mine, k)) for k in pieces]
     go_near_relay = net.add(peer["c"], in_place(xs.at[block ^ 2]))
-    go_own_y = net.add(peer["y"], span(mine) + span((y * 2 + 1 - x) * 8 + 4 * p))
-    go_other_y = net.add(peer["y"], span(other))
+    go_own_y = [net.add(peer["y"], span(mine, k) + span((y * 2 + 1 - x) * 8 + 4 * p, k)) for k in pieces]
+    go_other_y = [net.add(peer["y"], span(other, k)) for k in pieces]
     go_far_l0 = net.add(peer["l"], in_place(xs.at[block ^ 4, upper]))
     go_far_l1 = net.add(peer["l"], in_place(xs.at[block ^ 4, lower]))
     go_far_relay = net.add(peer["c"], in_place(xs.at[block ^ 4]))
-    go_other_x = net.add(peer["x"], span(other) + span(((1 - y) * 2 + x) * 8 + 4 * (1 - p)))
+    go_other_x = [net.add(peer["x"], span(other, k) + span(((1 - y) * 2 + x) * 8 + 4 * (1 - p), k)) for k in pieces]
     go_far_l_relay = net.add(peer["c"], in_place(xs.at[block ^ 6]))
     go_mlp_c = net.add(peer["c"], half(1 - c))
     go_mlp_near = net.add(peer["l"], chip(y, x, p, l))
     go_mlp_x = net.add(peer["x"], chip(y, x, p, l))
-    go_mlp_y = net.add(peer["y"], chip(y, x, p, 1 - l))
+    moves = quarter(t) + half(c) + [(tok.at[p], xs.at[block])]
+    taken = [pltpu.make_async_copy(src, stage, in_sem.at[k]) for k, ((src, dst), stage) in enumerate(zip(moves, staged))]
+    own = [pltpu.make_async_copy(stage, dst, local_sem.at[k]) for k, ((src, dst), stage) in enumerate(zip(moves, staged))]
+    for copy in taken:
+        copy.start()
     greet(list(peer.values()))
-    net.start(go_first_l, go_first_d, go_first_c, go_near_c, go_mlp_c)
-    own = [
-        pltpu.make_async_copy(src, dst, local_sem.at[k])
-        for k, (src, dst) in enumerate(quarter(t) + half(c) + [(tok.at[p], xs.at[block])])
-    ]
+    net.start(go_first_l, go_first_d, go_first_c, go_far_0, go_near_c, go_mlp_c)
+    for copy in taken:
+        copy.wait()
     for copy in own:
         copy.start()
 
@@ -573,28 +582,29 @@
     for copy in own:
         copy.wait()
     net.arrived(go_first_l, go_first_d, go_first_c)
-    net.start(go_across, go_own_x, go_near)
-    table(0, 16)
-    net.arrived(go_own_x)
-    net.start(go_own_y)
+    net.start(*go_across, *go_own_x, go_near)
+    table(0, 12)
+    for k in pieces:
+        net.arrived(go_across[k])
+        net.start(go_other_y[k])
+    net.start(go_far_1)
     net.arrived(go_mlp_c)
     net.start(go_mlp_x)
-    net.arrived(go_across)
-    net.start(go_other_y, go_far_0, go_far_1)
     net.arrived(go_near)
-    net.start(go_near_relay, go_mlp_near)
-    table(16, 32)
-    net.arrived(go_other_y)
-    net.start(go_other_x)
+    net.start(go_near_relay)
+    for k in pieces:
+        net.arrived(go_other_y[k])
+        net.start(go_other_x[k])
+    net.arrived(*go_own_x)
+    net.start(*go_own_y, go_mlp_near)
     net.arrived(go_far_0)
     net.start(go_far_l0)
-    net.arrived(go_mlp_near)
-    net.start(go_mlp_y)
+    table(12, 32)
     net.arrived(go_far_1)
     net.start(go_far_l1, go_far_relay)
     net.arrived(go_far_l0, go_far_l1)
     net.start(go_far_l_relay)
-    net.arrived(go_near_c, go_near_relay, go_far_relay, go_far_l_relay, go_own_y, go_other_x, go_mlp_x, go_mlp_y)
+    net.arrived(go_near_c, go_near_relay, go_far_relay, go_far_l_relay, *go_own_y, *go_other_x, go_mlp_x, go_mlp_near)
     net.sent()
 
 
@@ -620,6 +630,16 @@
             pltpu.SemaphoreType.DMA((copies,)),
             pltpu.SemaphoreType.DMA((copies,)),
             pltpu.SemaphoreType.DMA((9,)),
+            pltpu.SemaphoreType.DMA((9,)),
+            pltpu.VMEM((32, 512), bf16),
+            pltpu.VMEM((32, 256), bf16),
+            pltpu.VMEM((32, 256), bf16),
+            pltpu.VMEM((64, 256), bf16),
+            pltpu.VMEM((8, 128), jnp.float32),
+            pltpu.VMEM((32, HALF_FF), bf16),
+            pltpu.VMEM((32, HALF_FF), bf16),
+            pltpu.VMEM((96, 512), bf16),
+            pltpu.VMEM((ROWS, MODEL_DIM), bf16),
         ],
         compiler_params=pltpu.CompilerParams(collective_id=0, has_side_effects=True),
         name="front_gather",
@@ -641,8 +661,9 @@
         self.where = where[2:]
         self.src, self.dst, self.send_sem, self.recv_sem = src, dst, send_sem, recv_sem
 
-    def stays(self, first, second, third, fourth):
-        return (first == second) & (second == third) & (third == fourth)
+    def stays(self, index):
+        p, l, c = self.where
+        return (p == c) & (index == c)
 
     def local(self, c0):
         p, l, c = self.where
@@ -655,27 +676,29 @@
             dst_ref=self.dst.at[p],
             send_sem=self.send_sem.at[c0],
             recv_sem=self.recv_sem.at[p],
-            device_id={"p": l, "l": c, "c": c0},
+            device_id={"p": c, "l": (p + l + c) % 2, "c": c0},
             device_id_type=MESH,
         )
 
+    def start_one(self, c0):
+        here = self.stays(c0)
+
+        @pl.when(here)
+        def _():
+            self.local(c0).start()
+
+        @pl.when(jnp.logical_not(here))
+        def _():
+            self.remote(c0).start()
+
     def start(self):
-        p, l, c = self.where
         for c0 in range(2):
-            here = self.stays(p, l, c, c0)
-
-            @pl.when(here)
-            def _():
-                self.local(c0).start()
-
-            @pl.when(jnp.logical_not(here))
-            def _():
-                self.remote(c0).start()
+            self.start_one(c0)
 
     def wait(self):
         p, l, c = self.where
         for c0 in range(2):
-            here = self.stays(p, l, c, c0)
+            here = self.stays(c0)
 
             @pl.when(here)
             def _():
@@ -687,14 +710,14 @@
 
         for seq in range(2):
 
-            @pl.when(jnp.logical_not(self.stays(seq, p, l, c)))
+            @pl.when(jnp.logical_not(self.stays(seq)))
             def _():
                 pltpu.make_async_remote_copy(
                     src_ref=self.src.at[pl.ds(0, ROWS)],
                     dst_ref=self.dst.at[seq],
                     send_sem=self.send_sem.at[0],
                     recv_sem=self.recv_sem.at[seq],
-                    device_id={"p": l, "l": c, "c": 1 - c},
+                    device_id={"p": 1 - p},
                     device_id_type=MESH,
                 ).wait_recv()
 
@@ -704,22 +727,22 @@
         self.where = where[2:]
         self.src, self.dst, self.send_sem, self.recv_sem = src, dst, send_sem, recv_sem
 
-    def here(self, first):
+    def here(self, index):
         p, l, c = self.where
-        return (first == p) & (p == l) & (l == c)
+        return (p == c) & (index == c)
 
     def local(self, seq):
         p, l, c = self.where
-        return pltpu.make_async_copy(self.src.at[seq], self.dst.at[l, c], self.send_sem.at[seq])
+        return pltpu.make_async_copy(self.src.at[seq], self.dst.at[p, c], self.send_sem.at[seq])
 
     def remote(self, seq):
         p, l, c = self.where
         return pltpu.make_async_remote_copy(
             src_ref=self.src.at[seq],
-            dst_ref=self.dst.at[l, c],
+            dst_ref=self.dst.at[p, c],
             send_sem=self.send_sem.at[seq],
             recv_sem=self.recv_sem.at[c],
-            device_id={"p": seq, "l": p, "c": l},
+            device_id={"p": seq, "l": (seq + l + p) % 2, "c": p},
             device_id_type=MESH,
         )
 
@@ -748,14 +771,14 @@
 
         for block in range(2):
 
-            @pl.when(jnp.logical_not((l == p) & (c == l) & (block == c)))
+            @pl.when(jnp.logical_not(self.here(block)))
             def _():
                 pltpu.make_async_remote_copy(
                     src_ref=self.src.at[0],
                     dst_ref=self.dst.at[c, block],
                     send_sem=self.send_sem.at[0],
                     recv_sem=self.recv_sem.at[block],
-                    device_id={"p": l, "l": c, "c": 1 - c},
+                    device_id={"p": 1 - p},
                     device_id_type=MESH,
                 ).wait_recv()
 
@@ -779,7 +802,7 @@
 def attend_kernel(
     flags, x_ref, w_ref, ga_ref, gq_ref, gk_ref, cos_ref, sin_ref, woq, wgu_in, wdn_in,
     n_ref, q_ref, k_ref, v_ref, qr_ref, kr_ref, o_ref, lse_ref, wo, wgu, wdn,
-    send_sem, recv_sem, local_sem,
+    stage, send_sem, recv_sem, local_sem,
 ):
     y, x, p, l, c = place()
     peer = peers_of(x, y, p, l, c)
@@ -795,8 +818,9 @@
 
     go_mlp_y = net.add(peer["y"], chip(y, x, p, l) + chip(y, 1 - x, p, l))
     go_mlp_x = net.add(peer["x"], chip(y, x, p, 1 - l) + chip(1 - y, x, p, 1 - l))
-    go_far = net.add(peer["p"], chip(y, x, p, l))
-    go_far_l = net.add(peer["l"], chip(y, x, 1 - p, l))
+    go_far = [net.add(peer["p"], [pair]) for pair in chip(y, x, p, l)]
+    go_far_l = [net.add(peer["l"], [pair]) for pair in chip(y, x, 1 - p, l)]
+    go_near_y = net.add(peer["y"], chip(y, x, p, 1 - l))
     go_wo_l = net.add(peer["l"], [rows_of(2 * (1 - l) + c)])
     go_wo_d = net.add(peer["d"], [rows_of(2 * (1 - l) + 1 - c)])
     go_wo_c = net.add(peer["c"], [rows_of(2 * l + 1 - c)])
@@ -805,10 +829,11 @@
     @pl.when(step == 0)
     def _():
         greet(list(peer.values()))
-        net.start(go_far, go_mlp_y, go_mlp_x, go_wo_l, go_wo_d, go_wo_c)
-        copy = pltpu.make_async_copy(*rows_of(t), local_sem.at[0])
+        net.start(go_near_y, *go_far, go_wo_l, go_wo_d, go_wo_c)
+        copy = pltpu.make_async_copy(rows_of(t)[0], stage, local_sem.at[0])
         copy.start()
         copy.wait()
+        pltpu.make_async_copy(stage, rows_of(t)[1], local_sem.at[1]).start()
 
     @pl.when(step < PROJECT)
     def _():
@@ -829,10 +854,17 @@
             at = (QH + KH + h) * HEAD_DIM
             v_ref[h, rows, :] = full[:, at : at + HEAD_DIM].astype(jnp.bfloat16)
 
-    @pl.when(step == PROJECT + 4)
+    @pl.when(step == PROJECT)
     def _():
-        net.arrived(go_far)
-        net.start(go_far_l)
+        net.arrived(go_near_y)
+        net.start(go_mlp_x, go_mlp_y)
+
+    for k, at in enumerate((PROJECT + 2, PROJECT + 4)):
+
+        @pl.when(step == at)
+        def _():
+            net.arrived(go_far[k])
+            net.start(go_far_l[k])
 
     @pl.when(step >= PROJECT)
     def _():
@@ -867,7 +899,8 @@
 
     @pl.when(step == PROJECT + 2 * NBLK - 1)
     def _():
-        net.arrived(go_mlp_y, go_mlp_x, go_far_l, go_wo_l, go_wo_d, go_wo_c)
+        pltpu.make_async_copy(stage, rows_of(t)[1], local_sem.at[1]).wait()
+        net.arrived(go_mlp_y, go_mlp_x, *go_far_l, go_wo_l, go_wo_d, go_wo_c)
         net.sent()
 
 
@@ -925,7 +958,9 @@
                 pl.BlockSpec((2, 8, BLK), lambda s, f: (late(s) // NBLK, 0, late(s) % NBLK)),
             ]
             + [any_spec] * 3,
-            scratch_shapes=[pltpu.SemaphoreType.DMA((copies,))] * 2 + [pltpu.SemaphoreType.DMA((1,))],
+            scratch_shapes=[pltpu.VMEM((512, 256), bf16)]
+            + [pltpu.SemaphoreType.DMA((copies,))] * 2
+            + [pltpu.SemaphoreType.DMA((2,))],
         ),
         input_output_aliases={9: 9, 10: 10},
         compiler_params=pltpu.CompilerParams(
@@ -940,7 +975,7 @@
 
 def resid_kernel(
     attn, wo, g_mlp, xs, cot, wgu_in, wdn_in,
-    resid, mlp_in, wgu, wdn, wdx, wdo, dy,
+    resid, mlp_in, wgu, wdn, wdx, dy,
     send_c, recv_c, send_l, recv_l, keep, x_own, send_sem, recv_sem, local_sem, dy_send, dy_recv,
 ):
     where = place()
@@ -959,10 +994,14 @@
             found.append((wdn.at[rows_at((1 - c) * 8 + slot, 192)], wdx.at[rows_at(slot, 192)]))
         return found
 
-    go_far_x = net.add(peer["x"], chip(y, x, 1 - p, l))
-    go_far_y = net.add(peer["y"], chip(y, x, 1 - p, l) + chip(y, 1 - x, 1 - p, l))
-    go_fal_y = net.add(peer["y"], chip(y, x, 1 - p, 1 - l))
-    go_fal_x = net.add(peer["x"], chip(y, x, 1 - p, 1 - l) + chip(1 - y, x, 1 - p, 1 - l))
+    def hop(name, *chips):
+        found = [chip(*one) for one in chips]
+        return [net.add(peer[name], [pairs[k] for pairs in found]) for k in range(2)]
+
+    go_far_x = hop("x", (y, x, 1 - p, l))
+    go_far_y = hop("y", (y, x, 1 - p, l), (y, 1 - x, 1 - p, l))
+    go_fal_y = hop("y", (y, x, 1 - p, 1 - l))
+    go_fal_x = hop("x", (y, x, 1 - p, 1 - l), (1 - y, x, 1 - p, 1 - l))
     go_down_me = net.add(peer["c"], down(p, l))
     go_down_near = net.add(peer["c"], down(p, 1 - l))
     go_down_far = net.add(peer["c"], down(1 - p, l))
@@ -974,13 +1013,13 @@
     go_dy_c = net.add(peer["c"], in_place(dy.at[c]))
     spread = Spread(where, cot, dy, dy_send, dy_recv)
     greet(line_peers(p, l, c) + [peer["x"], peer["y"]])
-    net.start(go_far_x, go_fal_y, go_down_me, go_down_near)
-    fetch = pltpu.make_async_copy(xs.at[rows_at(2 * l + c, OWN)], x_own, local_sem.at[0])
+    spread.start()
+    net.start(go_far_x[1], go_fal_y[1], go_far_x[0], go_fal_y[0], go_down_me, go_down_near)
+    fetch = pltpu.make_async_copy(xs.at[rows_at(owned(p, l, c), OWN)], x_own, local_sem.at[0])
     fetch.start()
-    own_down = pltpu.make_async_copy(wdn.at[rows_at(c, HALF_FF)], wdo, local_sem.at[1])
 
     def project(ll, cc, write):
-        part = attn[rows_at(2 * ll + cc, OWN), :]
+        part = attn[rows_at(owned(p, ll, cc), OWN), :]
 
         def chunk(k, carry):
             cols = rows_at(k, 256)
@@ -1000,6 +1039,12 @@
             keep[k, :, cols] = value
 
         return write
+
+    def relay_hop(k):
+        net.arrived(go_far_x[k])
+        net.start(go_far_y[k])
+        net.arrived(go_fal_y[k])
+        net.start(go_fal_x[k])
 
     project(1 - l, 1 - c, give(0))
     net.start(go_give_0)
@@ -1007,15 +1052,12 @@
     net.arrived(go_give_0)
     send_l[...] = (keep[0] + recv_c[0].astype(jnp.float32)).astype(jnp.bfloat16)
     net.start(go_cross)
-    spread.start()
+    relay_hop(1)
     project(l, 1 - c, give(1))
     net.start(go_give_1)
     project(l, c, hold(1))
     fetch.wait()
-    net.arrived(go_far_x)
-    net.start(go_far_y)
-    net.arrived(go_fal_y)
-    net.start(go_fal_x)
+    relay_hop(0)
     net.arrived(go_give_1)
     keep[1] += recv_c[1].astype(jnp.float32) + x_own[...].astype(jnp.float32)
     net.arrived(go_cross)
@@ -1024,15 +1066,14 @@
     r = lax.rsqrt(jnp.mean(total * total, axis=-1, keepdims=True) + EPS)
     mlp_in[c] = (total * r * g_mlp[...]).astype(jnp.bfloat16)
     net.start(go_share)
-    net.arrived(go_far_y)
+    net.arrived(go_far_y[1])
     net.start(go_down_far)
     spread.wait()
     net.start(go_dy_c)
-    net.arrived(go_fal_x)
+    net.arrived(go_fal_x[1])
     net.start(go_down_fal)
-    own_down.start()
+    net.arrived(go_far_y[0], go_fal_x[0])
     net.arrived(go_down_me, go_down_near, go_down_far, go_down_fal, go_share, go_dy_c)
-    own_down.wait()
     net.sent()
 
 
@@ -1049,11 +1090,10 @@
             jax.ShapeDtypeStruct(wgu.shape, bf16),
             jax.ShapeDtypeStruct(wdn.shape, bf16),
             jax.ShapeDtypeStruct((HALF_FF, 512), bf16),
-            jax.ShapeDtypeStruct((HALF_FF, 512), bf16),
             jax.ShapeDtypeStruct((2, 2, ROWS, MODEL_DIM), bf16),
         ),
         in_specs=[vmem] * 3 + [any_spec] * 4,
-        out_specs=[vmem] * 2 + [any_spec] * 5,
+        out_specs=[vmem] * 2 + [any_spec] * 4,
         scratch_shapes=[
             pltpu.VMEM((2, OWN, MODEL_DIM), bf16),
             pltpu.VMEM((2, OWN, MODEL_DIM), bf16),
@@ -1063,7 +1103,7 @@
             pltpu.VMEM((OWN, MODEL_DIM), bf16),
             pltpu.SemaphoreType.DMA((copies,)),
             pltpu.SemaphoreType.DMA((copies,)),
-            pltpu.SemaphoreType.DMA((2,)),
+            pltpu.SemaphoreType.DMA((1,)),
             pltpu.SemaphoreType.DMA((2,)),
             pltpu.SemaphoreType.DMA((2,)),
         ],
@@ -1076,23 +1116,46 @@
 
 
 CHUNK = 512
+EARLY = 1024
 
 
 def forward_kernel(
-    m_ref, dy_ref, w_ref, wo_ref, wx_ref, resid, g_mlp,
-    gg, gu, gd, d_resid, db, res, dg,
-    mt, dyt, hid, dgt, dup, d_in, down, give, take, send_sem, recv_sem,
+    m_ref, dy_ref, w_ref, wdn, wx_ref, resid, g_mlp,
+    ggu, gdb, rb, d_resid, db, res, dg,
+    mt, dyt, hid, dgt, dup, d_in, down, give, take, all_down, ggv, gdv, send_sem, recv_sem, load_sem, out_sem,
 ):
-    y, x, p, l, c = place()
-    peer = {"c": 1 - c}
+    where = place()
+    y, x, p, l, c = where
+    peer = peers_of(x, y, p, l, c)
+    red = Reduction(where)
     net = Plan(send_sem, recv_sem)
-    go_d_in = net.add(peer, [(give.at[0], take.at[0])])
-    go_down = net.add(peer, [(give.at[1], take.at[1])])
+    go_d_in = net.add(peer["c"], [(give.at[0], take.at[0])])
+    go_down = net.add(peer["c"], [(give.at[1], take.at[1])])
+    go_gd, go_wide, outs = [], [], []
+    for f in range(HALF_FF // CHUNK):
+        part_f = pl.ds(f * CHUNK, CHUNK)
+        go_gd.append(net.add(peer["c"], [(gdv.at[part_f, rows_at(1 - c, 512)], gdb.at[c, part_f])]))
+        outs.append(
+            [
+                pltpu.make_async_copy(ggv.at[:, :, part_f], ggu.at[:, :, part_f], out_sem.at[2 * f]),
+                pltpu.make_async_copy(gdv.at[part_f, rows_at(c, 512)], gdb.at[c, part_f], out_sem.at[2 * f + 1]),
+            ]
+        )
+        go_wide.append([])
+        if f * CHUNK < EARLY:
+            for n, kind in enumerate(KINDS):
+                pairs = []
+                for k in range(2):
+                    slot = chip_slot(*red.place(kind, k, True), *red.z[kind])
+                    pairs.append((ggv.at[:, rows_at(slot, 64), part_f], rb.at[n, k, :, :, part_f]))
+                go_wide[f].append(net.add(peer[red.first_peer(kind)], pairs))
     step = pl.program_id(0)
+    fetch = pltpu.make_async_copy(wdn.at[rows_at(c, HALF_FF)], all_down, load_sem.at[0])
 
     @pl.when(step == 0)
     def _():
-        greet([peer])
+        fetch.start()
+        greet([peer["c"], peer["x"], peer["y"]])
 
         def flip(k, carry):
             rows = rows_at(k, 256)
@@ -1103,11 +1166,13 @@
         lax.fori_loop(0, 4, flip, 0)
         d_in[...] = jnp.zeros_like(d_in)
         down[...] = jnp.zeros_like(down)
-
+        fetch.wait()
+
+    wo_ref = all_down.at[rows_at(step, CHUNK)]
     own_cols, other_cols = rows_at(c, 512), rows_at(1 - c, 512)
 
     def part(r, carry):
-        rows = rows_at(r, 256)
+        rows = rows_at(r, 512)
         value, grad = m_ref[rows, :], dy_ref
         gate, up = dot(value, w_ref[0]), dot(value, w_ref[1])
         d_hidden = dot(grad[rows, own_cols], wo_ref[...], NT) + dot(grad[rows, other_cols], wx_ref[...], NT)
@@ -1124,7 +1189,7 @@
         down[rows, other_cols] += dot(hidden, wx_ref[...])
         return carry
 
-    lax.fori_loop(0, 4, part, 0)
+    lax.fori_loop(0, 2, part, 0)
 
     @pl.when(step == pl.num_programs(0) - 1)
     def _():
@@ -1132,14 +1197,23 @@
         give[1] = down[rows_at(1 - c, OWN), :].astype(jnp.bfloat16)
         net.start(go_d_in, go_down)
 
+    now = rows_at(step, CHUNK)
+
     def weights(k, carry):
-        rows = rows_at(k, 256)
-        gg[rows, :] = dot(mt[rows, :], dgt[...]).astype(jnp.bfloat16)
-        gu[rows, :] = dot(mt[rows, :], dup[...]).astype(jnp.bfloat16)
-        gd[:, rows] = dot(dyt[rows, :], hid[...]).T.astype(jnp.bfloat16)
+        rows = rows_at(k, 512)
+        ggv[0, rows, now] = dot(mt[rows, :], dgt[...]).astype(jnp.bfloat16)
+        ggv[1, rows, now] = dot(mt[rows, :], dup[...]).astype(jnp.bfloat16)
+        gdv[now, rows] = dot(dyt[rows, :], hid[...]).T.astype(jnp.bfloat16)
         return carry
 
-    lax.fori_loop(0, 4, weights, 0)
+    lax.fori_loop(0, 2, weights, 0)
+    for f in range(HALF_FF // CHUNK):
+
+        @pl.when(step == f)
+        def _():
+            net.start(*go_wide[f], go_gd[f])
+            for copy in outs[f]:
+                copy.start()
 
     @pl.when(step == pl.num_programs(0) - 1)
     def _():
@@ -1162,34 +1236,39 @@
             return carry
 
         lax.fori_loop(0, 8, finish, 0)
+        for f in range(HALF_FF // CHUNK):
+            net.arrived(*go_wide[f], go_gd[f])
+            for copy in outs[f]:
+                copy.wait()
         net.sent()
 
 
-def feed_forward(mlp_in, dy, wgu, wdo, wdx, resid, g_mlp):
+def feed_forward(mlp_in, dy, wgu, wdn, wdx, resid, g_mlp):
     bf16, f32 = jnp.bfloat16, jnp.float32
 
     def whole(shape):
         return pl.BlockSpec(shape, lambda f: (0,) * len(shape), pipeline_mode=pl.Buffered(1))
 
     down = pl.BlockSpec((CHUNK, 512), lambda f: (f, 0))
-    wide = pl.BlockSpec((MODEL_DIM, CHUNK), lambda f: (0, f))
+    copies = 24
     rows = (1024, MODEL_DIM)
     own = (OWN, MODEL_DIM)
     return pl.pallas_call(
         forward_kernel,
         grid=(HALF_FF // CHUNK,),
         out_shape=(
-            jax.ShapeDtypeStruct((MODEL_DIM, HALF_FF), bf16),
-            jax.ShapeDtypeStruct((MODEL_DIM, HALF_FF), bf16),
-            jax.ShapeDtypeStruct((HALF_FF, MODEL_DIM), bf16),
+            jax.ShapeDtypeStruct((2, MODEL_DIM, HALF_FF), bf16),
+            jax.ShapeDtypeStruct((2, HALF_FF, 512), bf16),
+            jax.ShapeDtypeStruct((4, 2, 2, 64, EARLY), bf16),
             jax.ShapeDtypeStruct(own, f32),
             jax.ShapeDtypeStruct(own, bf16),
             jax.ShapeDtypeStruct(own, bf16),
             jax.ShapeDtypeStruct((8, MODEL_DIM), f32),
         ),
-        in_specs=[whole(rows), whole(rows), pl.BlockSpec((2, MODEL_DIM, CHUNK), lambda f: (0, 0, f)), down, down]
+        in_specs=[whole(rows), whole(rows), pl.BlockSpec((2, MODEL_DIM, CHUNK), lambda f: (0, 0, f))]
+        + [pl.BlockSpec(memory_space=pl.ANY), down]
         + [whole(own), whole((1, MODEL_DIM))],
-        out_specs=[wide, wide, pl.BlockSpec((CHUNK, MODEL_DIM), lambda f: (f, 0))]
+        out_specs=[pl.BlockSpec(memory_space=pl.ANY)] * 3
         + [whole(own), whole(own), whole(own), whole((8, MODEL_DIM))],
         scratch_shapes=[
             pltpu.VMEM(rows, bf16),
@@ -1201,14 +1280,19 @@
             pltpu.VMEM(rows, f32),
             pltpu.VMEM((2,) + own, bf16),
             pltpu.VMEM((2,) + own, bf16),
-            pltpu.SemaphoreType.DMA((2,)),
-            pltpu.SemaphoreType.DMA((2,)),
+            pltpu.VMEM((HALF_FF, 512), bf16),
+            pltpu.VMEM((2, MODEL_DIM, HALF_FF), bf16),
+            pltpu.VMEM((HALF_FF, MODEL_DIM), bf16),
+            pltpu.SemaphoreType.DMA((copies,)),
+            pltpu.SemaphoreType.DMA((copies,)),
+            pltpu.SemaphoreType.DMA((1,)),
+            pltpu.SemaphoreType.DMA((6,)),
         ],
         compiler_params=pltpu.CompilerParams(
-            collective_id=6, has_side_effects=True, vmem_limit_bytes=56 * 1024 * 1024
+            collective_id=6, has_side_effects=True, vmem_limit_bytes=60 * 1024 * 1024
         ),
         name="feed_forward",
-    )(mlp_in, dy, wgu, wdo, wdx, resid, g_mlp)
+    )(mlp_in, dy, wgu, wdn, wdx, resid, g_mlp)
 
 
 KINDS = ME, NEAR, FAR, FAL = range(4)
@@ -1243,10 +1327,10 @@
 
 
 def attend_back_kernel(
-    flags, q_in, k_in, v_in, o_in, db_in, wo_in, lse_in, qr_in, kr_in, cos_in, sin_in, gg, gu, gd, res, gq_ref, gk_ref,
-    d_out, goq, fw_out, fd_out, od_out, out, dg_ref,
+    flags, q_in, k_in, v_in, o_in, db_in, wo_in, lse_in, qr_in, kr_in, cos_in, sin_in, ggu, gdb, rb_in, res, gq_ref, gk_ref,
+    d_out, goq, og_out, od_out, fw_out, fd_out, out, dg_ref,
     q_ref, k_ref, v_ref, o_ref, dall, wo, lse_ref, qr_ref, kr_ref, cos_ref, sin_ref,
-    da, delta, dbuf, dq_acc, dk_acc, dv_acc, og, gdb, od, rb, rbd, rc, rcd, rz, rzd, go,
+    da, delta, dbuf, dq_acc, dk_acc, dv_acc, og, od, rb, rbd, rc, rcd, rz, rzd, go,
     send_sem, recv_sem, load_sem, own_sem, out_sem, back_send, back_recv,
 ):
     where = place()
@@ -1254,31 +1338,34 @@
     peer = peers_of(x, y, p, l, c)
     red = Reduction(where)
     net = Plan(send_sem, recv_sem)
-    wide_of, deep_of, second_of = {}, {}, {}
     t = 2 * l + c
 
     def block(index):
         return dall.at[rows_at(index, OWN)]
 
-    go_db_l = net.add(peer["l"], [(db_in, block(t))])
-    go_db_c = net.add(peer["c"], [(db_in, block(t))])
-    go_db_r = net.add(peer["c"], in_place(block(2 * (1 - l) + c)))
-    go_gd_c = net.add(peer["c"], [(gd.at[:, rows_at(1 - c, 512)], gdb.at[c])])
-    go_fal = net.add(peer["l"], [(og.at[1, red.kept(FAL)], rz), (od.at[3, red.kept(FAL)], rzd)])
+    mine = owned(p, l, c)
+    go_db_l = net.add(peer["l"], [(db_in, block(mine))])
+    go_db_c = net.add(peer["c"], [(db_in, block(mine))])
+    go_db_r = net.add(peer["c"], in_place(block(owned(p, 1 - l, c))))
+    early, late = pl.ds(0, EARLY), pl.ds(EARLY, HALF_FF - EARLY)
+    first_of, second_a, second_b = {}, {}, {}
     for n, kind in enumerate(KINDS):
-        wide, deep = [], []
+        pairs = []
         for k in range(2):
             yy, xx = red.place(kind, k, True)
             slot = chip_slot(yy, xx, *red.z[kind])
-            if n >= 2:
-                wide.append((gg.at[rows_at(slot, 64)], rb.at[n - 2, k, 0]))
-                wide.append((gu.at[rows_at(slot, 64)], rb.at[n - 2, k, 1]))
-            deep.append((gdb.at[yy, rows_at(xx * 4 + 2 * red.z[kind][0] + red.z[kind][1], 192)], rbd.at[n, k]))
-        deep_of[kind] = net.add(peer[red.first_peer(kind)], deep)
+            pairs.append((ggu.at[:, rows_at(slot, 64), late], rb.at[n, k, :, :, late]))
+            pairs.append((gdb.at[yy, rows_at(xx * 4 + 2 * red.z[kind][0] + red.z[kind][1], 192)], rbd.at[n, k]))
+        first_of[kind] = net.add(peer[red.first_peer(kind)], pairs)
         if n >= 2:
-            wide_of[kind] = net.add(peer[red.first_peer(kind)], wide)
-            away = 1 - red.kept(kind)
-            second_of[kind] = net.add(peer[red.second_peer(kind)], [(og.at[n - 2, away], rc.at[n - 2]), (od.at[n, away], rcd.at[n - 2])])
+            away, link = 1 - red.kept(kind), peer[red.second_peer(kind)]
+            second_a[kind] = net.add(link, [(og.at[n, away, :, :, early], rc.at[n - 2, :, :, early])])
+            second_b[kind] = net.add(link, [(og.at[n, away, :, :, late], rc.at[n - 2, :, :, late]), (od.at[n, away], rcd.at[n - 2])])
+    u_far, u_fal = red.kept(FAR), red.kept(FAL)
+    go_fal_a = net.add(peer["l"], [(og.at[FAL, u_fal, :, :, early], rz.at[:, :, early])])
+    go_fal_b = net.add(peer["l"], [(og.at[FAL, u_fal, :, :, late], rz.at[:, :, late]), (od.at[FAL, u_fal], rzd)])
+    go_far_a = net.add(peer["p"], [(og.at[FAR, u_far, :, :, early], fw_out.at[:, :, early])])
+    go_far_b = net.add(peer["p"], [(og.at[FAR, u_far, :, :, late], fw_out.at[:, :, late]), (od.at[FAR, u_far], fd_out)])
     home = Return(where, res, out, back_send, back_recv)
 
     def columns(q):
@@ -1292,50 +1379,38 @@
         pltpu.make_async_copy(src, dst, load_sem.at[k])
         for k, (src, dst) in enumerate(
             [
-                (db_in, block(t)), (wo_in, wo), (o_in, o_ref), (q_in, q_ref), (k_in, k_ref), (v_in, v_ref), (lse_in, lse_ref),
+                (db_in, block(mine)), (wo_in, wo), (o_in, o_ref), (q_in, q_ref), (k_in, k_ref), (v_in, v_ref), (lse_in, lse_ref),
                 (cos_in, cos_ref), (sin_in, sin_ref), (qr_in, qr_ref), (kr_in, kr_ref),
-                (gd.at[:, rows_at(c, 512)], gdb.at[c]),
             ]
         )
     ]
-    own = []
-    for n, kind in enumerate(KINDS[2:]):
-        for k in range(2):
-            slot = chip_slot(*red.place(kind, k, False), *red.z[kind])
-            for m, ref in enumerate((gg, gu)):
-                own.append(pltpu.make_async_copy(ref.at[rows_at(slot, 64)], og.at[n, k, m], own_sem.at[len(own)]))
-
-    def wide_sum(kind):
-        n = KINDS.index(kind) - 2
-        for k in range(2):
-
-            def wide(r, carry):
-                rows = rows_at(r, 16)
-                for m in range(2):
-                    total = og[n, k, m, rows, :].astype(jnp.float32) + rb[n, k, m, rows, :].astype(jnp.float32)
-                    og[n, k, m, rows, :] = total.astype(jnp.bfloat16)
-                return carry
-
-            lax.fori_loop(0, 4, wide, 0)
-
-    def deep_sum(kind):
-        n = KINDS.index(kind)
+    own = [pltpu.make_async_copy(rb_in, rb.at[:, :, :, :, early], own_sem.at[0])]
+    for n, kind in enumerate(KINDS):
         for k in range(2):
             yy, xx = red.place(kind, k, False)
-            at = (xx * 4 + 2 * red.z[kind][0] + red.z[kind][1]) * 192
-
-            def deep(r, carry):
-                rows = rows_at(r, 32)
-                mine = gdb[yy, pl.ds(pl.multiple_of(at + r * 32, 32), 32), :]
-                od[n, k, rows, :] = (mine.astype(jnp.float32) + rbd[n, k, rows, :].astype(jnp.float32)).astype(jnp.bfloat16)
-                return carry
-
-            lax.fori_loop(0, 6, deep, 0)
-
-    def more(kind, wide, deep):
-        n, u = KINDS.index(kind), red.kept(kind)
-        og[n - 2, u] = (og[n - 2, u].astype(jnp.float32) + wide.astype(jnp.float32)).astype(jnp.bfloat16)
-        od[n, u] = (od[n, u].astype(jnp.float32) + deep.astype(jnp.float32)).astype(jnp.bfloat16)
+            slot = chip_slot(yy, xx, *red.z[kind])
+            own.append(pltpu.make_async_copy(ggu.at[:, rows_at(slot, 64)], og.at[n, k], own_sem.at[len(own)]))
+            rows = rows_at(xx * 4 + 2 * red.z[kind][0] + red.z[kind][1], 192)
+            own.append(pltpu.make_async_copy(gdb.at[yy, rows], od.at[n, k], own_sem.at[len(own)]))
+
+    def plus(target, other):
+        target[...] = (target[...].astype(jnp.float32) + other[...].astype(jnp.float32)).astype(jnp.bfloat16)
+
+    def wide_sum(n, cols):
+        def wide(r, carry):
+            k, m, rows = r // 4, (r // 2) % 2, rows_at(r % 2, 32)
+            plus(og.at[n, k, m, rows, cols], rb.at[n, k, m, rows, cols])
+            return carry
+
+        lax.fori_loop(0, 8, wide, 0)
+
+    def deep_sum(n):
+        def deep(r, carry):
+            k, rows = r // 3, rows_at(r % 3, 64)
+            plus(od.at[n, k, rows, :], rbd.at[n, k, rows, :])
+            return carry
+
+        lax.fori_loop(0, 6, deep, 0)
 
     def branch(index):
         rows = rows_at(index, OWN)
@@ -1357,55 +1432,88 @@
 
     step = pl.program_id(0)
     b, g = step // KH, step % KH
-    i = 2 * ((l + b // 2) % 2) + b % 2
+    i = owned(p, (l + b // 2) % 2, b % 2)
 
     @pl.when(step == 0)
     def _():
-        for copy in loads:
+        for copy in loads[:3]:
+            copy.start()
+        for copy in own:
+            copy.start()
+        for copy in loads[3:]:
             copy.start()
         greet(line_peers(p, l, c) + [peer["x"], peer["y"]])
-        net.start(go_db_l, go_db_c, go_gd_c, wide_of[FAR], wide_of[FAL])
-        home.start()
-        for copy in own:
-            copy.start()
+        net.start(go_db_l, go_db_c, first_of[FAR], first_of[FAL])
         dk_acc[...] = jnp.zeros_like(dk_acc)
         dv_acc[...] = jnp.zeros_like(dv_acc)
         dg_ref[...] = jnp.zeros_like(dg_ref)
+        for copy in own:
+            copy.wait()
+        for kind in (FAR, FAL):
+            wide_sum(kind, early)
+            net.start(second_a[kind])
         for copy in loads[:3]:
             copy.wait()
-        branch(t)
-        loads[-1].wait()
-        net.arrived(go_gd_c)
-        net.start(deep_of[FAR], deep_of[FAL])
+        branch(mine)
         net.arrived(go_db_c)
-        branch(2 * l + 1 - c)
-        for copy in loads[3:-1]:
+        branch(owned(p, l, 1 - c))
+        for copy in loads[3:]:
             copy.wait()
+
+    @pl.when(step == 1)
+    def _():
+        net.arrived(second_a[FAL])
+        plus(og.at[FAL, u_fal, :, :, early], rc.at[1, :, :, early])
+        net.start(go_fal_a)
+        net.arrived(second_a[FAR])
+        plus(og.at[FAR, u_far, :, :, early], rc.at[0, :, :, early])
+
+    @pl.when(step == 2)
+    def _():
+        home.start()
+
+    @pl.when(step == 2)
+    def _():
+        for kind in (FAR, FAL):
+            net.arrived(first_of[kind])
+            wide_sum(kind, late)
+            deep_sum(kind)
+            net.start(second_b[kind])
+        net.start(first_of[ME], first_of[NEAR])
 
     @pl.when(step == 2 * KH)
     def _():
         net.arrived(go_db_l)
         net.start(go_db_r)
-        branch(2 * (1 - l) + c)
-        for copy in own:
-            copy.wait()
-        for kind in (FAR, FAL):
-            net.arrived(wide_of[kind], deep_of[kind])
-            wide_sum(kind)
-            deep_sum(kind)
-            net.start(second_of[kind])
+        branch(owned(p, 1 - l, c))
         net.arrived(go_db_r)
-        branch(2 * (1 - l) + 1 - c)
+        branch(owned(p, 1 - l, 1 - c))
+
+    @pl.when(step == 3)
+    def _():
+        net.arrived(go_fal_a)
+        plus(og.at[FAR, u_far, :, :, early], rz.at[:, :, early])
+        net.start(go_far_a)
+
+    @pl.when(step == 4)
+    def _():
+        net.arrived(second_b[FAL])
+        plus(og.at[FAL, u_fal, :, :, late], rc.at[1, :, :, late])
+        plus(od.at[FAL, u_fal], rcd.at[1])
+        net.start(go_fal_b)
+        net.arrived(second_b[FAR])
+        plus(og.at[FAR, u_far, :, :, late], rc.at[0, :, :, late])
+        plus(od.at[FAR, u_far], rcd.at[0])
+
+    @pl.when(step == 5)
+    def _():
+        net.arrived(go_fal_b)
+        plus(og.at[FAR, u_far, :, :, late], rz.at[:, :, late])
+        plus(od.at[FAR, u_far], rzd)
+        net.start(go_far_b)
 
     @pl.when(step == 3 * KH)
     def _():
-        net.arrived(second_of[FAL])
-        more(FAL, rc[1], rcd[1])
-        net.start(go_fal)
-        net.arrived(second_of[FAR])
-        more(FAR, rc[0], rcd[0])
-        net.start(deep_of[ME], deep_of[NEAR])
-
         def grad_out(k, carry):
             cols = rows_at(k, 256)
             go[cols, :] = dot(o_ref[:, cols], dall[...], TN).astype(jnp.bfloat16)
@@ -1464,19 +1572,17 @@
         outs = [pltpu.make_async_copy(dbuf, d_out, out_sem.at[0])]
         outs[0].start()
         for kind in (ME, NEAR):
-            net.arrived(deep_of[kind])
+            wide_sum(kind, early)
+            net.arrived(first_of[kind])
+            wide_sum(kind, late)
             deep_sum(kind)
-        net.arrived(go_fal)
-        more(FAR, rz[...], rzd[...])
-        u = red.kept(FAR)
         outs += [
-            pltpu.make_async_copy(og.at[0, u], fw_out, out_sem.at[2]),
-            pltpu.make_async_copy(od.at[2, u], fd_out, out_sem.at[3]),
-            pltpu.make_async_copy(od.at[pl.ds(0, 2)], od_out, out_sem.at[4]),
+            pltpu.make_async_copy(og.at[pl.ds(0, 2)], og_out, out_sem.at[2]),
+            pltpu.make_async_copy(od.at[pl.ds(0, 2)], od_out, out_sem.at[3]),
         ]
         for copy in outs[1:]:
             copy.start()
-        net.arrived(go_go_l, go_go_d, go_go_c)
+        net.arrived(go_go_l, go_go_d, go_go_c, go_far_a, go_far_b)
         own_go.wait()
         net.sent()
         home.wait()
@@ -1484,7 +1590,7 @@
             copy.wait()
 
 
-def attend_back(flags, q, k, v, o, db, wo, lse, qr, kr, cosine, sine, gg, gu, gd, res, gq, gk):
+def attend_back(flags, q, k, v, o, db, wo, lse, qr, kr, cosine, sine, ggu, gdb, rb, res, gq, gk):
     bf16, f32 = jnp.bfloat16, jnp.float32
     any_spec = pl.BlockSpec(memory_space=pl.ANY)
     gain = pl.BlockSpec((1, HEAD_DIM), lambda s, f: (0, 0))
@@ -1498,9 +1604,10 @@
         out_shape=(
             jax.ShapeDtypeStruct((SEQ_ROWS, 1024), bf16),
             jax.ShapeDtypeStruct((2048, 256), bf16),
+            jax.ShapeDtypeStruct((2, 2, 2, 64, HALF_FF), bf16),
+            jax.ShapeDtypeStruct((2, 2, 192, 512), bf16),
             jax.ShapeDtypeStruct((2, 64, HALF_FF), bf16),
             jax.ShapeDtypeStruct((192, 512), bf16),
-            jax.ShapeDtypeStruct((2, 2, 192, 512), bf16),
             jax.ShapeDtypeStruct((2, ROWS, MODEL_DIM), bf16),
             jax.ShapeDtypeStruct((2, 8, HEAD_DIM), f32),
         ),
@@ -1508,7 +1615,7 @@
             num_scalar_prefetch=1,
             grid=(4 * KH,),
             in_specs=[any_spec] * 15 + [gain] * 2,
-            out_specs=[any_spec] * 6 + [pl.BlockSpec((2, 8, HEAD_DIM), lambda s, f: (0, 0, 0))],
+            out_specs=[any_spec] * 7 + [pl.BlockSpec((2, 8, HEAD_DIM), lambda s, f: (0, 0, 0))],
             scratch_shapes=[vm(q), vm(k), vm(v), vm(o), pltpu.VMEM((SEQ_ROWS, MODEL_DIM), bf16), vm(wo), vm(lse), vm(qr), vm(kr)]
             + [vm(cosine), vm(sine)]
             + [
@@ -1518,10 +1625,9 @@
                 pltpu.VMEM((2, BLK, HEAD_DIM), f32),
                 pltpu.VMEM((KH, SEQ_ROWS, HEAD_DIM), f32),
                 pltpu.VMEM((KH, SEQ_ROWS, HEAD_DIM), f32),
-                pltpu.VMEM((2, 2, 2, 64, HALF_FF), bf16),
-                pltpu.VMEM((2, HALF_FF, 512), bf16),
+                pltpu.VMEM((4, 2, 2, 64, HALF_FF), bf16),
                 pltpu.VMEM((4, 2, 192, 512), bf16),
-                pltpu.VMEM((2, 2, 2, 64, HALF_FF), bf16),
+                pltpu.VMEM((4, 2, 2, 64, HALF_FF), bf16),
                 pltpu.VMEM((4, 2, 192, 512), bf16),
                 pltpu.VMEM((2, 2, 64, HALF_FF), bf16),
                 pltpu.VMEM((2, 192, 512), bf16),
@@ -1530,67 +1636,98 @@
                 pltpu.VMEM((512, MODEL_DIM), bf16),
                 pltpu.SemaphoreType.DMA((copies,)),
                 pltpu.SemaphoreType.DMA((copies,)),
-                pltpu.SemaphoreType.DMA((12,)),
-                pltpu.SemaphoreType.DMA((8,)),
-                pltpu.SemaphoreType.DMA((5,)),
+                pltpu.SemaphoreType.DMA((11,)),
+                pltpu.SemaphoreType.DMA((17,)),
+                pltpu.SemaphoreType.DMA((4,)),
                 pltpu.SemaphoreType.DMA((2,)),
                 pltpu.SemaphoreType.DMA((2,)),
             ],
         ),
         compiler_params=pltpu.CompilerParams(
-            collective_id=4, has_side_effects=True, vmem_limit_bytes=58 * 1024 * 1024
+            collective_id=4, has_side_effects=True, vmem_limit_bytes=60 * 1024 * 1024
         ),
         cost_estimate=pl.CostEstimate(
             flops=10 * QH * SEQ_ROWS * SEQ_ROWS * HEAD_DIM, bytes_accessed=40 << 20, transcendentals=QH * SEQ_ROWS * SEQ_ROWS
         ),
         name="attend_back",
-    )(flags, q, k, v, o, db, wo, lse, qr, kr, cosine, sine, gg, gu, gd, res, gq, gk)
-
-
-def normed_kernel(
-    d_in, w_in, n_in, xs, gg, gu, fw_in, fd_in, od_in, dr_ref, ga_ref,
-    gt, dg, pq, me_w, me_d, near_w, near_d,
-    d_ref, w_ref, n_ref, x_ref, send_c, recv_c, send_l, recv_l, keep, og, rb, od, rx, rxd, rz, rzd,
-    send_sem, recv_sem, load_sem, own_sem,
+    )(flags, q, k, v, o, db, wo, lse, qr, kr, cosine, sine, ggu, gdb, rb, res, gq, gk)
+
+
+def tail_kernel(
+    d_in, w_in, n_in, xs, og_in, od_in, fw_in, fd_in, goq_in, dr_ref, ga_ref, dgm_ref, dgh_ref,
+    out_query, out_key, out_value, out_out, out_gate, out_up, out_down, gout, tokens,
+    d_ref, w_ref, n_ref, x_ref, goq, send_c, recv_c, send_l, recv_l, keep, gt, landed,
+    og, od, rx, rxd, rz, rzd, total_w, total_d, fw, fd,
+    pq, work, wgo, ry, ryo, ox, oxo, rs, rso, rq, rqo, gs, gr,
+    send_sem, recv_sem, load_sem, back_send, back_recv,
 ):
     where = place()
     y, x, p, l, c = where
     peer = peers_of(x, y, p, l, c)
     red = Reduction(where)
     net = Plan(send_sem, recv_sem)
-    wide_of, deep_of, second_of = {}, {}, {}
+    second_of = {}
     t = 2 * l + c
-    two = KINDS[:2]
-    own = []
-    for n, kind in enumerate(two):
-        wide = []
-        for k in range(2):
-            away = chip_slot(*red.place(kind, k, True), *red.z[kind])
-            here = chip_slot(*red.place(kind, k, False), *red.z[kind])
-            for m, ref in enumerate((gg, gu)):
-                wide.append((ref.at[rows_at(away, 64)], rb.at[n, k, m]))
-                own.append(pltpu.make_async_copy(ref.at[rows_at(here, 64)], og.at[n, k, m], own_sem.at[len(own)]))
-        wide_of[kind] = net.add(peer[red.first_peer(kind)], wide)
+    for n, kind in enumerate(KINDS[:2]):
         away = 1 - red.kept(kind)
-        second_of[kind] = net.add(peer[red.second_peer(kind)], [(og.at[n, away], rx.at[n]), (od_in.at[n, away], rxd.at[n])])
-    go_far = net.add(peer["p"], [(fw_in, rz), (fd_in, rzd)])
+        second_of[kind] = net.add(peer[red.second_peer(kind)], [(og_in.at[n, away], rx.at[n]), (od_in.at[n, away], rxd.at[n])])
+    u_me, u_near = red.kept(ME), red.kept(NEAR)
+    go_near = net.add(peer["l"], [(og.at[1], rz.at[1]), (od.at[1], rzd.at[1])])
+    go_halves = net.add(peer["c"], [(total_w.at[1 - c], fw.at[c]), (total_d.at[1 - c], fd.at[c])])
     go_give_0 = net.add(peer["c"], [(send_c.at[0], recv_c.at[0])])
     go_give_1 = net.add(peer["c"], [(send_c.at[1], recv_c.at[1])])
-    go_cross = net.add(peer["l"], [(send_l, recv_l)])
+    halves = [pl.ds(k * ROWS, ROWS) for k in range(2)]
+    go_cross = [net.add(peer["l"], [(send_l.at[half], recv_l.at[half])]) for half in halves]
+
+    def group(yy, xx, pp):
+        return (yy * 2 + xx) * 2 + pp
+
+    def moved(sources, groups, targets, at=0):
+        return [(src.at[one], dst.at[at + k]) for k, one in enumerate(groups) for src, dst in zip(sources, targets)]
+
+    source, working, small = (pq, goq), (work, wgo), (rs, rso)
+    base, across = group(y, x, p), group(y, x, 1 - p)
+    give_y = (group(1 - y, 0, p), group(1 - y, 1, p))
+    give_x = (group(0, 1 - x, 1 - p), group(1, 1 - x, 1 - p))
+    go_own_y = [[net.add(peer["y"], moved((a,), give_y[k : k + 1], (b,), k)) for k in range(2)] for a, b in ((pq, ry), (goq_in, ryo))]
+    go_other_x = [[net.add(peer["x"], moved((a,), give_x[k : k + 1], (b,), k)) for k in range(2)] for a, b in ((pq, ox), (goq_in, oxo))]
+    go_own_x = [net.add(peer["x"], moved(working[k : k + 1], (group(y, 1 - x, p),), small[k : k + 1], 0)) for k in range(2)]
+    go_other_y = [net.add(peer["y"], moved(working[k : k + 1], (group(1 - y, x, 1 - p),), small[k : k + 1], 1)) for k in range(2)]
+    go_across = [net.add(peer["p"], moved(working[k : k + 1], (across,), small[k : k + 1], 2)) for k in range(2)]
+
+    def parts(q):
+        return [(work.at[base, rows_at(q, 32)], rq.at[t]), (wgo.at[base, rows_at(q, 64)], rqo.at[t])]
+
+    go_last_l = net.add(peer["l"], parts(2 * (1 - l) + c))
+    go_last_d = net.add(peer["d"], parts(2 * (1 - l) + 1 - c))
+    go_last_c = net.add(peer["c"], parts(2 * l + 1 - c))
+    go_gain = [net.add(peer[name], [(gs.at[k], gr.at[k])]) for k, name in enumerate(("c", "x", "y", "p", "l"))]
+    home = Return(where, gt, landed, back_send, back_recv)
+
+    def gain_hop(k):
+        net.arrived(go_gain[k])
+        gs[k + 1] = gs[k] + gr[k]
+        if k + 1 < len(AXES):
+            net.start(go_gain[k + 1])
 
     loads = [
         pltpu.make_async_copy(src, dst, load_sem.at[k])
-        for k, (src, dst) in enumerate([(d_in, d_ref), (w_in, w_ref), (n_in, n_ref), (od_in, od), (xs.at[rows_at(t, OWN)], x_ref)])
+        for k, (src, dst) in enumerate(
+            [
+                (d_in, d_ref), (w_in, w_ref), (n_in, n_ref), (goq_in, goq), (xs.at[rows_at(owned(p, l, c), OWN)], x_ref),
+                (og_in.at[0, u_me], og.at[0]), (og_in.at[1, u_near], og.at[1]),
+                (od_in.at[0, u_me], od.at[0]), (od_in.at[1, u_near], od.at[1]),
+                (fw_in, rz.at[0]), (fd_in, rzd.at[0]),
+            ]
+        )
     ]
     for copy in loads:
         copy.start()
-    for copy in own:
-        copy.start()
-    greet(list(peer.values()))
-    net.start(wide_of[ME], wide_of[NEAR], go_far)
+    greet(line_peers(p, l, c) + [peer["x"], peer["y"]])
+    net.start(second_of[NEAR], second_of[ME], *go_own_y[1], *go_other_x[1])
 
     def project(ll, cc, write):
-        part = d_ref[rows_at(2 * ll + cc, OWN), :]
+        part = d_ref[rows_at(owned(p, ll, cc), OWN), :]
 
         def chunk(k, carry):
             cols = rows_at(k, 256)
@@ -1610,6 +1747,27 @@
             keep[k, :, cols] = value
 
         return write
+
+    def add(k, at, left, right, place_at):
+        total = left[at].astype(jnp.float32) + right[place_at].astype(jnp.float32)
+        working[k][at] = total.astype(jnp.bfloat16)
+
+    def first_sums(k):
+        net.arrived(*go_other_x[k])
+        for yy in (0, 1):
+            add(k, group(yy, x, 1 - p), source[k], (ox, oxo)[k], yy)
+        net.start(go_other_y[k])
+        net.arrived(*go_own_y[k])
+        for xx in (0, 1):
+            add(k, group(y, xx, p), source[k], (ry, ryo)[k], xx)
+        net.start(go_own_x[k])
+
+    def second_sums(k):
+        net.arrived(go_other_y[k])
+        add(k, across, working[k], small[k], 1)
+        net.start(go_across[k])
+        net.arrived(go_own_x[k])
+        add(k, base, working[k], small[k], 0)
 
     loads[0].wait()
     loads[1].wait()
@@ -1618,39 +1776,51 @@
     project(1 - l, c, hold(0))
     net.arrived(go_give_0)
     send_l[...] = (keep[0] + recv_c[0].astype(jnp.float32)).astype(jnp.bfloat16)
-    net.start(go_cross)
+    net.start(*go_cross)
+    for copy in loads[2:]:
+        copy.wait()
+
+    def grad_qkv(yy, xx):
+        k = yy * 2 + xx
+        value = dot(n_ref[:, rows_at(k, 256)], d_ref[...], TN).astype(jnp.bfloat16)
+        pq[2 * k] = value[:128]
+        pq[2 * k + 1] = value[128:]
+
+    def start_if(index, groups):
+        for k in range(2):
+
+            @pl.when(index == k)
+            def _():
+                net.start(groups[k])
+
+    def one_chunk(k, carry):
+        yy, xx = jnp.where(k % 2 == 0, 1 - y, y), jnp.where(k < 2, 1 - x, x)
+        grad_qkv(yy, xx)
+
+        @pl.when(k < 2)
+        def _():
+            start_if(yy, go_other_x[0])
+
+        @pl.when(k % 2 == 0)
+        def _():
+            start_if(xx, go_own_y[0])
+
+        return carry
+
+    lax.fori_loop(0, 4, one_chunk, 0)
+    first_sums(1)
     project(l, 1 - c, give(1))
     net.start(go_give_1)
     project(l, c, hold(1))
-    for copy in own:
-        copy.wait()
-    for copy in loads[2:]:
-        copy.wait()
-    for n, kind in enumerate(two):
-        net.arrived(wide_of[kind])
-        for k in range(2):
-
-            def wide(r, carry):
-                rows = rows_at(r, 16)
-                for m in range(2):
-                    total = og[n, k, m, rows, :].astype(jnp.float32) + rb[n, k, m, rows, :].astype(jnp.float32)
-                    og[n, k, m, rows, :] = total.astype(jnp.bfloat16)
-                return carry
-
-            lax.fori_loop(0, 4, wide, 0)
-        net.start(second_of[kind])
-
-    def grad_qkv(k, carry):
-        cols = rows_at(k, 256)
-        pq[cols, :] = dot(n_ref[:, cols], d_ref[...], TN).astype(jnp.bfloat16)
-        return carry
-
-    lax.fori_loop(0, 4, grad_qkv, 0)
-    net.arrived(go_give_1, go_cross)
-
-    dg[...] = jnp.zeros_like(dg)
-
-    def rows_back(k, carry):
+    net.arrived(second_of[NEAR])
+    og[1] = (og[1].astype(jnp.float32) + rx[1].astype(jnp.float32)).astype(jnp.bfloat16)
+    od[1] = (od[1].astype(jnp.float32) + rxd[1].astype(jnp.float32)).astype(jnp.bfloat16)
+    net.start(go_near)
+    second_sums(1)
+    net.arrived(go_give_1)
+    gs[0] = jnp.zeros_like(gs[0])
+
+    def rows_back(k, total):
         rows = rows_at(k, 64)
         value = x_ref[rows, :].astype(jnp.float32)
         grad = keep[1, rows, :] + recv_c[1, rows, :].astype(jnp.float32) + recv_l[rows, :].astype(jnp.float32)
@@ -1659,160 +1829,60 @@
         gained = grad * ga_ref[...]
         back = r * (gained - scaled * jnp.mean(scaled * gained, axis=-1, keepdims=True))
         gt[rows, :] = (dr_ref[rows, :] + back).astype(jnp.bfloat16)
-        dg[...] += jnp.sum((grad * scaled).reshape(-1, 8, MODEL_DIM), axis=0)
-        return carry
-
-    lax.fori_loop(0, 8, rows_back, 0)
-    net.arrived(second_of[NEAR])
-    u = red.kept(NEAR)
-    near_w[...] = (og[1, u].astype(jnp.float32) + rx[1].astype(jnp.float32)).astype(jnp.bfloat16)
-    near_d[...] = (od[1, u].astype(jnp.float32) + rxd[1].astype(jnp.float32)).astype(jnp.bfloat16)
-    net.arrived(second_of[ME], go_far)
-    u = red.kept(ME)
-    me_w[...] = og[0, u].astype(jnp.float32) + rx[0].astype(jnp.float32) + rz[...].astype(jnp.float32)
-    me_d[...] = od[0, u].astype(jnp.float32) + rxd[0].astype(jnp.float32) + rzd[...].astype(jnp.float32)
-    net.sent()
-
-
-def normed_back(d, w, normed, xs, gg, gu, fw, fd, od, d_resid, g_attn):
-    bf16, f32 = jnp.bfloat16, jnp.float32
-    any_spec = pl.BlockSpec(memory_space=pl.ANY)
-    vmem = pl.BlockSpec(memory_space=pltpu.VMEM)
-    copies = 24
-    wide, deep = (2, 64, HALF_FF), (192, 512)
-
-    def vm(a):
-        return pltpu.VMEM(a.shape, a.dtype)
-
-    return pl.pallas_call(
-        normed_kernel,
-        out_shape=(
-            jax.ShapeDtypeStruct((OWN, MODEL_DIM), bf16),
-            jax.ShapeDtypeStruct((8, MODEL_DIM), f32),
-            jax.ShapeDtypeStruct((1024, 1024), bf16),
-            jax.ShapeDtypeStruct(wide, f32),
-            jax.ShapeDtypeStruct(deep, f32),
-            jax.ShapeDtypeStruct(wide, bf16),
-            jax.ShapeDtypeStruct(deep, bf16),
-        ),
-        in_specs=[any_spec] * 9 + [vmem] * 2,
-        out_specs=[vmem] * 7,
-        scratch_shapes=[
-            vm(d), vm(w), vm(normed),
-            pltpu.VMEM((OWN, MODEL_DIM), bf16),
-            pltpu.VMEM((2, OWN, MODEL_DIM), bf16),
-            pltpu.VMEM((2, OWN, MODEL_DIM), bf16),
-            pltpu.VMEM((OWN, MODEL_DIM), bf16),
-            pltpu.VMEM((OWN, MODEL_DIM), bf16),
-            pltpu.VMEM((2, OWN, MODEL_DIM), f32),
-            pltpu.VMEM((2, 2) + wide, bf16),
-            pltpu.VMEM((2, 2) + wide, bf16),
-            pltpu.VMEM((2, 2) + deep, bf16),
-            pltpu.VMEM((2,) + wide, bf16),
-            pltpu.VMEM((2,) + deep, bf16),
-            pltpu.VMEM(wide, bf16),
-            pltpu.VMEM(deep, bf16),
-            pltpu.SemaphoreType.DMA((copies,)),
-            pltpu.SemaphoreType.DMA((copies,)),
-            pltpu.SemaphoreType.DMA((6,)),
-            pltpu.SemaphoreType.DMA((8,)),
-        ],
-        compiler_params=pltpu.CompilerParams(
-            collective_id=5, has_side_effects=True, vmem_limit_bytes=58 * 1024 * 1024
-        ),
-        name="normed_back",
-    )(d, w, normed, xs, gg, gu, fw, fd, od, d_resid, g_attn)
-
-
-def back_kernel(
-    pq, go, gp, near_w, near_d, me_w, me_d, gt,
-    out_query, out_key, out_value, out_out, out_gate, out_up, out_down, gout, tokens,
-    work, wgo, wgp, ry, ryo, ryg, ox, oxo, oxg, rs, rso, rsg, rq, rqo, rqg,
-    zw, zd, total_w, total_d, fw, fd, landed,
-    send_sem, recv_sem, back_send, back_recv,
-):
-    where = place()
-    y, x, p, l, c = where
-    peer = peers_of(x, y, p, l, c)
-    net = Plan(send_sem, recv_sem)
-    me = 2 * l + c
-    home = Return(where, gt, landed, back_send, back_recv)
-
-    def group(yy, xx, pp):
-        return (yy * 2 + xx) * 2 + pp
-
-    def moved(sources, groups, targets, at=0):
-        return [
-            (src.at[one], dst.at[at + k])
-            for k, one in enumerate(groups)
-            for src, dst in zip(sources, targets)
-        ]
-
-    source, working, small = (pq, go, gp), (work, wgo, wgp), (rs, rso, rsg)
-    go_own_y = net.add(peer["y"], moved(source, (group(1 - y, 0, p), group(1 - y, 1, p)), (ry, ryo, ryg)))
-    go_other_x = net.add(peer["x"], moved(source, (group(0, 1 - x, 1 - p), group(1, 1 - x, 1 - p)), (ox, oxo, oxg)))
-    go_own_x = net.add(peer["x"], moved(working, (group(y, 1 - x, p),), small, 0))
-    go_other_y = net.add(peer["y"], moved(working, (group(1 - y, x, 1 - p),), small, 1))
-    go_across = net.add(peer["p"], moved(working, (group(y, x, 1 - p),), small, 2))
-    base = group(y, x, p)
-
-    def parts(q):
-        return [
-            (work.at[base, rows_at(q, 32)], rq.at[me]),
-            (wgo.at[base, rows_at(q, 64)], rqo.at[me]),
-            (wgp.at[base, q], rqg.at[me]),
-        ]
-
-    go_last_l = net.add(peer["l"], parts(2 * (1 - l) + c))
-    go_last_d = net.add(peer["d"], parts(2 * (1 - l) + 1 - c))
-    go_last_c = net.add(peer["c"], parts(2 * l + 1 - c))
-    go_near = net.add(peer["l"], [(near_w, zw), (near_d, zd)])
-    go_halves = net.add(peer["c"], [(total_w.at[1 - c], fw.at[c]), (total_d.at[1 - c], fd.at[c])])
-    greet(line_peers(p, l, c) + [peer["x"], peer["y"]])
-    net.start(go_own_y, go_other_x, go_near)
-    home.start()
-
-    def add(at, left, right, place_at):
-        for target, a, b in zip(working, left, right):
-            total = a[at].astype(jnp.float32) + b[place_at].astype(jnp.float32)
-            target[at] = total.astype(target.dtype)
-
-    net.arrived(go_own_y)
-    for xx in (0, 1):
-        add(group(y, xx, p), source, (ry, ryo, ryg), xx)
-    net.start(go_own_x)
-    net.arrived(go_other_x)
-    for yy in (0, 1):
-        add(group(yy, x, 1 - p), source, (ox, oxo, oxg), yy)
-    net.start(go_other_y)
+        return total + jnp.sum(grad * scaled, axis=0, keepdims=True)
+
+    d_attn = jnp.zeros((1, MODEL_DIM), jnp.float32)
+    for k in range(2):
+        net.arrived(go_cross[k])
+        d_attn = lax.fori_loop(4 * k, 4 * k + 4, rows_back, d_attn)
+        home.start_one(k)
+        if k == 0:
+            first_sums(0)
+    d_mlp = jnp.sum(dgm_ref[...], axis=0, keepdims=True)
+    for k in range(8):
+        lanes = slice(k * 128, (k + 1) * 128)
+        gs[0, k : k + 1, :] = d_attn[:, lanes]
+        gs[0, 8 + k : 9 + k, :] = d_mlp[:, lanes]
+    for k in range(2):
+        gs[0, 16 + k : 17 + k, :] = jnp.sum(dgh_ref[k], axis=0, keepdims=True)
+    net.start(go_gain[0])
+    second_sums(0)
+    gain_hop(0)
+    net.arrived(second_of[ME])
+    gain_hop(1)
     net.arrived(go_near)
     for cc in range(2):
         rows = pl.ds(32 * cc, 32)
-        total_w[cc] = me_w[:, rows, :] + zw[:, rows, :].astype(jnp.float32)
+        total_w[cc] = (
+            og[0, :, rows, :].astype(jnp.float32) + rx[0, :, rows, :].astype(jnp.float32)
+            + rz[0, :, rows, :].astype(jnp.float32) + rz[1, :, rows, :].astype(jnp.float32)
+        )
         rows = pl.ds(96 * cc, 96)
-        total_d[cc] = me_d[rows, :] + zd[rows, :].astype(jnp.float32)
+        total_d[cc] = (
+            od[0, rows, :].astype(jnp.float32) + rxd[0, rows, :].astype(jnp.float32)
+            + rzd[0, rows, :].astype(jnp.float32) + rzd[1, rows, :].astype(jnp.float32)
+        )
     net.start(go_halves)
-    net.arrived(go_other_y)
-    add(group(y, x, 1 - p), working, small, 1)
-    net.start(go_across)
-    net.arrived(go_own_x)
-    add(base, working, small, 0)
     fw[c] = total_w[c]
     fd[c] = total_d[c]
+    gain_hop(2)
     net.arrived(go_halves)
     for half in range(2):
         cols = slice(half * HALF_FF, (half + 1) * HALF_FF)
         out_gate[:, cols] = fw[half, 0]
         out_up[:, cols] = fw[half, 1]
         out_down[:, half * 512 : (half + 1) * 512] = fd[half]
-    net.arrived(go_across)
-    add(base, working, small, 2)
+    for k in (1, 0):
+        net.arrived(go_across[k])
+        add(k, base, working[k], small[k], 2)
     net.start(go_last_l, go_last_d, go_last_c)
-    rq[me] = work[base, rows_at(me, 32), :]
-    rqo[me] = wgo[base, rows_at(me, 64), :]
-    rqg[me] = wgp[base, me]
+    rq[t] = work[base, rows_at(t, 32), :]
+    rqo[t] = wgo[base, rows_at(t, 64), :]
+    gain_hop(3)
     home.wait()
     tokens[...] = landed[...].astype(jnp.float32)
+    gain_hop(4)
+    gout[...] = gs[len(AXES)]
     net.arrived(go_last_l, go_last_d, go_last_c)
     for q in range(4):
         value = rq[q].astype(jnp.float32)
@@ -1820,25 +1890,27 @@
         out_key[:, 256 * q : 256 * (q + 1)] = value[:, 512:768]
         out_value[:, 256 * q : 256 * (q + 1)] = value[:, 768:]
         out_out[:, 256 * q : 256 * (q + 1)] = rqo[q].astype(jnp.float32)
-    gout[...] = rqg[0] + rqg[1] + rqg[2] + rqg[3]
     net.sent()
 
 
-def back(pq, goq, gp, near_w, near_d, me_w, me_d, gt):
+def tail(d, w, normed, xs, og, od, fw, fd, goq, d_resid, g_attn, d_g_mlp, d_g_heads):
     bf16, f32 = jnp.bfloat16, jnp.float32
+    any_spec = pl.BlockSpec(memory_space=pl.ANY)
     vmem = pl.BlockSpec(memory_space=pltpu.VMEM)
-    copies = 40
-
-    def three(*lead):
-        return [
-            pltpu.VMEM(lead + (128, 1024), bf16),
-            pltpu.VMEM(lead + (256, 256), bf16),
-            pltpu.VMEM(lead + (4, 8, 128), f32),
-        ]
-
+    copies = 48
     wide, deep = (2, 64, HALF_FF), (192, 512)
+    own = (OWN, MODEL_DIM)
+    big, tall = (128, 1024), (256, 256)
+
+    def vm(a):
+        return pltpu.VMEM(a.shape, a.dtype)
+
+    def low(*shape):
+        return pltpu.VMEM(shape, bf16)
+
+    goq = goq.reshape(8, 256, 256)
     return pl.pallas_call(
-        back_kernel,
+        tail_kernel,
         out_shape=(
             jax.ShapeDtypeStruct((32, 2048), f32),
             jax.ShapeDtypeStruct((32, 1024), f32),
@@ -1847,33 +1919,35 @@
             jax.ShapeDtypeStruct((32, FF), f32),
             jax.ShapeDtypeStruct((32, FF), f32),
             jax.ShapeDtypeStruct((96, 1024), f32),
-            jax.ShapeDtypeStruct((8, 128), f32),
+            jax.ShapeDtypeStruct((24, 128), f32),
             jax.ShapeDtypeStruct((2, ROWS, MODEL_DIM), f32),
         ),
-        in_specs=[vmem] * 8,
+        in_specs=[any_spec] * 9 + [vmem] * 4,
         out_specs=[vmem] * 9,
-        scratch_shapes=three(8) + three(2) + three(2) + three(3)
-        + [
-            pltpu.VMEM((4, 32, 1024), bf16),
-            pltpu.VMEM((4, 64, 256), bf16),
-            pltpu.VMEM((4, 8, 128), f32),
-            pltpu.VMEM(wide, bf16),
-            pltpu.VMEM(deep, bf16),
-            pltpu.VMEM((2, 2, 32, HALF_FF), f32),
-            pltpu.VMEM((2, 96, 512), f32),
-            pltpu.VMEM((2, 2, 32, HALF_FF), f32),
-            pltpu.VMEM((2, 96, 512), f32),
-            pltpu.VMEM((2, ROWS, MODEL_DIM), bf16),
+        scratch_shapes=[
+            vm(d), vm(w), vm(normed), low(*own), vm(goq),
+            low(2, *own), low(2, *own), low(*own), low(*own),
+            pltpu.VMEM((2,) + own, f32),
+            low(*own), low(2, ROWS, MODEL_DIM),
+            low(2, *wide), low(2, *deep),
+            low(2, *wide), low(2, *deep), low(2, *wide), low(2, *deep),
+            pltpu.VMEM((2, 2, 32, HALF_FF), f32), pltpu.VMEM((2, 96, 512), f32),
+            pltpu.VMEM((2, 2, 32, HALF_FF), f32), pltpu.VMEM((2, 96, 512), f32),
+            low(8, *big), low(8, *big), low(8, *tall),
+            low(2, *big), low(2, *tall), low(2, *big), low(2, *tall), low(3, *big), low(3, *tall),
+            low(4, 32, 1024), low(4, 64, 256),
+            pltpu.VMEM((6, 24, 128), f32), pltpu.VMEM((5, 24, 128), f32),
             pltpu.SemaphoreType.DMA((copies,)),
             pltpu.SemaphoreType.DMA((copies,)),
+            pltpu.SemaphoreType.DMA((11,)),
             pltpu.SemaphoreType.DMA((2,)),
             pltpu.SemaphoreType.DMA((2,)),
         ],
         compiler_params=pltpu.CompilerParams(
-            collective_id=1, has_side_effects=True, vmem_limit_bytes=58 * 1024 * 1024
+            collective_id=5, has_side_effects=True, vmem_limit_bytes=60 * 1024 * 1024
         ),
-        name="back_reduce",
-    )(pq.reshape(8, 128, 1024), goq.reshape(8, 256, 256), gp.reshape(8, 4, 8, 128), near_w, near_d, me_w, me_d, gt)
+        name="tail_reduce",
+    )(d, w, normed, xs, og, od, fw, fd, goq, d_resid, g_attn, d_g_mlp, d_g_heads)
 
 
 def pick(value, index):
@@ -1901,20 +1975,19 @@
     normed, q, k, v, q_raw, k_raw, attn, lse, wo, wgu, wdn = attend(
         flags, xs, w_qkv, g_attn, g_q, g_k, cosine, sine, woq, wgu, wdn
     )
-    resid, mlp_in, wgu, wdn, wdx, wdo, dy = finish_resid(attn, wo, g_mlp, xs, cotangent, wgu, wdn)
-    grad_gate, grad_up, grad_down, d_resid, d_branch, result, d_g_mlp = feed_forward(
-        mlp_in.reshape(1024, MODEL_DIM), dy.reshape(1024, MODEL_DIM), wgu, wdo, wdx, resid, g_mlp
-    )
-    d_qkv, goq, fw, fd, od, output, d_g_heads = attend_back(
-        flags, q, k, v, attn, d_branch, wo, lse, q_raw, k_raw, cosine, sine, grad_gate, grad_up, grad_down, result, g_q, g_k
-    )
-    gt, d_g_attn, pq, me_w, me_d, near_w, near_d = normed_back(
-        d_qkv, w_qkv, normed, xs, grad_gate, grad_up, fw, fd, od, d_resid, g_attn
-    )
-    d_gains = jnp.concatenate([jnp.sum(d_g_attn, axis=0), jnp.sum(d_g_mlp, axis=0), jnp.sum(d_g_heads, axis=1).reshape(256)])
-    gp = jnp.pad(d_gains.reshape(32, 72), ((0, 0), (0, 952))).reshape(32, 8, 128)
-    *grads, gains_sum, grad_tokens = back(pq, goq, gp, near_w, near_d, me_w, me_d, gt)
-    return (output, grad_tokens, *grads, gains_sum.reshape(1024)[:72])
+    resid, mlp_in, wgu, wdn, wdx, dy = finish_resid(attn, wo, g_mlp, xs, cotangent, wgu, wdn)
+    ggu, gdb, rb, d_resid, d_branch, result, d_g_mlp = feed_forward(
+        mlp_in.reshape(1024, MODEL_DIM), dy.reshape(1024, MODEL_DIM), wgu, wdn, wdx, resid, g_mlp
+    )
+    d_qkv, goq, og, od, fw, fd, output, d_g_heads = attend_back(
+        flags, q, k, v, attn, d_branch, wo, lse, q_raw, k_raw, cosine, sine, ggu, gdb, rb, result, g_q, g_k
+    )
+    *grads, gains_sum, grad_tokens = tail(
+        d_qkv, w_qkv, normed, xs, og, od, fw, fd, goq, d_resid, g_attn, d_g_mlp, d_g_heads
+    )
+    device = lax.axis_index(AXES)
+    out_gains = lax.dynamic_slice(gains_sum.reshape(3072), (device * 72,), (72,))
+    return (output, grad_tokens, *grads, out_gains)
 
 
 def fast_solution(mesh):

time: 460 us -> 409 us (0.89)
  Pallas kernels: 439 us -> 387 us
    pallas_call x1, Pallas kernels: 97.4 us -> 71.8 us  [front(): pl.pallas_call(front_kernel, out_shape=(jax.ShapeDtypeStruct((8, ROWS, MO...]
    pallas_call x2 -> x1, Pallas kernels: 111 us -> 86 us  [tail(): pl.pallas_call(tail_kernel, out_shape=(jax.ShapeDtypeStruct((32, 2048), f...]
    pallas_call x1, Pallas kernels: 53.2 us -> 48.3 us  [finish_resid(): pl.pallas_call(resid_kernel, out_shape=(jax.ShapeDtypeStruct((OWN, MODEL_...]
    unnamed x66 -> x60, local copies, waits for them, and re-layouts: 15.3 us -> 16.5 us
where the time goes in v3:
time: 409 us; the launch traced here: 408 us
  Pallas kernels  387 us (95%)
  local copies, waits for them, and re-layouts  18.6 us (5%)
    pallas_call x1, Pallas kernels, attend_back(): pl.pallas_call(attend_back_kernel, out_shape=(jax.ShapeDtypeStruct((SEQ_R...  86.3 us
    pallas_call x1, Pallas kernels, tail(): pl.pallas_call(tail_kernel, out_shape=(jax.ShapeDtypeStruct((32, 2048), f...  86 us
    pallas_call x1, Pallas kernels, front(): pl.pallas_call(front_kernel, out_shape=(jax.ShapeDtypeStruct((8, ROWS, MO...  71.8 us
    pallas_call x1, Pallas kernels, attend(): pl.pallas_call(attend_kernel, out_shape=(jax.ShapeDtypeStruct((SEQ_ROWS,...  50.1 us
    pallas_call x1, Pallas kernels, finish_resid(): pl.pallas_call(resid_kernel, out_shape=(jax.ShapeDtypeStruct((OWN, MODEL_...  48.3 us
    pallas_call x1, Pallas kernels, feed_forward(): pl.pallas_call(forward_kernel, grid=(HALF_FF // CHUNK,), out_shape=(jax.S...  44.8 us
    unnamed x60, local copies, waits for them, and re-layouts  16.5 us

profile of v3, /device:TPU:0, one launch (start us, length us, event | category | flops | bytes accessed | tf_op | source)
XLA Modules:
  0.0 408.2 jit_solution(10895891704147991985)
XLA Ops:
  0.6 0.0 copy-start
  0.7 0.7 copy-done
  1.3 0.1 compare_reduce_fusion
  1.4 0.0 copy-start.12
  1.5 0.1 pad_maximum_fusion
  1.5 0.6 broadcast_in_dim.20.inverse
  2.1 1.2 bitcast_convert_fusion.gn
  3.4 71.8 %front_gather.1 = (bf16[8,256,1024]{2,1,0:T(8,128)(2,1)}, bf16[1024,1024]{1,0:T(8,128)(2,1)}, bf16[2048,256]{1,0:T(8,128)(2,1)}, f32[32,8,128]{2,1,0:T(8,128)}, ...) custom-call(bf16[2,256,1024]{2,1,0:T(8,128)(2,1)} %tok.1, ...), custom_call_target="tpu_custom_call" | custom-call | tf_op jit(solution)/shard_map/front_gather/pallas_call | solution.py:615
  75.1 0.9 copy.27
  76.1 0.1 reshape.55
  76.2 0.0 copy-start.8
  76.2 0.0 copy-start.9
  76.2 0.0 copy-start.7
  76.2 0.0 copy-start.6
  76.2 0.0 copy-start.10
  76.3 1.2 copy-done.10
  77.5 0.0 copy-start.11
  77.5 1.2 copy-done.11
  78.7 0.0 copy-start.4
  78.7 50.1 %attend.1 = (bf16[2048,1024]{1,0:T(8,128)(2,1)}, bf16[4,2048,128]{2,1,0:T(8,128)(2,1)}, bf16[2,2048,128]{2,1,0:T(8,128)(2,1)S(1)}, bf16[2,2048,128]{2,1,0:T(8,12...) custom-call(s32[8]{0:T(128)S(1)} %convert_element_type.6.flags, ...), custom_call_target="tpu_custom_call", output_to_operand_aliasing={{9}: (9, {}), {10}: (10, {})} | custom-call | flops 8589934592 | bytes 25165824 | tf_op jit(solution)/shard_map/attend/pallas_call | solution.py:930
  128.8 0.0 copy-done.12
  128.8 0.0 copy-done.8
  128.8 0.0 copy-done.9
  128.8 0.0 copy-done.7
  128.8 0.0 copy-start.13
  128.8 1.0 copy-done.13
  129.8 0.0 copy-start.14
  129.8 1.0 copy-done.14
  130.8 0.7 copy-done.15
  131.5 0.0 copy-done.6
  131.5 0.0 copy-done.4
  131.5 48.3 %residual.1 = (f32[512,1024]{1,0:T(8,128)S(1)}, bf16[2,512,1024]{2,1,0:T(8,128)(2,1)}, bf16[2,1024,1536]{2,1,0:T(8,128)(2,1)}, bf16[3072,512]{1,0:T(8,128)(2,1)}...) custom-call(bf16[2048,512]{1,0:T(8,128)(2,1)} %get-tuple-element.70., ...), custom_call_target="tpu_custom_call", output_to_operand_aliasing={{2}: (5, {}), {3}: (6, {})} | custom-call | tf_op jit(solution)/shard_map/residual/pallas_call | solution.py:1085
  179.8 0.0 copy-done.5
  179.8 0.0 copy-start.2
  179.8 1.3 copy-done.2
  181.1 1.2 copy-done.3
  182.3 44.8 %feed_forward.1 = (bf16[2,1024,1536]{2,1,0:T(8,128)(2,1)}, bf16[2,1536,512]{2,1,0:T(8,128)(2,1)}, bf16[4,2,2,64,1024]{4,3,2,1,0:T(8,128)(2,1)}, f32[512,1024]{1,...) custom-call(bf16[1024,1024]{1,0:T(8,128)(2,1)} %bitcast.27, ...), custom_call_target="tpu_custom_call" | custom-call | tf_op jit(solution)/shard_map/feed_forward/pallas_call | solution.py:1256
  227.1 86.3 %attend_back.1 = (bf16[2048,1024]{1,0:T(8,128)(2,1)}, bf16[2048,256]{1,0:T(8,128)(2,1)}, bf16[2,2,2,64,1536]{4,3,2,1,0:T(8,128)(2,1)}, bf16[2,2,192,512]{3,2,1,0...) custom-call(s32[8]{0:T(128)} %copy-done.12, ...), custom_call_target="tpu_custom_call" | custom-call | flops 21474836480 | bytes 41943040 | tf_op jit(solution)/shard_map/attend_back/pallas_call | solution.py:1602
  313.4 0.0 copy-start.17
  313.4 86.0 %tail_reduce.1 = (f32[32,2048]{1,0:T(8,128)}, f32[32,1024]{1,0:T(8,128)}, f32[32,1024]{1,0:T(8,128)}, f32[64,1024]{1,0:T(8,128)}, f32[32,3072]{1,0:T(8,128)}, /*...) custom-call(bf16[2048,1024]{1,0:T(8,128)(2,1)} %get-tuple-element.89.d_in, ...), custom_call_target="tpu_custom_call" | custom-call | tf_op jit(solution)/shard_map/tail_reduce/pallas_call | solution.py:1912
  399.4 0.0 copy-start.16
  399.4 1.4 dynamic_slice.8
  400.8 0.0 copy-done.17
  400.8 1.0 copy.41
  401.8 0.0 copy-done.16
  401.8 0.0 copy-start.21
  401.8 0.0 copy-start.20
  401.8 0.0 copy-start.1
  401.9 1.3 copy.42
  403.2 0.0 copy-done.22
  403.2 0.7 copy.43
  403.9 0.0 copy-done.24
  403.9 0.7 copy.44
  404.5 0.0 copy-done.23
  404.6 0.7 copy.45
  405.2 0.0 copy-done.21
  405.2 0.7 copy.46
  405.9 0.0 copy-done.20
  405.9 0.7 copy.47
  406.7 0.0 copy-done.19
  406.7 0.7 copy.48
  407.4 0.0 copy-done.18
  407.4 0.7 copy.49
  408.2 0.0 copy-done.1
  (15 shorter events, 0.0 us)
Async XLA Ops:
  0.6 0.7 copy-start
  1.4 127.4 %copy-start.12 = (s32[8]{0:T(128)}, s32[8]{0:T(128)S(1)}, u32[]{:S(2)}) copy-start(s32[8]{0:T(128)S(1)} %convert_element_type.6.flags) | copy-start | bytes 100
  76.2 52.6 %copy-start.8 = (f32[1,128]{1,0:T(1,128)}, f32[1,128]{1,0:T(1,128)S(1)}, u32[]{:S(2)}) copy-start(f32[1,128]{1,0:T(1,128)S(1)} %get-tuple-element.110.gk_ref) | copy-start | bytes 1540
  76.2 52.6 %copy-start.9 = (f32[1,128]{1,0:T(1,128)}, f32[1,128]{1,0:T(1,128)S(1)}, u32[]{:S(2)}) copy-start(f32[1,128]{1,0:T(1,128)S(1)} %get-tuple-element.111.gq_ref) | copy-start | bytes 1540
  76.2 52.6 %copy-start.7 = (f32[1024]{0:T(1024)}, f32[1024]{0:T(1024)S(1)}, u32[]{:S(2)}) copy-start(f32[1024]{0:T(1024)S(1)} %get-tuple-element.109) | copy-start | bytes 12292
  76.2 55.3 %copy-start.6 = (f32[1024]{0:T(1024)}, f32[1024]{0:T(1024)S(1)}, u32[]{:S(2)}) copy-start(f32[1024]{0:T(1024)S(1)} %get-tuple-element.108) | copy-start | bytes 12292
  76.2 1.2 copy-start.10
  77.5 1.2 copy-start.11
  78.7 52.8 %copy-start.4 = (bf16[2,256,1024]{2,1,0:T(8,128)(2,1)S(1)}, bf16[2,256,1024]{2,1,0:T(8,128)(2,1)}, u32[]{:S(2)}) copy-start(bf16[2,256,1024]{2,1,0:T(8,128)(2,1)} %cot.1) | copy-start | bytes 3145732
  128.8 1.0 copy-start.13
  129.8 1.0 copy-start.14
  130.8 0.7 copy-start.15
  131.5 48.3 %copy-start.5 = (bf16[512,1024]{1,0:T(8,128)(2,1)}, bf16[512,1024]{1,0:T(8,128)(2,1)S(1)}, u32[]{:S(2)}) copy-start(bf16[512,1024]{1,0:T(8,128)(2,1)S(1)} %get-tuple-element.71.wo.wo_in) | copy-start | bytes 3145732
  179.8 1.3 copy-start.2
  181.1 1.2 copy-start.3
  313.4 87.4 %copy-start.17 = (bf16[2,256,1024]{2,1,0:T(8,128)(2,1)S(1)}, bf16[2,256,1024]{2,1,0:T(8,128)(2,1)}, u32[]{:S(2)}) copy-start(bf16[2,256,1024]{2,1,0:T(8,128)(2,1)} %get-tuple-element.122) | copy-start | bytes 3145732
  399.4 2.4 copy-start.16
  401.8 1.4 copy-start.22
  401.8 2.1 copy-start.24
  401.8 2.7 copy-start.23
  401.8 3.4 copy-start.21
  401.8 4.1 copy-start.20
  401.8 6.3 %copy-start.1 = (s32[2,4]{1,0:T(2,128)S(1)}, s32[2,4]{1,0:T(2,128)}, u32[]{:S(2)}) copy-start(s32[2,4]{1,0:T(2,128)} %param.13) | copy-start | bytes 100
  403.2 3.5 copy-start.19
  403.2 4.2 %copy-start.18 = (f32[96,1024]{1,0:T(8,128)S(1)}, f32[96,1024]{1,0:T(8,128)}, u32[]{:S(2)}) copy-start(f32[96,1024]{1,0:T(8,128)} %get-tuple-element.130) | copy-start | bytes 1179652

commit v4 on v3

--- a/solution.py
+++ b/solution.py
@@ -412,6 +412,7 @@
 MESH = pl.DeviceIdType.MESH
 SCALE = 1.0 / math.sqrt(HEAD_DIM)
 LOG2E = 1.4426950408889634
+VMEM_LIMIT = 62 * 1024 * 1024
 NT = (((1,), (1,)), ((), ()))
 TN = (((0,), (0,)), ((), ()))
 
@@ -641,7 +642,9 @@
             pltpu.VMEM((96, 512), bf16),
             pltpu.VMEM((ROWS, MODEL_DIM), bf16),
         ],
-        compiler_params=pltpu.CompilerParams(collective_id=0, has_side_effects=True),
+        compiler_params=pltpu.CompilerParams(
+            collective_id=0, has_side_effects=True, vmem_limit_bytes=VMEM_LIMIT
+        ),
         name="front_gather",
     )(tok, wq, wk, wv, wo, gn, wg, wu, wd, inverse)
 
@@ -964,7 +967,7 @@
         ),
         input_output_aliases={9: 9, 10: 10},
         compiler_params=pltpu.CompilerParams(
-            collective_id=2, has_side_effects=True, vmem_limit_bytes=48 * 1024 * 1024
+            collective_id=2, has_side_effects=True, vmem_limit_bytes=VMEM_LIMIT
         ),
         cost_estimate=pl.CostEstimate(
             flops=4 * QH * SEQ_ROWS * SEQ_ROWS * HEAD_DIM, bytes_accessed=24 << 20, transcendentals=QH * SEQ_ROWS * SEQ_ROWS
@@ -1006,10 +1009,11 @@
     go_down_near = net.add(peer["c"], down(p, 1 - l))
     go_down_far = net.add(peer["c"], down(1 - p, l))
     go_down_fal = net.add(peer["c"], down(1 - p, 1 - l))
-    go_give_0 = net.add(peer["c"], [(send_c.at[0], recv_c.at[0])])
+    halves = [pl.ds(n * ROWS, ROWS) for n in range(2)]
+    go_give_0 = [net.add(peer["c"], [(send_c.at[0, half], recv_c.at[0, half])]) for half in halves]
     go_give_1 = net.add(peer["c"], [(send_c.at[1], recv_c.at[1])])
-    go_cross = net.add(peer["l"], [(send_l, recv_l)])
-    go_share = net.add(peer["c"], in_place(mlp_in.at[c]))
+    go_cross = [net.add(peer["l"], [(send_l.at[half], recv_l.at[half])]) for half in halves]
+    go_share = [net.add(peer["c"], in_place(mlp_in.at[c, half])) for half in halves]
     go_dy_c = net.add(peer["c"], in_place(dy.at[c]))
     spread = Spread(where, cot, dy, dy_send, dy_recv)
     greet(line_peers(p, l, c) + [peer["x"], peer["y"]])
@@ -1018,25 +1022,25 @@
     fetch = pltpu.make_async_copy(xs.at[rows_at(owned(p, l, c), OWN)], x_own, local_sem.at[0])
     fetch.start()
 
-    def project(ll, cc, write):
-        part = attn[rows_at(owned(p, ll, cc), OWN), :]
-
-        def chunk(k, carry):
-            cols = rows_at(k, 256)
-            write(cols, dot(part, wo[:, cols]))
+    def project(ll, cc, write, first=0, count=OWN):
+        part = attn[pl.ds(pl.multiple_of(owned(p, ll, cc) * OWN + first, ROWS), count), :]
+
+        def chunk(n, carry):
+            cols = rows_at(n, 256)
+            write(pl.ds(first, count), cols, dot(part, wo[:, cols]))
             return carry
 
         lax.fori_loop(0, 4, chunk, 0)
 
-    def give(k):
-        def write(cols, value):
-            send_c[k, :, cols] = value.astype(jnp.bfloat16)
+    def give(n):
+        def write(rows, cols, value):
+            send_c[n, rows, cols] = value.astype(jnp.bfloat16)
 
         return write
 
-    def hold(k):
-        def write(cols, value):
-            keep[k, :, cols] = value
+    def hold(n):
+        def write(rows, cols, value):
+            keep[n, rows, cols] = value
 
         return write
 
@@ -1046,12 +1050,13 @@
         net.arrived(go_fal_y[k])
         net.start(go_fal_x[k])
 
-    project(1 - l, 1 - c, give(0))
-    net.start(go_give_0)
-    project(1 - l, c, hold(0))
-    net.arrived(go_give_0)
-    send_l[...] = (keep[0] + recv_c[0].astype(jnp.float32)).astype(jnp.bfloat16)
-    net.start(go_cross)
+    for n, half in enumerate(halves):
+        project(1 - l, 1 - c, give(0), n * ROWS, ROWS)
+        net.start(go_give_0[n])
+        project(1 - l, c, hold(0), n * ROWS, ROWS)
+        net.arrived(go_give_0[n])
+        send_l[half, :] = (keep[0, half, :] + recv_c[0, half, :].astype(jnp.float32)).astype(jnp.bfloat16)
+        net.start(go_cross[n])
     relay_hop(1)
     project(l, 1 - c, give(1))
     net.start(go_give_1)
@@ -1060,12 +1065,13 @@
     relay_hop(0)
     net.arrived(go_give_1)
     keep[1] += recv_c[1].astype(jnp.float32) + x_own[...].astype(jnp.float32)
-    net.arrived(go_cross)
-    total = keep[1] + recv_l[...].astype(jnp.float32)
-    resid[...] = total
-    r = lax.rsqrt(jnp.mean(total * total, axis=-1, keepdims=True) + EPS)
-    mlp_in[c] = (total * r * g_mlp[...]).astype(jnp.bfloat16)
-    net.start(go_share)
+    for n, half in enumerate(halves):
+        net.arrived(go_cross[n])
+        total = keep[1, half, :] + recv_l[half, :].astype(jnp.float32)
+        resid[half, :] = total
+        r = lax.rsqrt(jnp.mean(total * total, axis=-1, keepdims=True) + EPS)
+        mlp_in[c, half, :] = (total * r * g_mlp[...]).astype(jnp.bfloat16)
+        net.start(go_share[n])
     net.arrived(go_far_y[1])
     net.start(go_down_far)
     spread.wait()
@@ -1073,7 +1079,7 @@
     net.arrived(go_fal_x[1])
     net.start(go_down_fal)
     net.arrived(go_far_y[0], go_fal_x[0])
-    net.arrived(go_down_me, go_down_near, go_down_far, go_down_fal, go_share, go_dy_c)
+    net.arrived(go_down_me, go_down_near, go_down_far, go_down_fal, *go_share, go_dy_c)
     net.sent()
 
 
@@ -1109,7 +1115,7 @@
         ],
         input_output_aliases={5: 2, 6: 3},
         compiler_params=pltpu.CompilerParams(
-            collective_id=3, has_side_effects=True, vmem_limit_bytes=48 * 1024 * 1024
+            collective_id=3, has_side_effects=True, vmem_limit_bytes=VMEM_LIMIT
         ),
         name="residual",
     )(attn, wo, g_mlp, xs, cot, wgu, wdn)
@@ -1289,7 +1295,7 @@
             pltpu.SemaphoreType.DMA((6,)),
         ],
         compiler_params=pltpu.CompilerParams(
-            collective_id=6, has_side_effects=True, vmem_limit_bytes=60 * 1024 * 1024
+            collective_id=6, has_side_effects=True, vmem_limit_bytes=VMEM_LIMIT
         ),
         name="feed_forward",
     )(mlp_in, dy, wgu, wdn, wdx, resid, g_mlp)
@@ -1460,7 +1466,7 @@
         for copy in loads[3:]:
             copy.wait()
 
-    @pl.when(step == 1)
+    @pl.when(step == 2)
     def _():
         net.arrived(second_a[FAL])
         plus(og.at[FAL, u_fal, :, :, early], rc.at[1, :, :, early])
@@ -1468,11 +1474,11 @@
         net.arrived(second_a[FAR])
         plus(og.at[FAR, u_far, :, :, early], rc.at[0, :, :, early])
 
-    @pl.when(step == 2)
+    @pl.when(step == 1)
     def _():
         home.start()
 
-    @pl.when(step == 2)
+    @pl.when(step == 3)
     def _():
         for kind in (FAR, FAL):
             net.arrived(first_of[kind])
@@ -1489,13 +1495,13 @@
         net.arrived(go_db_r)
         branch(owned(p, 1 - l, 1 - c))
 
-    @pl.when(step == 3)
+    @pl.when(step == 5)
     def _():
         net.arrived(go_fal_a)
         plus(og.at[FAR, u_far, :, :, early], rz.at[:, :, early])
         net.start(go_far_a)
 
-    @pl.when(step == 4)
+    @pl.when(step == 5)
     def _():
         net.arrived(second_b[FAL])
         plus(og.at[FAL, u_fal, :, :, late], rc.at[1, :, :, late])
@@ -1505,14 +1511,14 @@
         plus(og.at[FAR, u_far, :, :, late], rc.at[0, :, :, late])
         plus(od.at[FAR, u_far], rcd.at[0])
 
-    @pl.when(step == 5)
+    @pl.when(step == 7)
     def _():
         net.arrived(go_fal_b)
         plus(og.at[FAR, u_far, :, :, late], rz.at[:, :, late])
         plus(od.at[FAR, u_far], rzd)
         net.start(go_far_b)
 
-    @pl.when(step == 3 * KH)
+    @pl.when(step == 5)
     def _():
         def grad_out(k, carry):
             cols = rows_at(k, 256)
@@ -1533,6 +1539,7 @@
     def tile(j, mask=None):
         keys = rows_at(j, BLK)
         k, v = k_ref[g, keys, :], v_ref[g, keys, :]
+        turned = k.T
         dv, dk = None, None
         for n, h in enumerate(heads):
             probs = jnp.exp2(dot(k, queries[n], NT) * (SCALE * LOG2E) - lse_ref[h, 0:1, rows])
@@ -1541,7 +1548,7 @@
             d_scores = (probs * (dot(v, grads[n], NT) - delta[h, 0:1, rows])).astype(jnp.bfloat16)
             dv_more, dk_more = dot(probs.astype(jnp.bfloat16), grads[n]), dot(d_scores, queries[n])
             dv, dk = (dv_more, dk_more) if dv is None else (dv + dv_more, dk + dk_more)
-            dq_acc[n] += dot(d_scores, k, TN)
+            dq_acc[n] += dot(turned, d_scores)
         dv_acc[g, keys, :] += dv
         dk_acc[g, keys, :] += dk
 
@@ -1552,7 +1559,7 @@
     tile(i, block_mask(0, flags, i))
     lax.fori_loop(0, i, loop, 0)
     for n, h in enumerate(heads):
-        low, total = unrope(dq_acc[n], qr_ref[h, rows, :], gq_ref[...], rows)
+        low, total = unrope(dq_acc[n].T, qr_ref[h, rows, :], gq_ref[...], rows)
         dbuf[rows, spans[n]] = low
         dg_ref[0] += total
 
@@ -1622,7 +1629,7 @@
                 pltpu.VMEM((SEQ_ROWS, QH * HEAD_DIM), bf16),
                 pltpu.VMEM((QH, 8, SEQ_ROWS), f32),
                 pltpu.VMEM((SEQ_ROWS, 1024), bf16),
-                pltpu.VMEM((2, BLK, HEAD_DIM), f32),
+                pltpu.VMEM((2, HEAD_DIM, BLK), f32),
                 pltpu.VMEM((KH, SEQ_ROWS, HEAD_DIM), f32),
                 pltpu.VMEM((KH, SEQ_ROWS, HEAD_DIM), f32),
                 pltpu.VMEM((4, 2, 2, 64, HALF_FF), bf16),
@@ -1644,7 +1651,7 @@
             ],
         ),
         compiler_params=pltpu.CompilerParams(
-            collective_id=4, has_side_effects=True, vmem_limit_bytes=60 * 1024 * 1024
+            collective_id=4, has_side_effects=True, vmem_limit_bytes=VMEM_LIMIT
         ),
         cost_estimate=pl.CostEstimate(
             flops=10 * QH * SEQ_ROWS * SEQ_ROWS * HEAD_DIM, bytes_accessed=40 << 20, transcendentals=QH * SEQ_ROWS * SEQ_ROWS
@@ -1655,10 +1662,10 @@
 
 def tail_kernel(
     d_in, w_in, n_in, xs, og_in, od_in, fw_in, fd_in, goq_in, dr_ref, ga_ref, dgm_ref, dgh_ref,
-    out_query, out_key, out_value, out_out, out_gate, out_up, out_down, gout, tokens,
-    d_ref, w_ref, n_ref, x_ref, goq, send_c, recv_c, send_l, recv_l, keep, gt, landed,
-    og, od, rx, rxd, rz, rzd, total_w, total_d, fw, fd,
-    pq, work, wgo, ry, ryo, ox, oxo, rs, rso, rq, rqo, gs, gr,
+    rq, rqo, fw, fd, gout, landed,
+    d_ref, w_ref, n_ref, x_ref, goq, send_c, recv_c, send_l, recv_l, keep, gt,
+    og, od, rx, rxd, rz, rzd, total_w, total_d,
+    pq, work, wgo, ry, ryo, ox, oxo, rs, rso, gs, gr,
     send_sem, recv_sem, load_sem, back_send, back_recv,
 ):
     where = place()
@@ -1776,7 +1783,10 @@
     project(1 - l, c, hold(0))
     net.arrived(go_give_0)
     send_l[...] = (keep[0] + recv_c[0].astype(jnp.float32)).astype(jnp.bfloat16)
-    net.start(*go_cross)
+    net.start(go_cross[0])
+    project(l, 1 - c, give(1))
+    net.start(go_give_1)
+    project(l, c, hold(1))
     for copy in loads[2:]:
         copy.wait()
 
@@ -1807,17 +1817,6 @@
 
         return carry
 
-    lax.fori_loop(0, 4, one_chunk, 0)
-    first_sums(1)
-    project(l, 1 - c, give(1))
-    net.start(go_give_1)
-    project(l, c, hold(1))
-    net.arrived(second_of[NEAR])
-    og[1] = (og[1].astype(jnp.float32) + rx[1].astype(jnp.float32)).astype(jnp.bfloat16)
-    od[1] = (od[1].astype(jnp.float32) + rxd[1].astype(jnp.float32)).astype(jnp.bfloat16)
-    net.start(go_near)
-    second_sums(1)
-    net.arrived(go_give_1)
     gs[0] = jnp.zeros_like(gs[0])
 
     def rows_back(k, total):
@@ -1831,13 +1830,23 @@
         gt[rows, :] = (dr_ref[rows, :] + back).astype(jnp.bfloat16)
         return total + jnp.sum(grad * scaled, axis=0, keepdims=True)
 
-    d_attn = jnp.zeros((1, MODEL_DIM), jnp.float32)
-    for k in range(2):
-        net.arrived(go_cross[k])
-        d_attn = lax.fori_loop(4 * k, 4 * k + 4, rows_back, d_attn)
-        home.start_one(k)
-        if k == 0:
-            first_sums(0)
+    lax.fori_loop(0, 1, one_chunk, 0)
+    net.start(go_cross[1])
+    lax.fori_loop(1, 2, one_chunk, 0)
+    net.arrived(go_give_1, go_cross[0])
+    d_attn = lax.fori_loop(0, 4, rows_back, jnp.zeros((1, MODEL_DIM), jnp.float32))
+    home.start_one(0)
+    lax.fori_loop(2, 4, one_chunk, 0)
+    first_sums(1)
+    net.arrived(go_cross[1])
+    d_attn = lax.fori_loop(4, 8, rows_back, d_attn)
+    home.start_one(1)
+    net.arrived(second_of[NEAR])
+    og[1] = (og[1].astype(jnp.float32) + rx[1].astype(jnp.float32)).astype(jnp.bfloat16)
+    od[1] = (od[1].astype(jnp.float32) + rxd[1].astype(jnp.float32)).astype(jnp.bfloat16)
+    net.start(go_near)
+    first_sums(0)
+    second_sums(1)
     d_mlp = jnp.sum(dgm_ref[...], axis=0, keepdims=True)
     for k in range(8):
         lanes = slice(k * 128, (k + 1) * 128)
@@ -1867,11 +1876,6 @@
     fd[c] = total_d[c]
     gain_hop(2)
     net.arrived(go_halves)
-    for half in range(2):
-        cols = slice(half * HALF_FF, (half + 1) * HALF_FF)
-        out_gate[:, cols] = fw[half, 0]
-        out_up[:, cols] = fw[half, 1]
-        out_down[:, half * 512 : (half + 1) * 512] = fd[half]
     for k in (1, 0):
         net.arrived(go_across[k])
         add(k, base, working[k], small[k], 2)
@@ -1880,17 +1884,52 @@
     rqo[t] = wgo[base, rows_at(t, 64), :]
     gain_hop(3)
     home.wait()
-    tokens[...] = landed[...].astype(jnp.float32)
     gain_hop(4)
     gout[...] = gs[len(AXES)]
     net.arrived(go_last_l, go_last_d, go_last_c)
+    net.sent()
+
+
+def finish_kernel(
+    rq, rqo, fw, fd, landed, result,
+    output, tokens, out_query, out_key, out_value, out_out, out_gate, out_up, out_down,
+):
+    output[...] = result[...]
+    tokens[...] = landed[...].astype(jnp.float32)
+    for half in range(2):
+        cols = slice(half * HALF_FF, (half + 1) * HALF_FF)
+        out_gate[:, cols] = fw[half, 0]
+        out_up[:, cols] = fw[half, 1]
+        out_down[:, half * 512 : (half + 1) * 512] = fd[half]
     for q in range(4):
         value = rq[q].astype(jnp.float32)
         out_query[:, 512 * q : 512 * (q + 1)] = value[:, :512]
         out_key[:, 256 * q : 256 * (q + 1)] = value[:, 512:768]
         out_value[:, 256 * q : 256 * (q + 1)] = value[:, 768:]
         out_out[:, 256 * q : 256 * (q + 1)] = rqo[q].astype(jnp.float32)
-    net.sent()
+
+
+def finish(rq, rqo, fw, fd, landed, result):
+    f32 = jnp.float32
+    vmem = pl.BlockSpec(memory_space=pltpu.VMEM)
+    return pl.pallas_call(
+        finish_kernel,
+        out_shape=(
+            jax.ShapeDtypeStruct((2, ROWS, MODEL_DIM), jnp.bfloat16),
+            jax.ShapeDtypeStruct((2, ROWS, MODEL_DIM), f32),
+            jax.ShapeDtypeStruct((32, 2048), f32),
+            jax.ShapeDtypeStruct((32, 1024), f32),
+            jax.ShapeDtypeStruct((32, 1024), f32),
+            jax.ShapeDtypeStruct((64, 1024), f32),
+            jax.ShapeDtypeStruct((32, FF), f32),
+            jax.ShapeDtypeStruct((32, FF), f32),
+            jax.ShapeDtypeStruct((96, 1024), f32),
+        ),
+        in_specs=[vmem] * 6,
+        out_specs=[vmem] * 9,
+        compiler_params=pltpu.CompilerParams(vmem_limit_bytes=VMEM_LIMIT),
+        name="finish",
+    )(rq, rqo, fw, fd, landed, result)
 
 
 def tail(d, w, normed, xs, og, od, fw, fd, goq, d_resid, g_attn, d_g_mlp, d_g_heads):
@@ -1912,30 +1951,25 @@
     return pl.pallas_call(
         tail_kernel,
         out_shape=(
-            jax.ShapeDtypeStruct((32, 2048), f32),
-            jax.ShapeDtypeStruct((32, 1024), f32),
-            jax.ShapeDtypeStruct((32, 1024), f32),
-            jax.ShapeDtypeStruct((64, 1024), f32),
-            jax.ShapeDtypeStruct((32, FF), f32),
-            jax.ShapeDtypeStruct((32, FF), f32),
-            jax.ShapeDtypeStruct((96, 1024), f32),
+            jax.ShapeDtypeStruct((4, 32, 1024), bf16),
+            jax.ShapeDtypeStruct((4, 64, 256), bf16),
+            jax.ShapeDtypeStruct((2, 2, 32, HALF_FF), f32),
+            jax.ShapeDtypeStruct((2, 96, 512), f32),
             jax.ShapeDtypeStruct((24, 128), f32),
-            jax.ShapeDtypeStruct((2, ROWS, MODEL_DIM), f32),
+            jax.ShapeDtypeStruct((2, ROWS, MODEL_DIM), bf16),
         ),
         in_specs=[any_spec] * 9 + [vmem] * 4,
-        out_specs=[vmem] * 9,
+        out_specs=[vmem] * 6,
         scratch_shapes=[
             vm(d), vm(w), vm(normed), low(*own), vm(goq),
             low(2, *own), low(2, *own), low(*own), low(*own),
             pltpu.VMEM((2,) + own, f32),
-            low(*own), low(2, ROWS, MODEL_DIM),
+            low(*own),
             low(2, *wide), low(2, *deep),
             low(2, *wide), low(2, *deep), low(2, *wide), low(2, *deep),
             pltpu.VMEM((2, 2, 32, HALF_FF), f32), pltpu.VMEM((2, 96, 512), f32),
-            pltpu.VMEM((2, 2, 32, HALF_FF), f32), pltpu.VMEM((2, 96, 512), f32),
             low(8, *big), low(8, *big), low(8, *tall),
             low(2, *big), low(2, *tall), low(2, *big), low(2, *tall), low(3, *big), low(3, *tall),
-            low(4, 32, 1024), low(4, 64, 256),
             pltpu.VMEM((6, 24, 128), f32), pltpu.VMEM((5, 24, 128), f32),
             pltpu.SemaphoreType.DMA((copies,)),
             pltpu.SemaphoreType.DMA((copies,)),
@@ -1944,7 +1978,7 @@
             pltpu.SemaphoreType.DMA((2,)),
         ],
         compiler_params=pltpu.CompilerParams(
-            collective_id=5, has_side_effects=True, vmem_limit_bytes=60 * 1024 * 1024
+            collective_id=5, has_side_effects=True, vmem_limit_bytes=VMEM_LIMIT
         ),
         name="tail_reduce",
     )(d, w, normed, xs, og, od, fw, fd, goq, d_resid, g_attn, d_g_mlp, d_g_heads)
@@ -1982,12 +2016,12 @@
     d_qkv, goq, og, od, fw, fd, output, d_g_heads = attend_back(
         flags, q, k, v, attn, d_branch, wo, lse, q_raw, k_raw, cosine, sine, ggu, gdb, rb, result, g_q, g_k
     )
-    *grads, gains_sum, grad_tokens = tail(
+    rq, rqo, wide, deep, gains_sum, landed = tail(
         d_qkv, w_qkv, normed, xs, og, od, fw, fd, goq, d_resid, g_attn, d_g_mlp, d_g_heads
     )
     device = lax.axis_index(AXES)
     out_gains = lax.dynamic_slice(gains_sum.reshape(3072), (device * 72,), (72,))
-    return (output, grad_tokens, *grads, out_gains)
+    return (*finish(rq, rqo, wide, deep, landed, output), out_gains)
 
 
 def fast_solution(mesh):

time: 409 us -> 389 us (0.951)
  local copies, waits for them, and re-layouts: 18.6 us -> 4.7 us
  Pallas kernels: 387 us -> 381 us
    unnamed x60 -> x5, local copies, waits for them, and re-layouts: 16.5 us -> 1.6 us
    pallas_call x1, Pallas kernels: 86.3 us -> 81.2 us  [attend_back(): pl.pallas_call(attend_back_kernel, out_shape=(jax.ShapeDtypeStruct((SEQ_R...]
    pallas_call x1 -> x2, Pallas kernels: 86 us -> 83.3 us  [the longest x1 78.8 us: tail(): pl.pallas_call(tail_kernel, out_shape=(jax.ShapeDtypeStruct((4, 32, 1024)...]
where the time goes in v4:
time: 389 us; the launch traced here: 388 us
  Pallas kernels  381 us (98%)
  local copies, waits for them, and re-layouts  4.7 us (1%)
    pallas_call x1, Pallas kernels, attend_back(): pl.pallas_call(attend_back_kernel, out_shape=(jax.ShapeDtypeStruct((SEQ_R...  81.2 us
    pallas_call x1, Pallas kernels, tail(): pl.pallas_call(tail_kernel, out_shape=(jax.ShapeDtypeStruct((4, 32, 1024)...  78.8 us
    pallas_call x1, Pallas kernels, front(): pl.pallas_call(front_kernel, out_shape=(jax.ShapeDtypeStruct((8, ROWS, MO...  71.7 us
    pallas_call x1, Pallas kernels, attend(): pl.pallas_call(attend_kernel, out_shape=(jax.ShapeDtypeStruct((SEQ_ROWS,...  50.9 us
    pallas_call x1, Pallas kernels, finish_resid(): pl.pallas_call(resid_kernel, out_shape=(jax.ShapeDtypeStruct((OWN, MODEL_...  48.3 us
    pallas_call x1, Pallas kernels, feed_forward(): pl.pallas_call(forward_kernel, grid=(HALF_FF // CHUNK,), out_shape=(jax.S...  45.4 us

profile of v4, /device:TPU:0, one launch (start us, length us, event | category | flops | bytes accessed | tf_op | source)
XLA Modules:
  0.0 388.3 jit_solution(8599583339258905505)
XLA Ops:
  0.6 0.0 copy-start
  0.7 0.7 copy-done
  1.3 0.1 compare_reduce_fusion
  1.4 0.5 convert_element_type.6.flags
  2.0 0.1 pad_maximum_fusion
  2.0 0.6 broadcast_in_dim.20.inverse
  2.6 1.2 bitcast_convert_fusion.gn
  3.9 71.7 %front_gather.1 = (bf16[8,256,1024]{2,1,0:T(8,128)(2,1)}, bf16[1024,1024]{1,0:T(8,128)(2,1)}, bf16[2048,256]{1,0:T(8,128)(2,1)}, f32[32,8,128]{2,1,0:T(8,128)}, ...) custom-call(bf16[2,256,1024]{2,1,0:T(8,128)(2,1)} %tok.1, ...), custom_call_target="tpu_custom_call" | custom-call | tf_op jit(solution)/shard_map/front_gather/pallas_call | solution.py:616
  75.6 0.9 copy.27
  76.6 0.1 reshape.55
  76.7 0.5 slice_bitcast_fusion
  77.2 0.6 fusion
  77.8 50.9 %attend.1 = (bf16[2048,1024]{1,0:T(8,128)(2,1)}, bf16[4,2048,128]{2,1,0:T(8,128)(2,1)}, bf16[2,2048,128]{2,1,0:T(8,128)(2,1)}, bf16[2,2048,128]{2,1,0:T(8,128)(2...) custom-call(s32[8]{0:T(128)} %convert_element_type.6.flags, ...), custom_call_target="tpu_custom_call", output_to_operand_aliasing={{9}: (9, {}), {10}: (10, {})} | custom-call | flops 8589934592 | bytes 25165824 | tf_op jit(solution)/shard_map/attend/pallas_call | solution.py:933
  128.7 48.3 %residual.1 = (f32[512,1024]{1,0:T(8,128)}, bf16[2,512,1024]{2,1,0:T(8,128)(2,1)}, bf16[2,1024,1536]{2,1,0:T(8,128)(2,1)}, bf16[3072,512]{1,0:T(8,128)(2,1)}, bf...) custom-call(bf16[2048,512]{1,0:T(8,128)(2,1)} %get-tuple-element.76.attn., ...), custom_call_target="tpu_custom_call", output_to_operand_aliasing={{2}: (5, {}), {3}: (6, {})} | custom-call | tf_op jit(solution)/shard_map/residual/pallas_call | solution.py:1091
  176.9 45.4 %feed_forward.1 = (bf16[2,1024,1536]{2,1,0:T(8,128)(2,1)}, bf16[2,1536,512]{2,1,0:T(8,128)(2,1)}, bf16[4,2,2,64,1024]{4,3,2,1,0:T(8,128)(2,1)}, f32[512,1024]{1,...) custom-call(bf16[1024,1024]{1,0:T(8,128)(2,1)} %bitcast.23, ...), custom_call_target="tpu_custom_call" | custom-call | tf_op jit(solution)/shard_map/feed_forward/pallas_call | solution.py:1262
  222.3 81.2 %attend_back.1 = (bf16[2048,1024]{1,0:T(8,128)(2,1)}, bf16[2048,256]{1,0:T(8,128)(2,1)}, bf16[2,2,2,64,1536]{4,3,2,1,0:T(8,128)(2,1)}, bf16[2,2,192,512]{3,2,1,0...) custom-call(s32[8]{0:T(128)} %convert_element_type.6.flags, ...), custom_call_target="tpu_custom_call" | custom-call | flops 21474836480 | bytes 41943040 | tf_op jit(solution)/shard_map/attend_back/pallas_call | solution.py:1609
  303.5 0.0 copy-start.1
  303.5 78.8 %tail_reduce.1 = (bf16[4,32,1024]{2,1,0:T(8,128)(2,1)}, bf16[4,64,256]{2,1,0:T(8,128)(2,1)}, f32[2,2,32,1536]{3,2,1,0:T(8,128)}, f32[2,96,512]{2,1,0:T(8,128)}, ...) custom-call(bf16[2048,1024]{1,0:T(8,128)(2,1)} %get-tuple-element.94.d_in, ...), custom_call_target="tpu_custom_call" | custom-call | tf_op jit(solution)/shard_map/tail_reduce/pallas_call | solution.py:1951
  382.4 1.3 dynamic_slice.8
  383.7 4.5 %finish.1 = (bf16[2,256,1024]{2,1,0:T(8,128)(2,1)}, f32[2,256,1024]{2,1,0:T(8,128)}, f32[32,2048]{1,0:T(8,128)}, f32[32,1024]{1,0:T(8,128)}, f32[32,1024]{1,0:T(...) custom-call(bf16[4,32,1024]{2,1,0:T(8,128)(2,1)} %get-tuple-element.104.rq, ...), custom_call_target="tpu_custom_call" | custom-call | tf_op jit(solution)/shard_map/finish/pallas_call | solution.py:1915
  388.1 0.0 copy-done.1
  (4 shorter events, 0.0 us)
Async XLA Ops:
  0.6 0.7 copy-start
  303.5 84.7 %copy-start.1 = (s32[2,4]{1,0:T(2,128)S(1)}, s32[2,4]{1,0:T(2,128)}, u32[]{:S(2)}) copy-start(s32[2,4]{1,0:T(2,128)} %param.13) | copy-start | bytes 100

commit v5 on v4

--- a/solution.py
+++ b/solution.py
@@ -597,12 +597,12 @@
         net.arrived(go_other_y[k])
         net.start(go_other_x[k])
     net.arrived(*go_own_x)
-    net.start(*go_own_y, go_mlp_near)
+    net.start(*go_own_y)
     net.arrived(go_far_0)
     net.start(go_far_l0)
     table(12, 32)
     net.arrived(go_far_1)
-    net.start(go_far_l1, go_far_relay)
+    net.start(go_far_l1, go_far_relay, go_mlp_near)
     net.arrived(go_far_l0, go_far_l1)
     net.start(go_far_l_relay)
     net.arrived(go_near_c, go_near_relay, go_far_relay, go_far_l_relay, *go_own_y, *go_other_x, go_mlp_x, go_mlp_near)
@@ -862,7 +862,7 @@
         net.arrived(go_near_y)
         net.start(go_mlp_x, go_mlp_y)
 
-    for k, at in enumerate((PROJECT + 2, PROJECT + 4)):
+    for k, at in enumerate((PROJECT + 3, PROJECT + 5)):
 
         @pl.when(step == at)
         def _():
@@ -1474,7 +1474,7 @@
         net.arrived(second_a[FAR])
         plus(og.at[FAR, u_far, :, :, early], rc.at[0, :, :, early])
 
-    @pl.when(step == 1)
+    @pl.when(step == 0)
     def _():
         home.start()
 
@@ -1495,7 +1495,7 @@
         net.arrived(go_db_r)
         branch(owned(p, 1 - l, 1 - c))
 
-    @pl.when(step == 5)
+    @pl.when(step == 4)
     def _():
         net.arrived(go_fal_a)
         plus(og.at[FAR, u_far, :, :, early], rz.at[:, :, early])
@@ -1783,7 +1783,7 @@
     project(1 - l, c, hold(0))
     net.arrived(go_give_0)
     send_l[...] = (keep[0] + recv_c[0].astype(jnp.float32)).astype(jnp.bfloat16)
-    net.start(go_cross[0])
+    net.start(*go_cross)
     project(l, 1 - c, give(1))
     net.start(go_give_1)
     project(l, c, hold(1))
@@ -1830,9 +1830,7 @@
         gt[rows, :] = (dr_ref[rows, :] + back).astype(jnp.bfloat16)
         return total + jnp.sum(grad * scaled, axis=0, keepdims=True)
 
-    lax.fori_loop(0, 1, one_chunk, 0)
-    net.start(go_cross[1])
-    lax.fori_loop(1, 2, one_chunk, 0)
+    lax.fori_loop(0, 2, one_chunk, 0)
     net.arrived(go_give_1, go_cross[0])
     d_attn = lax.fori_loop(0, 4, rows_back, jnp.zeros((1, MODEL_DIM), jnp.float32))
     home.start_one(0)

time: 389 us -> 384 us (0.987)
  Pallas kernels: 381 us -> 376 us
where the time goes in v5:
time: 384 us; the launch traced here: 383 us
  Pallas kernels  376 us (98%)
  local copies, waits for them, and re-layouts  4.7 us (1%)
    pallas_call x1, Pallas kernels, attend_back(): pl.pallas_call(attend_back_kernel, out_shape=(jax.ShapeDtypeStruct((SEQ_R...  79.8 us
    pallas_call x1, Pallas kernels, tail(): pl.pallas_call(tail_kernel, out_shape=(jax.ShapeDtypeStruct((4, 32, 1024)...  77.7 us
    pallas_call x1, Pallas kernels, front(): pl.pallas_call(front_kernel, out_shape=(jax.ShapeDtypeStruct((8, ROWS, MO...  71.7 us
    pallas_call x1, Pallas kernels, finish_resid(): pl.pallas_call(resid_kernel, out_shape=(jax.ShapeDtypeStruct((OWN, MODEL_...  48.8 us
    pallas_call x1, Pallas kernels, attend(): pl.pallas_call(attend_kernel, out_shape=(jax.ShapeDtypeStruct((SEQ_ROWS,...  47.6 us
    pallas_call x1, Pallas kernels, feed_forward(): pl.pallas_call(forward_kernel, grid=(HALF_FF // CHUNK,), out_shape=(jax.S...  45.5 us

profile of v5, /device:TPU:0, one launch (start us, length us, event | category | flops | bytes accessed | tf_op | source)
XLA Modules:
  0.0 383.3 jit_solution(10348533197422200587)
XLA Ops:
  0.6 0.0 copy-start
  0.7 0.7 copy-done
  1.3 0.1 compare_reduce_fusion
  1.4 0.5 convert_element_type.6.flags
  2.0 0.1 pad_maximum_fusion
  2.0 0.6 broadcast_in_dim.20.inverse
  2.6 1.2 bitcast_convert_fusion.gn
  3.9 71.7 %front_gather.1 = (bf16[8,256,1024]{2,1,0:T(8,128)(2,1)}, bf16[1024,1024]{1,0:T(8,128)(2,1)}, bf16[2048,256]{1,0:T(8,128)(2,1)}, f32[32,8,128]{2,1,0:T(8,128)}, ...) custom-call(bf16[2,256,1024]{2,1,0:T(8,128)(2,1)} %tok.1, ...), custom_call_target="tpu_custom_call" | custom-call | tf_op jit(solution)/shard_map/front_gather/pallas_call | solution.py:616
  75.6 0.9 copy.27
  76.6 0.1 reshape.55
  76.7 0.5 slice_bitcast_fusion
  77.2 0.6 fusion
  77.8 47.6 %attend.1 = (bf16[2048,1024]{1,0:T(8,128)(2,1)}, bf16[4,2048,128]{2,1,0:T(8,128)(2,1)}, bf16[2,2048,128]{2,1,0:T(8,128)(2,1)}, bf16[2,2048,128]{2,1,0:T(8,128)(2...) custom-call(s32[8]{0:T(128)} %convert_element_type.6.flags, ...), custom_call_target="tpu_custom_call", output_to_operand_aliasing={{9}: (9, {}), {10}: (10, {})} | custom-call | flops 8589934592 | bytes 25165824 | tf_op jit(solution)/shard_map/attend/pallas_call | solution.py:933
  125.4 48.8 %residual.1 = (f32[512,1024]{1,0:T(8,128)}, bf16[2,512,1024]{2,1,0:T(8,128)(2,1)}, bf16[2,1024,1536]{2,1,0:T(8,128)(2,1)}, bf16[3072,512]{1,0:T(8,128)(2,1)}, bf...) custom-call(bf16[2048,512]{1,0:T(8,128)(2,1)} %get-tuple-element.76.attn., ...), custom_call_target="tpu_custom_call", output_to_operand_aliasing={{2}: (5, {}), {3}: (6, {})} | custom-call | tf_op jit(solution)/shard_map/residual/pallas_call | solution.py:1091
  174.3 45.5 %feed_forward.1 = (bf16[2,1024,1536]{2,1,0:T(8,128)(2,1)}, bf16[2,1536,512]{2,1,0:T(8,128)(2,1)}, bf16[4,2,2,64,1024]{4,3,2,1,0:T(8,128)(2,1)}, f32[512,1024]{1,...) custom-call(bf16[1024,1024]{1,0:T(8,128)(2,1)} %bitcast.23, ...), custom_call_target="tpu_custom_call" | custom-call | tf_op jit(solution)/shard_map/feed_forward/pallas_call | solution.py:1262
  219.8 79.8 %attend_back.1 = (bf16[2048,1024]{1,0:T(8,128)(2,1)}, bf16[2048,256]{1,0:T(8,128)(2,1)}, bf16[2,2,2,64,1536]{4,3,2,1,0:T(8,128)(2,1)}, bf16[2,2,192,512]{3,2,1,0...) custom-call(s32[8]{0:T(128)} %convert_element_type.6.flags, ...), custom_call_target="tpu_custom_call" | custom-call | flops 21474836480 | bytes 41943040 | tf_op jit(solution)/shard_map/attend_back/pallas_call | solution.py:1609
  299.5 0.0 copy-start.1
  299.6 77.7 %tail_reduce.1 = (bf16[4,32,1024]{2,1,0:T(8,128)(2,1)}, bf16[4,64,256]{2,1,0:T(8,128)(2,1)}, f32[2,2,32,1536]{3,2,1,0:T(8,128)}, f32[2,96,512]{2,1,0:T(8,128)}, ...) custom-call(bf16[2048,1024]{1,0:T(8,128)(2,1)} %get-tuple-element.94.d_in, ...), custom_call_target="tpu_custom_call" | custom-call | tf_op jit(solution)/shard_map/tail_reduce/pallas_call | solution.py:1949
  377.3 1.3 dynamic_slice.8
  378.6 4.5 %finish.1 = (bf16[2,256,1024]{2,1,0:T(8,128)(2,1)}, f32[2,256,1024]{2,1,0:T(8,128)}, f32[32,2048]{1,0:T(8,128)}, f32[32,1024]{1,0:T(8,128)}, f32[32,1024]{1,0:T(...) custom-call(bf16[4,32,1024]{2,1,0:T(8,128)(2,1)} %get-tuple-element.104.rq, ...), custom_call_target="tpu_custom_call" | custom-call | tf_op jit(solution)/shard_map/finish/pallas_call | solution.py:1913
  383.1 0.0 copy-done.1
  (4 shorter events, 0.0 us)
Async XLA Ops:
  0.6 0.7 copy-start
  299.5 83.5 %copy-start.1 = (s32[2,4]{1,0:T(2,128)S(1)}, s32[2,4]{1,0:T(2,128)}, u32[]{:S(2)}) copy-start(s32[2,4]{1,0:T(2,128)} %param.13) | copy-start | bytes 100

commit v6 on v5

--- a/solution.py
+++ b/solution.py
@@ -1128,7 +1128,7 @@
 def forward_kernel(
     m_ref, dy_ref, w_ref, wdn, wx_ref, resid, g_mlp,
     ggu, gdb, rb, d_resid, db, res, dg,
-    mt, dyt, hid, dgt, dup, d_in, down, give, take, all_down, ggv, gdv, send_sem, recv_sem, load_sem, out_sem,
+    mt, hid, dgt, dup, d_in, down, give, take, all_down, ggv, gdv, send_sem, recv_sem, load_sem, out_sem,
 ):
     where = place()
     y, x, p, l, c = where
@@ -1166,7 +1166,6 @@
         def flip(k, carry):
             rows = rows_at(k, 256)
             mt[:, rows] = m_ref[rows, :].T
-            dyt[:, rows] = dy_ref[rows, :].T
             return carry
 
         lax.fori_loop(0, 4, flip, 0)
@@ -1206,13 +1205,13 @@
     now = rows_at(step, CHUNK)
 
     def weights(k, carry):
-        rows = rows_at(k, 512)
+        rows = rows_at(k, 1024)
         ggv[0, rows, now] = dot(mt[rows, :], dgt[...]).astype(jnp.bfloat16)
         ggv[1, rows, now] = dot(mt[rows, :], dup[...]).astype(jnp.bfloat16)
-        gdv[now, rows] = dot(dyt[rows, :], hid[...]).T.astype(jnp.bfloat16)
+        gdv[now, rows] = dot(hid[...], dy_ref[:, rows], TN).astype(jnp.bfloat16)
         return carry
 
-    lax.fori_loop(0, 2, weights, 0)
+    lax.fori_loop(0, 1, weights, 0)
     for f in range(HALF_FF // CHUNK):
 
         @pl.when(step == f)
@@ -1277,7 +1276,6 @@
         out_specs=[pl.BlockSpec(memory_space=pl.ANY)] * 3
         + [whole(own), whole(own), whole(own), whole((8, MODEL_DIM))],
         scratch_shapes=[
-            pltpu.VMEM(rows, bf16),
             pltpu.VMEM(rows, bf16),
             pltpu.VMEM((1024, CHUNK), bf16),
             pltpu.VMEM((1024, CHUNK), bf16),

time: 384 us -> 383 us (level)
  no operation moved by 1% of the time
where the time goes in v6:
time: 383 us; the launch traced here: 382 us
  Pallas kernels  374 us (98%)
  local copies, waits for them, and re-layouts  4.7 us (1%)
    pallas_call x1, Pallas kernels, attend_back(): pl.pallas_call(attend_back_kernel, out_shape=(jax.ShapeDtypeStruct((SEQ_R...  80.1 us
    pallas_call x1, Pallas kernels, tail(): pl.pallas_call(tail_kernel, out_shape=(jax.ShapeDtypeStruct((4, 32, 1024)...  77.6 us
    pallas_call x1, Pallas kernels, front(): pl.pallas_call(front_kernel, out_shape=(jax.ShapeDtypeStruct((8, ROWS, MO...  71.7 us
    pallas_call x1, Pallas kernels, finish_resid(): pl.pallas_call(resid_kernel, out_shape=(jax.ShapeDtypeStruct((OWN, MODEL_...  48.8 us
    pallas_call x1, Pallas kernels, attend(): pl.pallas_call(attend_kernel, out_shape=(jax.ShapeDtypeStruct((SEQ_ROWS,...  47.6 us
    pallas_call x1, Pallas kernels, feed_forward(): pl.pallas_call(forward_kernel, grid=(HALF_FF // CHUNK,), out_shape=(jax.S...  44 us

profile of v6, /device:TPU:0, one launch (start us, length us, event | category | flops | bytes accessed | tf_op | source)
XLA Modules:
  0.0 382.0 jit_solution(6971980460703635807)
XLA Ops:
  0.6 0.0 copy-start
  0.7 0.7 copy-done
  1.3 0.1 compare_reduce_fusion
  1.4 0.5 convert_element_type.6.flags
  2.0 0.1 pad_maximum_fusion
  2.0 0.6 broadcast_in_dim.20.inverse
  2.6 1.2 bitcast_convert_fusion.gn
  3.9 71.7 %front_gather.1 = (bf16[8,256,1024]{2,1,0:T(8,128)(2,1)}, bf16[1024,1024]{1,0:T(8,128)(2,1)}, bf16[2048,256]{1,0:T(8,128)(2,1)}, f32[32,8,128]{2,1,0:T(8,128)}, ...) custom-call(bf16[2,256,1024]{2,1,0:T(8,128)(2,1)} %tok.1, ...), custom_call_target="tpu_custom_call" | custom-call | tf_op jit(solution)/shard_map/front_gather/pallas_call | solution.py:616
  75.6 0.9 copy.27
  76.6 0.1 reshape.55
  76.7 0.5 slice_bitcast_fusion
  77.2 0.6 fusion
  77.8 47.6 %attend.1 = (bf16[2048,1024]{1,0:T(8,128)(2,1)}, bf16[4,2048,128]{2,1,0:T(8,128)(2,1)}, bf16[2,2048,128]{2,1,0:T(8,128)(2,1)}, bf16[2,2048,128]{2,1,0:T(8,128)(2...) custom-call(s32[8]{0:T(128)} %convert_element_type.6.flags, ...), custom_call_target="tpu_custom_call", output_to_operand_aliasing={{9}: (9, {}), {10}: (10, {})} | custom-call | flops 8589934592 | bytes 25165824 | tf_op jit(solution)/shard_map/attend/pallas_call | solution.py:933
  125.4 48.8 %residual.1 = (f32[512,1024]{1,0:T(8,128)}, bf16[2,512,1024]{2,1,0:T(8,128)(2,1)}, bf16[2,1024,1536]{2,1,0:T(8,128)(2,1)}, bf16[3072,512]{1,0:T(8,128)(2,1)}, bf...) custom-call(bf16[2048,512]{1,0:T(8,128)(2,1)} %get-tuple-element.76.attn., ...), custom_call_target="tpu_custom_call", output_to_operand_aliasing={{2}: (5, {}), {3}: (6, {})} | custom-call | tf_op jit(solution)/shard_map/residual/pallas_call | solution.py:1091
  174.3 44.0 %feed_forward.1 = (bf16[2,1024,1536]{2,1,0:T(8,128)(2,1)}, bf16[2,1536,512]{2,1,0:T(8,128)(2,1)}, bf16[4,2,2,64,1024]{4,3,2,1,0:T(8,128)(2,1)}, f32[512,1024]{1,...) custom-call(bf16[1024,1024]{1,0:T(8,128)(2,1)} %bitcast.23, ...), custom_call_target="tpu_custom_call" | custom-call | tf_op jit(solution)/shard_map/feed_forward/pallas_call | solution.py:1261
  218.3 80.1 %attend_back.1 = (bf16[2048,1024]{1,0:T(8,128)(2,1)}, bf16[2048,256]{1,0:T(8,128)(2,1)}, bf16[2,2,2,64,1536]{4,3,2,1,0:T(8,128)(2,1)}, bf16[2,2,192,512]{3,2,1,0...) custom-call(s32[8]{0:T(128)} %convert_element_type.6.flags, ...), custom_call_target="tpu_custom_call" | custom-call | flops 21474836480 | bytes 41943040 | tf_op jit(solution)/shard_map/attend_back/pallas_call | solution.py:1607
  298.4 0.0 copy-start.1
  298.4 77.6 %tail_reduce.1 = (bf16[4,32,1024]{2,1,0:T(8,128)(2,1)}, bf16[4,64,256]{2,1,0:T(8,128)(2,1)}, f32[2,2,32,1536]{3,2,1,0:T(8,128)}, f32[2,96,512]{2,1,0:T(8,128)}, ...) custom-call(bf16[2048,1024]{1,0:T(8,128)(2,1)} %get-tuple-element.94.d_in, ...), custom_call_target="tpu_custom_call" | custom-call | tf_op jit(solution)/shard_map/tail_reduce/pallas_call | solution.py:1947
  376.0 1.3 dynamic_slice.8
  377.3 4.5 %finish.1 = (bf16[2,256,1024]{2,1,0:T(8,128)(2,1)}, f32[2,256,1024]{2,1,0:T(8,128)}, f32[32,2048]{1,0:T(8,128)}, f32[32,1024]{1,0:T(8,128)}, f32[32,1024]{1,0:T(...) custom-call(bf16[4,32,1024]{2,1,0:T(8,128)(2,1)} %get-tuple-element.104.rq, ...), custom_call_target="tpu_custom_call" | custom-call | tf_op jit(solution)/shard_map/finish/pallas_call | solution.py:1911
  381.8 0.0 copy-done.1
  (4 shorter events, 0.0 us)
Async XLA Ops:
  0.6 0.7 copy-start
  298.4 83.4 %copy-start.1 = (s32[2,4]{1,0:T(2,128)S(1)}, s32[2,4]{1,0:T(2,128)}, u32[]{:S(2)}) copy-start(s32[2,4]{1,0:T(2,128)} %param.13) | copy-start | bytes 100

commit v7 on v6

--- a/solution.py
+++ b/solution.py
@@ -799,7 +799,8 @@
     return (key <= query) | ((key // PIECE == upper) & (piece > 0))
 
 
-PROJECT = 8
+PROJECT = 4
+TALL = SEQ_ROWS // PROJECT
 
 
 def attend_kernel(
@@ -846,7 +847,7 @@
         n_ref[...] = normed
         full = dot(normed, w_ref[...])
         cosine, sine = cos_ref[...], sin_ref[...]
-        rows = rows_at(jnp.minimum(step, PROJECT - 1), 256)
+        rows = rows_at(jnp.minimum(step, PROJECT - 1), TALL)
         for h in range(QH + KH):
             u = full[:, h * HEAD_DIM : (h + 1) * HEAD_DIM]
             raw_ref, out_ref, g_ref, at = (qr_ref, q_ref, gq_ref, h) if h < QH else (kr_ref, k_ref, gk_ref, h - QH)
@@ -917,13 +918,13 @@
         return jnp.maximum(s - PROJECT, 0)
 
     def row(width):
-        return pl.BlockSpec((256, width), lambda s, f: (early(s), 0))
+        return pl.BlockSpec((TALL, width), lambda s, f: (early(s), 0))
 
     def whole(shape):
         return pl.BlockSpec(shape, lambda s, f: (0,) * len(shape))
 
     def heads(n):
-        return pl.BlockSpec((n, 256, HEAD_DIM), lambda s, f: (0, early(s), 0))
+        return pl.BlockSpec((n, TALL, HEAD_DIM), lambda s, f: (0, early(s), 0))
 
     def shape(n, dtype):
         return jax.ShapeDtypeStruct((n, SEQ_ROWS, HEAD_DIM), dtype)

time: 383 us -> 383 us (level)
  no operation moved by 1% of the time
where the time goes in v7:
time: 383 us
  Pallas kernels  375 us (98%)
  local copies, waits for them, and re-layouts  4.7 us (1%)
    pallas_call x1, Pallas kernels, attend_back(): pl.pallas_call(attend_back_kernel, out_shape=(jax.ShapeDtypeStruct((SEQ_R...  79.7 us
    pallas_call x1, Pallas kernels, tail(): pl.pallas_call(tail_kernel, out_shape=(jax.ShapeDtypeStruct((4, 32, 1024)...  77.8 us
    pallas_call x1, Pallas kernels, front(): pl.pallas_call(front_kernel, out_shape=(jax.ShapeDtypeStruct((8, ROWS, MO...  71.7 us
    pallas_call x1, Pallas kernels, attend(): pl.pallas_call(attend_kernel, out_shape=(jax.ShapeDtypeStruct((SEQ_ROWS,...  49.1 us
    pallas_call x1, Pallas kernels, finish_resid(): pl.pallas_call(resid_kernel, out_shape=(jax.ShapeDtypeStruct((OWN, MODEL_...  48.5 us
    pallas_call x1, Pallas kernels, feed_forward(): pl.pallas_call(forward_kernel, grid=(HALF_FF // CHUNK,), out_shape=(jax.S...  44 us

profile of v7, /device:TPU:0, one launch (start us, length us, event | category | flops | bytes accessed | tf_op | source)
XLA Modules:
  0.0 382.8 jit_solution(9004720517110964535)
XLA Ops:
  0.6 0.0 copy-start
  0.7 0.7 copy-done
  1.3 0.1 compare_reduce_fusion
  1.4 0.5 convert_element_type.6.flags
  2.0 0.1 pad_maximum_fusion
  2.0 0.6 broadcast_in_dim.20.inverse
  2.6 1.2 bitcast_convert_fusion.gn
  3.9 71.7 %front_gather.1 = (bf16[8,256,1024]{2,1,0:T(8,128)(2,1)}, bf16[1024,1024]{1,0:T(8,128)(2,1)}, bf16[2048,256]{1,0:T(8,128)(2,1)}, f32[32,8,128]{2,1,0:T(8,128)}, ...) custom-call(bf16[2,256,1024]{2,1,0:T(8,128)(2,1)} %tok.1, ...), custom_call_target="tpu_custom_call" | custom-call | tf_op jit(solution)/shard_map/front_gather/pallas_call | solution.py:616
  75.6 0.9 copy.27
  76.6 0.1 reshape.55
  76.7 0.5 slice_bitcast_fusion
  77.2 0.6 fusion
  77.8 49.1 %attend.1 = (bf16[2048,1024]{1,0:T(8,128)(2,1)}, bf16[4,2048,128]{2,1,0:T(8,128)(2,1)}, bf16[2,2048,128]{2,1,0:T(8,128)(2,1)}, bf16[2,2048,128]{2,1,0:T(8,128)(2...) custom-call(s32[8]{0:T(128)} %convert_element_type.6.flags, ...), custom_call_target="tpu_custom_call", output_to_operand_aliasing={{9}: (9, {}), {10}: (10, {})} | custom-call | flops 8589934592 | bytes 25165824 | tf_op jit(solution)/shard_map/attend/pallas_call | solution.py:934
  126.9 48.5 %residual.1 = (f32[512,1024]{1,0:T(8,128)}, bf16[2,512,1024]{2,1,0:T(8,128)(2,1)}, bf16[2,1024,1536]{2,1,0:T(8,128)(2,1)}, bf16[3072,512]{1,0:T(8,128)(2,1)}, bf...) custom-call(bf16[2048,512]{1,0:T(8,128)(2,1)} %get-tuple-element.76.attn., ...), custom_call_target="tpu_custom_call", output_to_operand_aliasing={{2}: (5, {}), {3}: (6, {})} | custom-call | tf_op jit(solution)/shard_map/residual/pallas_call | solution.py:1092
  175.4 44.0 %feed_forward.1 = (bf16[2,1024,1536]{2,1,0:T(8,128)(2,1)}, bf16[2,1536,512]{2,1,0:T(8,128)(2,1)}, bf16[4,2,2,64,1024]{4,3,2,1,0:T(8,128)(2,1)}, f32[512,1024]{1,...) custom-call(bf16[1024,1024]{1,0:T(8,128)(2,1)} %bitcast.23, ...), custom_call_target="tpu_custom_call" | custom-call | tf_op jit(solution)/shard_map/feed_forward/pallas_call | solution.py:1262
  219.4 79.7 %attend_back.1 = (bf16[2048,1024]{1,0:T(8,128)(2,1)}, bf16[2048,256]{1,0:T(8,128)(2,1)}, bf16[2,2,2,64,1536]{4,3,2,1,0:T(8,128)(2,1)}, bf16[2,2,192,512]{3,2,1,0...) custom-call(s32[8]{0:T(128)} %convert_element_type.6.flags, ...), custom_call_target="tpu_custom_call" | custom-call | flops 21474836480 | bytes 41943040 | tf_op jit(solution)/shard_map/attend_back/pallas_call | solution.py:1608
  299.1 0.0 copy-start.1
  299.1 77.8 %tail_reduce.1 = (bf16[4,32,1024]{2,1,0:T(8,128)(2,1)}, bf16[4,64,256]{2,1,0:T(8,128)(2,1)}, f32[2,2,32,1536]{3,2,1,0:T(8,128)}, f32[2,96,512]{2,1,0:T(8,128)}, ...) custom-call(bf16[2048,1024]{1,0:T(8,128)(2,1)} %get-tuple-element.94.d_in, ...), custom_call_target="tpu_custom_call" | custom-call | tf_op jit(solution)/shard_map/tail_reduce/pallas_call | solution.py:1948
  376.8 1.3 dynamic_slice.8
  378.1 4.5 %finish.1 = (bf16[2,256,1024]{2,1,0:T(8,128)(2,1)}, f32[2,256,1024]{2,1,0:T(8,128)}, f32[32,2048]{1,0:T(8,128)}, f32[32,1024]{1,0:T(8,128)}, f32[32,1024]{1,0:T(...) custom-call(bf16[4,32,1024]{2,1,0:T(8,128)(2,1)} %get-tuple-element.104.rq, ...), custom_call_target="tpu_custom_call" | custom-call | tf_op jit(solution)/shard_map/finish/pallas_call | solution.py:1912
  382.6 0.0 copy-done.1
  (4 shorter events, 0.0 us)
Async XLA Ops:
  0.6 0.7 copy-start
  299.1 83.6 %copy-start.1 = (s32[2,4]{1,0:T(2,128)S(1)}, s32[2,4]{1,0:T(2,128)}, u32[]{:S(2)}) copy-start(s32[2,4]{1,0:T(2,128)} %param.13) | copy-start | bytes 100
